TPU v7x, 256 devices: a whole 4x4x8 slice. The times are simulated.
256 devices in a mesh: kern: 4 (over z_lo, core), slab: 64 (over z_hi, y, x).
Axes of the slice: x: 4, y: 4, z: 8 (z_hi: 4, z_lo: 2; z = z_hi * 2 + z_lo), core: 2. Of those that a mesh axis runs over, the one named last changes fastest.
Arguments:
- layout: int32 [4096, 4096], P('slab', 'kern'), may hold values 0 or 1
- band_freqs: int32 [128], replicated, may hold values from -256 to 255, as said below
- kernels: float32 [2, 48, 128, 128], P(None, 'kern'), may hold values from -6 to 6
- eigen_values: float32 [48], P('kern'), may hold values from 0.1 to 1
- bake_rates: float32 [5], replicated, may hold values from 0.1 to 0.25
Outputs:
- aerial_image: float32 [4096, 4096], P('slab', 'kern')
- latent_acid: float32 [4096, 4096], P('slab', 'kern')
Inputs may be any that keep to these rules, and one draw needn't show every extreme that they name: `band_freqs`: the 128 numbers are distinct; both ends of the range are among them.
All inputs are finite; a program needn't handle non-finite values. No bound on the sum of `layout` on one device may be relied on, other than what follows from the above.
Results may differ from a plain program's by a relative error of at most 0.0017.
Values sent between devices are 32-bit elements; how exact they have to be, the bound alone decides.
No kernel may reach another device: no remote copies, remote signals or barrier semaphores. Data moves between devices by JAX's collectives and lax.ppermute only.
A program may use at most 64 MiB of HBM per device.

v0:
```python
import math

import jax
import jax.numpy as jnp
from jax import lax
from jax.sharding import PartitionSpec as P

N = 4096
W = 128
FIELDS = 48
STEPS = 2


highest = lax.Precision.HIGHEST


def padded_2(cells, sides, width):
    for axis, dim in sides:
        count = lax.axis_size(axis)
        head = lax.slice_in_dim(cells, 0, width, axis=dim)
        tail = lax.slice_in_dim(cells, cells.shape[dim] - width, cells.shape[dim], axis=dim)
        cells = jnp.concatenate(
            [
                lax.ppermute(tail, axis, [(i, (i + 1) % count) for i in range(count)]),
                cells,
                lax.ppermute(head, axis, [((i + 1) % count, i) for i in range(count)]),
            ],
            axis=dim,
        )
    return cells


def tables(frequencies, first_index, length):
    positions = first_index + jnp.arange(length, dtype=jnp.int32)
    angles = jnp.mod(positions[:, None] * frequencies[None, :], N).astype(jnp.float32) * (
        2.0 * math.pi / N
    )
    return (jnp.cos(angles), jnp.sin(angles))


def stencil(padded):
    centre = padded[:, 1:-1, 1:-1]
    return (
        padded[:, 2:, 1:-1]
        + padded[:, :-2, 1:-1]
        + padded[:, 1:-1, 2:]
        + padded[:, 1:-1, :-2]
        - 4.0 * centre
    )


def bake(aerial_image, bake_rates, extend):
    dill_rate, acid_rate, quench_rate, react_rate, quench_start = (
        bake_rates[0],
        bake_rates[1],
        bake_rates[2],
        bake_rates[3],
        bake_rates[4],
    )
    acid_field = 1.0 - jnp.exp(-4.0 * dill_rate * aerial_image)
    acid_diffusion = acid_rate * (0.5 + 0.5 * acid_field)
    quencher = jnp.zeros_like(acid_field) + quench_start
    for bake_step in range(STEPS):
        laplaces = stencil(extend(jnp.stack([acid_field, quencher])))
        reaction = 4.0 * react_rate * acid_field * quencher
        new_acid = acid_field + acid_diffusion * laplaces[0] - reaction
        quencher = quencher + quench_rate * laplaces[1] - reaction
        acid_field = new_acid
    return acid_field


def shards(layout, band_freqs, kernels, eigen_values, bake_rates):
    rows = layout.shape[0]
    cols = layout.shape[1]
    row_first = lax.axis_index("slab") * rows
    col_first = lax.axis_index("kern") * cols
    transmit = (2 * layout - 1).astype(jnp.float32)
    cos_col, sin_col = tables(band_freqs, col_first, cols)
    along_re = jnp.dot(transmit, cos_col, precision=highest)
    along_im = -jnp.dot(transmit, sin_col, precision=highest)
    cos_row, sin_row = tables(band_freqs, row_first, rows)
    first = (
        jnp.dot(cos_row.T, along_re, precision=highest)
        + jnp.dot(sin_row.T, along_im, precision=highest)
    ) / N
    second = (
        jnp.dot(cos_row.T, along_im, precision=highest)
        - jnp.dot(sin_row.T, along_re, precision=highest)
    ) / N
    spectrum = lax.psum(jnp.stack([first, second]), ("kern", "slab"))
    spec_re = spectrum[0]
    spec_im = spectrum[1]
    row_table = jnp.concatenate([cos_row, sin_row], 1).astype(jnp.bfloat16)
    cos_all, sin_all = tables(band_freqs, 0, N)
    col_table = jnp.concatenate(
        [jnp.concatenate([cos_all.T, sin_all.T], 1), jnp.concatenate([-sin_all.T, cos_all.T], 1)], 0
    ).astype(jnp.bfloat16)

    def one_field(total_sum, field_item):
        kern_re, kern_im, eigen_one = field_item
        prod_re = spec_re * kern_re - spec_im * kern_im
        prod_im = spec_re * kern_im + spec_im * kern_re
        spectral_block = jnp.concatenate(
            [jnp.concatenate([prod_re, prod_im], 1), jnp.concatenate([-prod_im, prod_re], 1)], 0
        ).astype(jnp.bfloat16)
        row_field = (
            jnp.dot(row_table, spectral_block, preferred_element_type=jnp.float32) / W
        ).astype(jnp.bfloat16)
        field_pair = jnp.dot(row_field, col_table, preferred_element_type=jnp.float32)
        power = field_pair[:, :N] * field_pair[:, :N] + field_pair[:, N:] * field_pair[:, N:]
        return (total_sum + eigen_one * power, None)

    partial_sum, unused = lax.scan(
        one_field, jnp.zeros((rows, N), jnp.float32), (kernels[0], kernels[1], eigen_values)
    )
    whole_image = lax.psum(partial_sum, "kern") / FIELDS

    def extend_rows(stacked):
        padded = padded_2(stacked, (("slab", 1),), 1)
        return jnp.concatenate([padded[:, :, -1:], padded, padded[:, :, :1]], 2)

    whole_acid = bake(whole_image, bake_rates, extend_rows)
    aerial_image = lax.dynamic_slice_in_dim(whole_image, col_first, cols, 1)
    latent_acid = lax.dynamic_slice_in_dim(whole_acid, col_first, cols, 1)
    return (aerial_image, latent_acid)


def solution(mesh):
    return jax.shard_map(
        shards,
        mesh=mesh,
        in_specs=(P("slab", "kern"), P(), P(None, "kern", None, None), P("kern"), P()),
        out_specs=(P("slab", "kern"), P("slab", "kern")),
        check_vma=False,
    )
```

profile of v0, /device:TPU:1, one launch (start us, length us, event | category | flops | bytes accessed | tf_op | source)
XLA Modules:
  0.0 427.0 jit_solution(13018393930706624220)
XLA Ops:
  7.3 3.4 convolution_negate_fusion
  10.7 2.5 fusion.68
  16.3 9.7 %fusion.63 = (bf16[128,4096]{1,0:T(8,128)(2,1)S(1)}, bf16[128,4096]{1,0:T(8,128)(2,1)S(1)}, bf16[128,4096]{1,0:T(8,128)(2,1)}) fusion(s32[128]{0:T(128)S(1)} %copy-done.3), kind=kLoop, calls=%fused_computation.106 | loop fusion | flops 9437184 | bytes 3146240 | tf_op jit(solution)/shard_map/convert.11
  26.0 2.7 slice_bitcast_fusion.1
  28.6 12.2 %maximum_maximum_fusion = bf16[256,8192]{1,0:T(8,128)(2,1)} fusion(bf16[128,4096]{1,0:T(8,128)(2,1)} %get-tuple-element.122, bf16[128,4096]{1,0:T(8,128)(2,1)S(1)} %get-tuple-element.121, bf16[128,4096]{1,0:T(8,128)(2,1)S(1)} %get-tuple-element.120), kind=kLoop, calls=%fused_computation.26 | loop fusion | flops 16777216 | bytes 7340032 | tf_op jit(solution)/shard_map/concatenate | solution.py:95
  40.8 223.5 %all-reduce.4.cloned.1.call-done = f32[2,128,128]{2,1,0:T(8,128)} async-done(((f32[2,128,128]{2,1,0:T(8,128)}), f32[2,128,128]{2,1,0:T(8,128)}) %all-reduce.4.cloned.1.call-update) | async-done | bytes 131088 | tf_op jit(solution)/shard_map/psum | solution.py:90
  265.3 72.9 %while.11 = (s32[]{:T(128)}, f32[64,4096]{1,0:T(8,128)S(1)}, f32[12]{0:T(128)S(1)}, f32[12,128,128]{2,1,0:T(8,128)}, f32[128,128]{1,0:T(8,128)S(1)}, /*index=5*/...) while((s32[]{:T(128)}, f32[64,4096]{1,0:T(8,128)S(1)}, ...), condition=%wide.region_2.3_spmd.clone, body=%wide.region_1.2_spmd.clone.sunk | while | flops 279117824 | bytes 11108491 | solution.py:113
  265.3 0.9 fusion.142
  266.2 3.3 fusion.143
  270.1 1.2 fusion.144
  271.4 0.9 fusion.142
  272.3 3.3 fusion.143
  276.2 1.2 fusion.144
  277.4 0.9 fusion.142
  278.3 3.3 fusion.143
  282.3 1.2 fusion.144
  283.5 0.9 fusion.142
  284.4 3.3 fusion.143
  288.3 1.2 fusion.144
  289.6 0.9 fusion.142
  290.5 3.3 fusion.143
  294.4 1.2 fusion.144
  295.6 0.9 fusion.142
  296.6 3.3 fusion.143
  300.5 1.2 fusion.144
  301.7 0.9 fusion.142
  302.6 3.3 fusion.143
  306.5 1.2 fusion.144
  308.7 3.3 fusion.143
  312.6 1.2 fusion.144
  314.8 3.3 fusion.143
  318.7 1.2 fusion.144
  320.9 3.3 fusion.143
  324.8 1.2 fusion.144
  326.9 3.3 fusion.143
  330.8 1.2 fusion.144
  333.0 3.3 fusion.143
  336.9 1.2 fusion.144
  338.1 1.0 copy-done
  340.5 42.9 %all-reduce.6.cloned.1.call-done = f32[64,4096]{1,0:T(8,128)} async-done(((f32[64,4096]{1,0:T(8,128)}), f32[64,4096]{1,0:T(8,128)}) %all-reduce.6.cloned.1.call-update) | async-done | bytes 1048592 | tf_op jit(solution)/shard_map/psum | solution.py:116
  383.4 2.1 add_multiply_fusion
  386.3 7.6 %collective-permute-start = (f32[2,1,4096]{2,1,0:T(1,128)S(1)}, f32[2,1,4096]{2,1,0:T(1,128)S(1)}, u32[]{:S(2)}, u32[]{:S(2)}) collective-permute-start(f32[2,1,4096]{2,1,0:T(1,128)S(1)} %get-tuple-element.110), channel_id=1, source_target_pairs={{1,0},{2,1},{3,2},{4,3},{5,4},{6,5},{7,6},{8,7},{9,8},{10,9},{11,1... | collective-permute-start | bytes 98312 | tf_op jit(solution)/shard_map/ppermute | solution.py:26
  395.4 8.0 %collective-permute-done.1 = f32[2,1,4096]{2,1,0:T(1,128)S(1)} collective-permute-done((f32[2,1,4096]{2,1,0:T(1,128)S(1)}, f32[2,1,4096]{2,1,0:T(1,128)S(1)}, u32[]{:S(2)}, u32[]{:S(2)}) %collective-permute-start.1) | collective-permute-done | bytes 32800 | tf_op jit(solution)/shard_map/ppermute | solution.py:24
  403.4 2.5 fusion.31
  405.9 2.4 fusion.61
  408.5 1.5 collective-permute-start.3
  411.3 6.4 %collective-permute-done.3 = f32[2,1,4096]{2,1,0:T(1,128)S(1)} collective-permute-done((f32[2,1,4096]{2,1,0:T(1,128)S(1)}, f32[2,1,4096]{2,1,0:T(1,128)S(1)}, u32[]{:S(2)}, u32[]{:S(2)}) %collective-permute-start.3) | collective-permute-done | bytes 32800 | tf_op jit(solution)/shard_map/ppermute | solution.py:24
  417.7 1.7 fusion.49
  (65 shorter events, 20.1 us)
Async XLA Ops:
  7.2 3.5 copy-start.4
  7.2 3.5 copy-start.3
  7.2 257.2 %all-reduce.4.cloned.1.call-start = ((), (), s32[]{:S(2)}) async-start(), calls=%async_computation | async-start | bytes 262144 | tf_op jit(solution)/shard_map/psum | solution.py:90
  15.8 367.6 %all-reduce.6.cloned.1.call-start = ((), (), s32[]{:S(2)}) async-start(), calls=%async_computation.1 | async-start | bytes 2097152 | tf_op jit(solution)/shard_map/psum | solution.py:116
  28.6 236.6 %copy-start.5 = (f32[12]{0:T(128)S(1)}, f32[12]{0:T(128)}, u32[]{:S(2)}) copy-start(f32[12]{0:T(128)} %param.10) | copy-start | bytes 148
  265.3 73.9 %copy-start.2 = (f32[5]{0:T(128)S(1)}, f32[5]{0:T(128)}, u32[]{:S(2)}) copy-start(f32[5]{0:T(128)} %param.11) | copy-start | bytes 64
  338.1 1.0 copy-start
  386.3 9.1 %collective-permute-start = (f32[2,1,4096]{2,1,0:T(1,128)S(1)}, f32[2,1,4096]{2,1,0:T(1,128)S(1)}, u32[]{:S(2)}, u32[]{:S(2)}) collective-permute-start(f32[2,1,4096]{2,1,0:T(1,128)S(1)} %get-tuple-element.110), channel_id=1, source_target_pairs={{1,0},{2,1},{3,2},{4,3},{5,4},{6,5},{7,6},{8,7},{9,8},{10,9},{11,1... | collective-permute-start | bytes 98312 | tf_op jit(solution)/shard_map/ppermute | solution.py:26
  393.9 9.5 %collective-permute-start.1 = (f32[2,1,4096]{2,1,0:T(1,128)S(1)}, f32[2,1,4096]{2,1,0:T(1,128)S(1)}, u32[]{:S(2)}, u32[]{:S(2)}) collective-permute-start(f32[2,1,4096]{2,1,0:T(1,128)S(1)} %get-tuple-element.109), channel_id=1, source_target_pairs={{0,1},{1,2},{2,3},{3,4},{4,5},{5,6},{6,7},{7,8},{8,9},{9,10},{10,1... | collective-permute-start | bytes 98312 | tf_op jit(solution)/shard_map/ppermute | solution.py:24
  395.4 10.6 %copy-start.1 = (f32[64,4096]{1,0:T(8,128)S(1)}, f32[64,4096]{1,0:T(8,128)}, u32[]{:S(2)}) copy-start(f32[64,4096]{1,0:T(8,128)} %all-reduce.6.cloned.1.call-done) | copy-start | bytes 3145732
  408.4 2.8 collective-permute-start.2
  408.5 9.2 %collective-permute-start.3 = (f32[2,1,4096]{2,1,0:T(1,128)S(1)}, f32[2,1,4096]{2,1,0:T(1,128)S(1)}, u32[]{:S(2)}, u32[]{:S(2)}) collective-permute-start(f32[2,1,4096]{2,1,0:T(1,128)S(1)} %get-tuple-element.103), channel_id=1, source_target_pairs={{0,1},{1,2},{2,3},{3,4},{4,5},{5,6},{6,7},{7,8},{8,9},{9,10},{10,1... | collective-permute-start | bytes 98312 | tf_op jit(solution)/shard_map/ppermute | solution.py:24
Sparse Core Ops, SparseCore 0:
  15.9 248.3 all-reduce.3
  339.3 44.1 all-reduce.5
where the time goes:
time: 429 us; the launch traced here: 427 us
  waiting for transfers between devices  281 us (66%)
  other arithmetic  58.7 us (14%)
  matrix products  47.6 us (11%)
  between operations  15.6 us (4%)
  local copies, waits for them, and re-layouts  13.8 us (3%)
  starting transfers between devices  9.44 us (2%)
    psum x1, waiting for transfers between devices, shards(): spectrum = lax.psum(jnp.stack([first, second]), ('kern', 'slab'))  224 us
    psum x1, waiting for transfers between devices, shards(): whole_image = lax.psum(partial_sum, 'kern') / FIELDS  42.9 us
    dot_general x12, matrix products, one_field(): jnp.dot(row_field, col_table, preferred_element_type=jnp.float32)  39.8 us
    another operation x26, other arithmetic  20.8 us
    add x12, other arithmetic, one_field(): return (total_sum + eigen_one * power, None)  14.7 us
    ppermute x2, waiting for transfers between devices, padded_2(): lax.ppermute(tail, axis, [(i, (i + 1) % count) for i in range(count)])  14.4 us
    concatenate x1, other arithmetic, shards(): jnp.concatenate([jnp.concatenate([cos_all.T, sin_all.T], 1), jnp.concaten...  12.2 us
  transfers between devices with their start and end apart: 6, of which 5 were waited for; matrix products, arithmetic and copies ran while one was open for 6% of the time, Pallas kernels for 0%

commit v1 on v0

v1 whole, which is shorter than its diff:
```python
import math

import jax
import jax.numpy as jnp
from jax import lax
from jax.experimental import pallas as pl
from jax.experimental.pallas import tpu as pltpu
from jax.sharding import PartitionSpec as P

N = 4096
W = 128
FIELDS = 48
STEPS = 2

ROWS = 64
COLS = 1024
RING_ROWS = 72
MXU_ROWS = 80
RING_COLS = 1152
WIDE = 2304
ALL = ("kern", "slab")
CHIP_Z, CORES, FAR_Z, SIDE = 2, 2, 4, 4


def device(z_lo, core, z_hi, y, x):
    return (z_lo * CORES + core) * 64 + (z_hi * SIDE + y) * SIDE + x


def column_groups():
    return [
        [device(a, b, c, y, x) for a in range(CHIP_Z) for b in range(CORES) for c in range(FAR_Z)]
        for y in range(SIDE)
        for x in range(SIDE)
    ]


def plane_groups():
    return [
        [device(a, b, c, y, x) for y in range(SIDE) for x in range(SIDE)]
        for a in range(CHIP_Z)
        for b in range(CORES)
        for c in range(FAR_Z)
    ]


def cos_sin(turns):
    m = jnp.bitwise_and(turns, N - 1)
    quarter = jnp.right_shift(m + N // 8, 10)
    t = (m - jnp.left_shift(quarter, 10)).astype(jnp.float32) * (2.0 * math.pi / N)
    t2 = t * t
    s = t * (1.0 + t2 * (-1.0 / 6 + t2 * (1.0 / 120 + t2 * (-1.0 / 5040 + t2 * (1.0 / 362880)))))
    c = 1.0 + t2 * (-0.5 + t2 * (1.0 / 24 + t2 * (-1.0 / 720 + t2 * (1.0 / 40320))))
    odd = jnp.bitwise_and(quarter, 1) == 1
    cos = jnp.where(odd, s, c)
    sin = jnp.where(odd, c, s)
    cos = jnp.where(jnp.bitwise_and(quarter + 1, 2) == 2, -cos, cos)
    sin = jnp.where(jnp.bitwise_and(quarter, 2) == 2, -sin, sin)
    return cos, sin


def split(values):
    high = values.astype(jnp.bfloat16)
    return high, (values - high.astype(jnp.float32)).astype(jnp.bfloat16)


def iota(shape, dim):
    return lax.broadcasted_iota(jnp.int32, shape, dim)


def transform_kernel(layout_ref, freqs_ref, out_ref, table):
    row_first = lax.axis_index("slab") * ROWS
    col_first = lax.axis_index("kern") * COLS
    freqs = freqs_ref[...]
    step = 32
    base_cos, base_sin = cos_sin((col_first + iota((step, W), 0)) * freqs)
    turn_cos, turn_sin = cos_sin((step * iota((COLS // step, W), 0)) * freqs)
    for a in range(COLS // step):
        ca, sa = turn_cos[a : a + 1, :], turn_sin[a : a + 1, :]
        cos = ca * base_cos - sa * base_sin
        sin = sa * base_cos + ca * base_sin
        cos_high, cos_low = split(cos)
        sin_high, sin_low = split(sin)
        at = pl.ds(a * step, step)
        table[at, 0:W] = cos_high
        table[at, W : 2 * W] = sin_high
        table[at, 2 * W : 3 * W] = cos_low
        table[at, 3 * W : 4 * W] = sin_low
    transmit = (2 * layout_ref[...] - 1).astype(jnp.float32).astype(jnp.bfloat16)
    along = jnp.dot(transmit, table[...], preferred_element_type=jnp.float32)
    along_re = along[:, 0:W] + along[:, 2 * W : 3 * W]
    along_im = -(along[:, W : 2 * W] + along[:, 3 * W : 4 * W])
    cos_row, sin_row = cos_sin((row_first + iota((ROWS, W), 0)) * freqs)
    left_high, left_low = split(jnp.concatenate([cos_row, sin_row], 0))
    right = jnp.concatenate(
        [
            jnp.concatenate([along_re, along_im], 1),
            jnp.concatenate([along_im, -along_re], 1),
        ],
        0,
    )
    right_high, right_low = split(right)
    both = lax.dot_general(
        jnp.concatenate([left_high, left_high, left_low], 0),
        jnp.concatenate([right_high, right_low, right_high], 0),
        (((0,), (0,)), ((), ())),
        preferred_element_type=jnp.float32,
    ) * (1.0 / N)
    out_ref[0:W, :] = both[:, 0:W]
    out_ref[W : 2 * W, :] = both[:, W : 2 * W]


def image_kernel(
    spec_ref, near_ref, far_ref, near_eigen, far_eigen, freqs_ref, freqs_col_ref,
    send_ref, keep_ref, table_re, table_im, fields, image,
):
    row_first = lax.axis_index("slab") * ROWS
    kern = lax.axis_index("kern")
    core = lax.rem(kern, CORES)
    wide_first = (kern - core) * COLS - 128

    freqs_col = jnp.broadcast_to(freqs_col_ref[...], (W, 128))
    cos, sin = cos_sin((wide_first + iota((W, 128), 1)) * freqs_col)
    turn_cos, turn_sin = cos_sin(128 * freqs_col)
    for tile in range(WIDE // 128):
        at = pl.ds(tile * 128, 128)
        table_re[0:W, at] = cos.astype(jnp.bfloat16)
        table_re[W : 2 * W, at] = (-sin).astype(jnp.bfloat16)
        table_im[0:W, at] = sin.astype(jnp.bfloat16)
        table_im[W : 2 * W, at] = cos.astype(jnp.bfloat16)
        cos, sin = cos * turn_cos - sin * turn_sin, sin * turn_cos + cos * turn_sin

    place = iota((MXU_ROWS, W), 0)
    place = jnp.where(place < ROWS + 4, place, place - RING_ROWS)
    cos_row, sin_row = cos_sin((row_first + place) * freqs_ref[...])
    row_table = jnp.concatenate([cos_row, sin_row], 1).astype(jnp.bfloat16)

    spec_re = spec_ref[0:W, :]
    spec_im = spec_ref[W : 2 * W, :]
    own = near_ref.shape[1]
    for kernels_ref, first in ((near_ref, 0), (far_ref, own)):

        def one_row_field(f, carry, kernels_ref=kernels_ref, first=first):
            kern_re = kernels_ref[0, f]
            kern_im = kernels_ref[1, f]
            prod_re = spec_re * kern_re - spec_im * kern_im
            prod_im = spec_re * kern_im + spec_im * kern_re
            re16 = prod_re.astype(jnp.bfloat16)
            im16 = prod_im.astype(jnp.bfloat16)
            block = jnp.concatenate(
                [
                    jnp.concatenate([re16, im16], 1),
                    jnp.concatenate([-im16, re16], 1),
                ],
                0,
            )
            row_field = jnp.dot(row_table, block, preferred_element_type=jnp.float32) / W
            at = pl.multiple_of((first + f) * MXU_ROWS, MXU_ROWS)
            fields[pl.ds(at, MXU_ROWS), :] = row_field.astype(jnp.bfloat16)
            return carry

        lax.fori_loop(0, own, one_row_field, 0, unroll=2)

    def one_pair(p, carry):
        at = pl.ds(pl.multiple_of(p * 256, 256), 256)
        rows = fields[...]
        real = jnp.dot(rows, table_re[:, at], preferred_element_type=jnp.float32)
        imag = jnp.dot(rows, table_im[:, at], preferred_element_type=jnp.float32)
        total = jnp.zeros((RING_ROWS, 256), jnp.float32)
        for f in range(2 * own):
            eigen = near_eigen[f] if f < own else far_eigen[f - own]
            re = real[f * MXU_ROWS : f * MXU_ROWS + RING_ROWS]
            im = imag[f * MXU_ROWS : f * MXU_ROWS + RING_ROWS]
            total = total + eigen * (re * re + im * im)
        image[:, at] = total
        return carry

    lax.fori_loop(0, WIDE // 256, one_pair, 0)

    for ref, which in ((keep_ref, core), (send_ref, 1 - core)):
        start = which * COLS
        before = image[:, pl.ds(pl.multiple_of(start, 128), 128)]
        after = image[:, pl.ds(pl.multiple_of(start + 128 + COLS, 128), 128)]
        ref[:, 0:COLS] = image[:, pl.ds(pl.multiple_of(start + 128, 128), COLS)]
        ref[:, COLS:RING_COLS] = jnp.where(iota((RING_ROWS, 128), 1) < 64, after, before)


def laplace(field):
    rows, cols = field.shape
    return (
        pltpu.roll(field, 1, 0)
        + pltpu.roll(field, rows - 1, 0)
        + pltpu.roll(field, 1, 1)
        + pltpu.roll(field, cols - 1, 1)
        - 4.0 * field
    )


def bake_kernel(keep_ref, got_ref, rates, image_ref, acid_ref):
    dill_rate, acid_rate, quench_rate, react_rate, quench_start = (rates[i] for i in range(5))
    aerial_image = (keep_ref[...] + got_ref[...]) / FIELDS
    image_ref[...] = aerial_image[0:ROWS, 0:COLS]
    acid_field = 1.0 - jnp.exp((-4.0 * dill_rate) * aerial_image)
    acid_diffusion = acid_rate * (0.5 + 0.5 * acid_field)
    quencher = jnp.zeros_like(acid_field) + quench_start
    for bake_step in range(STEPS):
        reaction = (4.0 * react_rate) * acid_field * quencher
        new_acid = acid_field + acid_diffusion * laplace(acid_field) - reaction
        quencher = quencher + quench_rate * laplace(quencher) - reaction
        acid_field = new_acid
    acid_ref[...] = acid_field[0:ROWS, 0:COLS]


VMEM = pl.BlockSpec(memory_space=pltpu.VMEM)
SMEM = pl.BlockSpec(memory_space=pltpu.SMEM)


def sum_everywhere(part):
    ring, plane = column_groups(), plane_groups()
    count = len(ring[0])
    piece = part.shape[0] // count

    def exchange(blocks, groups):
        return lax.all_to_all(blocks, ALL, 0, 0, tiled=True, axis_index_groups=groups)

    def total(blocks):
        return jnp.sum(blocks.reshape(-1, piece, part.shape[1]), 0)

    def copies(block, many):
        return jnp.broadcast_to(block[None], (many,) + block.shape).reshape(-1, block.shape[1])

    some = total(exchange(part, ring))
    full = total(exchange(copies(some, len(plane[0])), plane))
    return exchange(copies(full, count), ring)


def shards(layout, band_freqs, kernels, eigen_values, bake_rates):
    freqs = band_freqs.reshape(1, W)
    freqs_col = band_freqs.reshape(W, 1)
    f32 = jnp.float32
    across_z = [(i, (i + 128) % 256) for i in range(256)]
    far_kernels = lax.ppermute(kernels, ALL, across_z)
    far_eigen = lax.ppermute(eigen_values, ALL, across_z)
    part = pl.pallas_call(
        transform_kernel,
        out_shape=jax.ShapeDtypeStruct((2 * W, W), f32),
        in_specs=[VMEM, VMEM],
        out_specs=VMEM,
        scratch_shapes=[pltpu.VMEM((COLS, 4 * W), jnp.bfloat16)],
        name="transform",
    )(layout, freqs)
    spectrum = sum_everywhere(part)
    half = jax.ShapeDtypeStruct((RING_ROWS, RING_COLS), f32)
    own = kernels.shape[1]
    send, keep = pl.pallas_call(
        image_kernel,
        out_shape=(half, half),
        in_specs=[VMEM, VMEM, VMEM, SMEM, SMEM, VMEM, VMEM],
        out_specs=(VMEM, VMEM),
        scratch_shapes=[
            pltpu.VMEM((2 * W, WIDE), jnp.bfloat16),
            pltpu.VMEM((2 * W, WIDE), jnp.bfloat16),
            pltpu.VMEM((2 * own * MXU_ROWS, 2 * W), jnp.bfloat16),
            pltpu.VMEM((RING_ROWS, WIDE), f32),
        ],
        name="image",
    )(spectrum, kernels, far_kernels, eigen_values, far_eigen, freqs, freqs_col)
    across_cores = [(i, i + 64 if (i // 64) % 2 == 0 else i - 64) for i in range(256)]
    got = lax.ppermute(send, ALL, across_cores)
    block = jax.ShapeDtypeStruct((ROWS, COLS), f32)
    return pl.pallas_call(
        bake_kernel,
        out_shape=(block, block),
        in_specs=[VMEM, VMEM, SMEM],
        out_specs=(VMEM, VMEM),
        name="bake",
    )(keep, got, bake_rates)


def solution(mesh):
    return jax.shard_map(
        shards,
        mesh=mesh,
        in_specs=(P("slab", "kern"), P(), P(None, "kern", None, None), P("kern"), P()),
        out_specs=(P("slab", "kern"), P("slab", "kern")),
        check_vma=False,
    )
```

time: 429 us -> 93.6 us (0.22)
  waiting for transfers between devices: 281 us -> 8.6 us
  other arithmetic: 58.7 us -> 0.04 us
  blocking collectives: 0 us -> 55 us
  matrix products: 47.6 us -> 0 us
  Pallas kernels: 0 us -> 16.9 us
  between operations: 15.6 us -> 0.68 us
  local copies, waits for them, and re-layouts: 13.8 us -> 3.36 us
    psum x2 -> x0, waiting for transfers between devices: 266 us -> none  [the longest x1 224 us: shards(): spectrum = lax.psum(jnp.stack([first, second]), ('kern', 'slab'))]
    all_to_all x0 -> x2, blocking collectives: none -> 55 us  [exchange(): lax.all_to_all(blocks, ALL, 0, 0, tiled=True, axis_index_groups=groups)]
    dot_general x18 -> x0, matrix products: 47.6 us -> none  [the longest x12 39.8 us: one_field(): jnp.dot(row_field, col_table, preferred_element_type=jnp.float32)]
    another operation x28 -> x0, other arithmetic: 21.5 us -> none
    pallas_call x0 -> x3, Pallas kernels: none -> 16.9 us  [the longest x1 12.2 us: shards(): pl.pallas_call(image_kernel, out_shape=(half, half), in_specs=[VMEM, VMEM...]
    add x14 -> x0, other arithmetic: 14.7 us -> none  [the longest x12 14.7 us: one_field(): return (total_sum + eigen_one * power, None)]
    concatenate x2 -> x0, other arithmetic: 12.2 us -> none  [the longest x1 12.2 us: shards(): jnp.concatenate([jnp.concatenate([cos_all.T, sin_all.T], 1), jnp.concaten...]
    ppermute x4 -> x3, waiting for transfers between devices: 15 us -> 3.29 us  [the longest x1 1.84 us: shards(): got = lax.ppermute(send, ALL, across_cores)]
  transfers between devices with their start and end apart: 6 -> 4, of which waited for: 5 -> 3; matrix products, arithmetic and copies ran while one was open for 6% -> 2% of each run, Pallas kernels for 0% -> 3%
where the time goes in v1:
time: 93.6 us; the launch traced here: 93.3 us
  blocking collectives  55 us (59%)
  Pallas kernels  16.9 us (18%)
  starting transfers between devices  8.69 us (9%)
  waiting for transfers between devices  8.6 us (9%)
  local copies, waits for them, and re-layouts  3.36 us (4%)
    all_to_all x2, blocking collectives, exchange(): lax.all_to_all(blocks, ALL, 0, 0, tiled=True, axis_index_groups=groups)  55 us
    pallas_call x1, Pallas kernels, shards(): pl.pallas_call(image_kernel, out_shape=(half, half), in_specs=[VMEM, VMEM...  12.2 us
    all_to_all x1, waiting for transfers between devices, exchange(): lax.all_to_all(blocks, ALL, 0, 0, tiled=True, axis_index_groups=groups)  5.3 us
    all_to_all x1, starting transfers between devices, exchange(): lax.all_to_all(blocks, ALL, 0, 0, tiled=True, axis_index_groups=groups)  4.71 us
    ppermute x1, starting transfers between devices, shards(): far_kernels = lax.ppermute(kernels, ALL, across_z)  2.54 us
    pallas_call x1, Pallas kernels, shards(): pl.pallas_call(transform_kernel, out_shape=jax.ShapeDtypeStruct((2 * W, W...  2.43 us
    pallas_call x1, Pallas kernels, shards(): pl.pallas_call(bake_kernel, out_shape=(block, block), in_specs=[VMEM, VME...  2.23 us
    unnamed x12, local copies, waits for them, and re-layouts  1.94 us
  transfers between devices with their start and end apart: 4, of which 3 were waited for; matrix products, arithmetic and copies ran while one was open for 2% of the time, Pallas kernels for 3%

profile of v1, /device:TPU:1, one launch (start us, length us, event | category | flops | bytes accessed | tf_op | source)
XLA Modules:
  0.0 93.3 jit_solution(15512053418505045741)
XLA Ops:
  0.6 0.0 copy-start.3
  0.6 0.0 copy-start.4
  0.7 2.5 %collective-permute-start = (f32[2,12,128,128]{3,2,1,0:T(8,128)}, f32[2,12,128,128]{3,2,1,0:T(8,128)S(1)}, u32[]{:S(2)}, u32[]{:S(2)}) collective-permute-start(f32[2,12,128,128]{3,2,1,0:T(8,128)} %near_ref.1), channel_id=1, source_target_pairs={{0,128},{1,129},{2,130},{3,131},{4,132},{5,133},{6,134},{7,135},{8... | collective-permute-start | bytes 4718600 | tf_op jit(solution)/shard_map/ppermute | solution.py:241
  3.2 2.4 %transform.1 = f32[256,128]{1,0:T(8,128)} custom-call(s32[64,1024]{1,0:T(8,128)} %layout_ref.1, s32[1,128]{1,0:T(1,128)} %bitcast.6), custom_call_target="tpu_custom_call" | custom-call | tf_op jit(solution)/shard_map/transform/pallas_call | solution.py:243
  5.6 41.3 %all_to_all.23 = f32[16,16,128]{2,1,0:T(8,128)S(1)} all-to-all(f32[16,16,128]{2,1,0:T(8,128)} %bitcast.4), channel_id=1, replica_groups={{0,16,32,48,64,80,96,112,128,144,160,176,192,208,224,240},{1,17,33,49,6..., dimensions={0} | all-to-all | bytes 262144 | tf_op jit(solution)/shard_map/all_to_all | solution.py:223
  46.9 13.8 %all_to_all.24 = f32[16,16,128]{2,1,0:T(8,128)S(1)} all-to-all(f32[16,16,128]{2,1,0:T(8,128)S(1)} %broadcast_in_dim.4), channel_id=1, replica_groups={{0,1,2,3,4,5,6,7,8,9,10,11,12,13,14,15},{16,17,18,19,20,21,22,23,24,25,..., dimensions={0} | all-to-all | bytes 262144 | tf_op jit(solution)/shard_map/all_to_all | solution.py:223
  60.7 0.7 broadcast_in_dim.5
  61.4 4.7 %all-to-all-start.2 = ((f32[16,16,128]{2,1,0:T(8,128)}), f32[16,16,128]{2,1,0:T(8,128)S(1)}, u32[]{:S(2)}, u32[]{:S(2)}) async-start(f32[16,16,128]{2,1,0:T(8,128)} %broadcast_in_dim.5), calls=%async_computation.2 | async-start | bytes 262144 | tf_op jit(solution)/shard_map/all_to_all | solution.py:223
  66.1 0.0 copy-done.4
  66.1 1.4 %collective-permute-start.1 = (f32[12]{0:T(128)S(1)}, f32[12]{0:T(128)S(1)}, u32[]{:S(2)}, u32[]{:S(2)}) collective-permute-start(f32[12]{0:T(128)S(1)} %copy-done.4), channel_id=1, source_target_pairs={{0,128},{1,129},{2,130},{3,131},{4,132},{5,133},{6,134},{7,135},{8... | collective-permute-start | bytes 152 | tf_op jit(solution)/shard_map/ppermute | solution.py:242
  67.5 0.0 copy-done.3
  67.5 0.7 copy.8.freqs_col_ref
  68.3 1.4 %collective-permute-done.1.far_eigen = f32[12]{0:T(128)S(1)} collective-permute-done((f32[12]{0:T(128)S(1)}, f32[12]{0:T(128)S(1)}, u32[]{:S(2)}, u32[]{:S(2)}) %collective-permute-start.1) | collective-permute-done | bytes 80 | tf_op jit(solution)/shard_map/ppermute | solution.py:242
  69.7 0.0 copy-start.5
  69.7 5.3 %all-to-all-done.2 = f32[16,16,128]{2,1,0:T(8,128)S(1)} async-done(((f32[16,16,128]{2,1,0:T(8,128)}), f32[16,16,128]{2,1,0:T(8,128)S(1)}, u32[]{:S(2)}, u32[]{:S(2)}) %all-to-all-start.2) | async-done | bytes 131104 | tf_op jit(solution)/shard_map/all_to_all | solution.py:223
  75.0 0.0 copy-start.1
  75.0 0.0 collective-permute-done.far_ref
  75.0 0.0 copy-start
  75.0 0.0 copy-done.5
  75.0 0.6 copy-done.1
  75.7 0.5 copy-done
  76.2 12.2 %image.1 = (f32[72,1152]{1,0:T(8,128)}, f32[72,1152]{1,0:T(8,128)}) custom-call(f32[256,128]{1,0:T(8,128)} %bitcast.5, f32[2,12,128,128]{3,2,1,0:T(8,128)} %near_ref.1, f32[2,12,128,128]{3,2,1,0:T(8,128)} %copy-done, f32[12]{0:T(128)} %near_eigen.1, f32[12]{0:T(128)} %copy-done.5, s32[1,128]{1,0:T(1,128)} %bitcast.7, s32[128,1]{1,0:T(8,128)} %copy.8.freqs_col_ref), custom_call_target="tpu_custom_call" | custom-call | tf_op jit(solution)/shard_map/image/pallas_call | solution.py:254
  88.5 0.0 collective-permute-start.2
  88.5 1.8 %collective-permute-done.2.got_ref = f32[72,1152]{1,0:T(8,128)S(1)} collective-permute-done((f32[72,1152]{1,0:T(8,128)}, f32[72,1152]{1,0:T(8,128)S(1)}, u32[]{:S(2)}, u32[]{:S(2)}) %collective-permute-start.2) | collective-permute-done | bytes 331808 | tf_op jit(solution)/shard_map/ppermute | solution.py:268
  90.3 0.0 copy-start.2
  90.3 0.7 copy-done.2
  91.0 2.2 %bake.1 = (f32[64,1024]{1,0:T(8,128)}, f32[64,1024]{1,0:T(8,128)}) custom-call(f32[72,1152]{1,0:T(8,128)} %get-tuple-element.4.keep_ref, f32[72,1152]{1,0:T(8,128)} %copy-done.2, f32[5]{0:T(128)} %rates.1), custom_call_target="tpu_custom_call" | custom-call | tf_op jit(solution)/shard_map/bake/pallas_call | solution.py:270
  (3 shorter events, 0.0 us)
Async XLA Ops:
  0.6 66.9 %copy-start.3 = (s32[128]{0:T(128)S(1)}, s32[128]{0:T(128)}, u32[]{:S(2)}) copy-start(s32[128]{0:T(128)} %param.6) | copy-start | bytes 1540
  0.6 65.4 %copy-start.4 = (f32[12]{0:T(128)S(1)}, f32[12]{0:T(128)}, u32[]{:S(2)}) copy-start(f32[12]{0:T(128)} %near_eigen.1) | copy-start | bytes 148
  0.7 74.4 %collective-permute-start = (f32[2,12,128,128]{3,2,1,0:T(8,128)}, f32[2,12,128,128]{3,2,1,0:T(8,128)S(1)}, u32[]{:S(2)}, u32[]{:S(2)}) collective-permute-start(f32[2,12,128,128]{3,2,1,0:T(8,128)} %near_ref.1), channel_id=1, source_target_pairs={{0,128},{1,129},{2,130},{3,131},{4,132},{5,133},{6,134},{7,135},{8... | collective-permute-start | bytes 4718600 | tf_op jit(solution)/shard_map/ppermute | solution.py:241
  61.4 13.7 %all-to-all-start.2 = ((f32[16,16,128]{2,1,0:T(8,128)}), f32[16,16,128]{2,1,0:T(8,128)S(1)}, u32[]{:S(2)}, u32[]{:S(2)}) async-start(f32[16,16,128]{2,1,0:T(8,128)} %broadcast_in_dim.5), calls=%async_computation.2 | async-start | bytes 262144 | tf_op jit(solution)/shard_map/all_to_all | solution.py:223
  66.1 3.6 %collective-permute-start.1 = (f32[12]{0:T(128)S(1)}, f32[12]{0:T(128)S(1)}, u32[]{:S(2)}, u32[]{:S(2)}) collective-permute-start(f32[12]{0:T(128)S(1)} %copy-done.4), channel_id=1, source_target_pairs={{0,128},{1,129},{2,130},{3,131},{4,132},{5,133},{6,134},{7,135},{8... | collective-permute-start | bytes 152 | tf_op jit(solution)/shard_map/ppermute | solution.py:242
  69.7 5.3 %copy-start.5 = (f32[12]{0:T(128)}, f32[12]{0:T(128)S(1)}, u32[]{:S(2)}) copy-start(f32[12]{0:T(128)S(1)} %collective-permute-done.1.far_eigen) | copy-start | bytes 148
  75.0 0.7 copy-start.1
  75.0 1.2 %copy-start = (f32[2,12,128,128]{3,2,1,0:T(8,128)}, f32[2,12,128,128]{3,2,1,0:T(8,128)S(1)}, u32[]{:S(2)}) copy-start(f32[2,12,128,128]{3,2,1,0:T(8,128)S(1)} %collective-permute-done.far_ref) | copy-start | bytes 4718596
  88.5 1.8 %collective-permute-start.2 = (f32[72,1152]{1,0:T(8,128)}, f32[72,1152]{1,0:T(8,128)S(1)}, u32[]{:S(2)}, u32[]{:S(2)}) collective-permute-start(f32[72,1152]{1,0:T(8,128)} %get-tuple-element.5), channel_id=1, source_target_pairs={{0,64},{1,65},{2,66},{3,67},{4,68},{5,69},{6,70},{7,71},{8,72},{9,... | collective-permute-start | bytes 995336 | tf_op jit(solution)/shard_map/ppermute | solution.py:268
  90.3 0.7 copy-start.2

commit v2 on v1

--- a/solution.py
+++ b/solution.py
@@ -2,6 +2,8 @@
 
 import jax
 import jax.numpy as jnp
+import ml_dtypes
+import numpy as np
 from jax import lax
 from jax.experimental import pallas as pl
 from jax.experimental.pallas import tpu as pltpu
@@ -17,7 +19,9 @@
 RING_ROWS = 72
 MXU_ROWS = 80
 RING_COLS = 1152
-WIDE = 2304
+SPARSE = 4
+COARSE = N // SPARSE
+HALF = COARSE // 2
 ALL = ("kern", "slab")
 CHIP_Z, CORES, FAR_Z, SIDE = 2, 2, 4, 4
 
@@ -109,19 +113,15 @@
     out_ref[W : 2 * W, :] = both[:, W : 2 * W]
 
 
-def image_kernel(
-    spec_ref, near_ref, far_ref, near_eigen, far_eigen, freqs_ref, freqs_col_ref,
-    send_ref, keep_ref, table_re, table_im, fields, image,
-):
+def image_kernel(spec_ref, kernels_ref, eigen, freqs_ref, send_ref, keep_ref, table_re, table_im, fields):
     row_first = lax.axis_index("slab") * ROWS
-    kern = lax.axis_index("kern")
-    core = lax.rem(kern, CORES)
-    wide_first = (kern - core) * COLS - 128
-
-    freqs_col = jnp.broadcast_to(freqs_col_ref[...], (W, 128))
-    cos, sin = cos_sin((wide_first + iota((W, 128), 1)) * freqs_col)
-    turn_cos, turn_sin = cos_sin(128 * freqs_col)
-    for tile in range(WIDE // 128):
+    core = lax.rem(lax.axis_index("kern"), CORES)
+    freqs = freqs_ref[...]
+
+    freqs_col = jnp.broadcast_to(freqs, (W, W)).astype(jnp.float32).T.astype(jnp.int32)
+    cos, sin = cos_sin((SPARSE * iota((W, 128), 1)) * freqs_col)
+    turn_cos, turn_sin = cos_sin((SPARSE * 128) * freqs_col)
+    for tile in range(COARSE // 128):
         at = pl.ds(tile * 128, 128)
         table_re[0:W, at] = cos.astype(jnp.bfloat16)
         table_re[W : 2 * W, at] = (-sin).astype(jnp.bfloat16)
@@ -131,57 +131,46 @@
 
     place = iota((MXU_ROWS, W), 0)
     place = jnp.where(place < ROWS + 4, place, place - RING_ROWS)
-    cos_row, sin_row = cos_sin((row_first + place) * freqs_ref[...])
+    cos_row, sin_row = cos_sin((row_first + place) * freqs)
     row_table = jnp.concatenate([cos_row, sin_row], 1).astype(jnp.bfloat16)
 
     spec_re = spec_ref[0:W, :]
     spec_im = spec_ref[W : 2 * W, :]
-    own = near_ref.shape[1]
-    for kernels_ref, first in ((near_ref, 0), (far_ref, own)):
-
-        def one_row_field(f, carry, kernels_ref=kernels_ref, first=first):
-            kern_re = kernels_ref[0, f]
-            kern_im = kernels_ref[1, f]
-            prod_re = spec_re * kern_re - spec_im * kern_im
-            prod_im = spec_re * kern_im + spec_im * kern_re
-            re16 = prod_re.astype(jnp.bfloat16)
-            im16 = prod_im.astype(jnp.bfloat16)
-            block = jnp.concatenate(
-                [
-                    jnp.concatenate([re16, im16], 1),
-                    jnp.concatenate([-im16, re16], 1),
-                ],
-                0,
-            )
-            row_field = jnp.dot(row_table, block, preferred_element_type=jnp.float32) / W
-            at = pl.multiple_of((first + f) * MXU_ROWS, MXU_ROWS)
-            fields[pl.ds(at, MXU_ROWS), :] = row_field.astype(jnp.bfloat16)
-            return carry
-
-        lax.fori_loop(0, own, one_row_field, 0, unroll=2)
-
-    def one_pair(p, carry):
-        at = pl.ds(pl.multiple_of(p * 256, 256), 256)
-        rows = fields[...]
-        real = jnp.dot(rows, table_re[:, at], preferred_element_type=jnp.float32)
-        imag = jnp.dot(rows, table_im[:, at], preferred_element_type=jnp.float32)
-        total = jnp.zeros((RING_ROWS, 256), jnp.float32)
-        for f in range(2 * own):
-            eigen = near_eigen[f] if f < own else far_eigen[f - own]
-            re = real[f * MXU_ROWS : f * MXU_ROWS + RING_ROWS]
-            im = imag[f * MXU_ROWS : f * MXU_ROWS + RING_ROWS]
-            total = total + eigen * (re * re + im * im)
-        image[:, at] = total
-        return carry
-
-    lax.fori_loop(0, WIDE // 256, one_pair, 0)
-
-    for ref, which in ((keep_ref, core), (send_ref, 1 - core)):
-        start = which * COLS
-        before = image[:, pl.ds(pl.multiple_of(start, 128), 128)]
-        after = image[:, pl.ds(pl.multiple_of(start + 128 + COLS, 128), 128)]
-        ref[:, 0:COLS] = image[:, pl.ds(pl.multiple_of(start + 128, 128), COLS)]
-        ref[:, COLS:RING_COLS] = jnp.where(iota((RING_ROWS, 128), 1) < 64, after, before)
+    count = kernels_ref.shape[1]
+    for f in range(count):
+        kern_re = kernels_ref[0, f]
+        kern_im = kernels_ref[1, f]
+        re16 = (spec_re * kern_re - spec_im * kern_im).astype(jnp.bfloat16)
+        im16 = (spec_re * kern_im + spec_im * kern_re).astype(jnp.bfloat16)
+        block = jnp.concatenate(
+            [jnp.concatenate([re16, im16], 1), jnp.concatenate([-im16, re16], 1)], 0
+        )
+        row_field = jnp.dot(row_table, block, preferred_element_type=jnp.float32) / W
+        fields[f * MXU_ROWS : (f + 1) * MXU_ROWS, :] = row_field.astype(jnp.bfloat16)
+
+    for ref, which in ((send_ref, 1 - core), (keep_ref, core)):
+        for p in range(HALF // 256):
+            at = pl.ds(pl.multiple_of(which * HALF + p * 256, 256), 256)
+            rows = fields[...]
+            real = jnp.dot(rows, table_re[:, at], preferred_element_type=jnp.float32)
+            imag = jnp.dot(rows, table_im[:, at], preferred_element_type=jnp.float32)
+            total = jnp.zeros((RING_ROWS, 256), jnp.float32)
+            for f in range(count):
+                re = real[f * MXU_ROWS : f * MXU_ROWS + RING_ROWS]
+                im = imag[f * MXU_ROWS : f * MXU_ROWS + RING_ROWS]
+                total = total + eigen[f] * (re * re + im * im)
+            ref[:, p * 256 : (p + 1) * 256] = total
+
+
+def dirichlet():
+    distance = np.mod(np.arange(N)[None, :] - SPARSE * np.arange(32)[:, None], N)
+    turn = np.pi * distance / N
+    sine = np.where(distance == 0, 1.0, COARSE * np.sin(turn))
+    kernel = np.where(distance % SPARSE == 0, distance == 0, np.sin(COARSE * turn) * np.cos(turn) / sine)
+    kernel = kernel.astype(np.float32)
+    high = kernel.astype(ml_dtypes.bfloat16)
+    low = (kernel - high.astype(np.float32)).astype(ml_dtypes.bfloat16)
+    return high, low
 
 
 def laplace(field):
@@ -195,9 +184,37 @@
     )
 
 
-def bake_kernel(keep_ref, got_ref, rates, image_ref, acid_ref):
+def bake_kernel(own_ref, other_ref, high_ref, low_ref, rates, image_ref, acid_ref, parts, ring):
+    kern = lax.axis_index("kern")
+    core = lax.rem(kern, CORES)
+    for ref, which in ((own_ref, core), (other_ref, 1 - core)):
+        for p in range(HALF // 256):
+            block = jnp.bitwise_and(which * (HALF // 256) + p - kern, COARSE // 256 - 1)
+            at = pl.ds(pl.multiple_of(block * 256, 256), 256)
+            high, low = split(ref[:, p * 256 : (p + 1) * 256])
+            parts[0:RING_ROWS, at] = high
+            parts[MXU_ROWS : MXU_ROWS + RING_ROWS, at] = low
+
+    def weights(ref, tiles):
+        rows = [
+            jnp.concatenate([ref[:, ((t - m) % 32) * 128 : ((t - m) % 32) * 128 + 128] for t in tiles], 1)
+            for m in range(COARSE // 32)
+        ]
+        return jnp.concatenate(rows, 0)
+
+    for p in range(5):
+        tiles = (2 * p, 2 * p + 1) if p < 4 else (8, 31)
+        wide = jnp.dot(parts[...], weights(high_ref, tiles), preferred_element_type=jnp.float32)
+        fine = jnp.dot(parts[0:MXU_ROWS, :], weights(low_ref, tiles), preferred_element_type=jnp.float32)
+        value = wide[0:RING_ROWS] + (wide[MXU_ROWS : MXU_ROWS + RING_ROWS] + fine[0:RING_ROWS])
+        if p < 4:
+            ring[:, p * 256 : (p + 1) * 256] = value
+        else:
+            side = iota((RING_ROWS, 128), 1) < 64
+            ring[:, COLS:RING_COLS] = jnp.where(side, value[:, 0:128], value[:, 128:256])
+
     dill_rate, acid_rate, quench_rate, react_rate, quench_start = (rates[i] for i in range(5))
-    aerial_image = (keep_ref[...] + got_ref[...]) / FIELDS
+    aerial_image = ring[...] / FIELDS
     image_ref[...] = aerial_image[0:ROWS, 0:COLS]
     acid_field = 1.0 - jnp.exp((-4.0 * dill_rate) * aerial_image)
     acid_diffusion = acid_rate * (0.5 + 0.5 * acid_field)
@@ -235,45 +252,51 @@
 
 def shards(layout, band_freqs, kernels, eigen_values, bake_rates):
     freqs = band_freqs.reshape(1, W)
-    freqs_col = band_freqs.reshape(W, 1)
     f32 = jnp.float32
-    across_z = [(i, (i + 128) % 256) for i in range(256)]
-    far_kernels = lax.ppermute(kernels, ALL, across_z)
-    far_eigen = lax.ppermute(eigen_values, ALL, across_z)
+    params = pltpu.CompilerParams(vmem_limit_bytes=24 * 2**20)
     part = pl.pallas_call(
         transform_kernel,
         out_shape=jax.ShapeDtypeStruct((2 * W, W), f32),
         in_specs=[VMEM, VMEM],
         out_specs=VMEM,
         scratch_shapes=[pltpu.VMEM((COLS, 4 * W), jnp.bfloat16)],
+        compiler_params=params,
         name="transform",
     )(layout, freqs)
     spectrum = sum_everywhere(part)
-    half = jax.ShapeDtypeStruct((RING_ROWS, RING_COLS), f32)
-    own = kernels.shape[1]
+    half = jax.ShapeDtypeStruct((RING_ROWS, HALF), f32)
     send, keep = pl.pallas_call(
         image_kernel,
         out_shape=(half, half),
-        in_specs=[VMEM, VMEM, VMEM, SMEM, SMEM, VMEM, VMEM],
+        in_specs=[VMEM, VMEM, SMEM, VMEM],
         out_specs=(VMEM, VMEM),
         scratch_shapes=[
-            pltpu.VMEM((2 * W, WIDE), jnp.bfloat16),
-            pltpu.VMEM((2 * W, WIDE), jnp.bfloat16),
-            pltpu.VMEM((2 * own * MXU_ROWS, 2 * W), jnp.bfloat16),
-            pltpu.VMEM((RING_ROWS, WIDE), f32),
+            pltpu.VMEM((2 * W, COARSE), jnp.bfloat16),
+            pltpu.VMEM((2 * W, COARSE), jnp.bfloat16),
+            pltpu.VMEM((kernels.shape[1] * MXU_ROWS, 2 * W), jnp.bfloat16),
         ],
+        compiler_params=params,
         name="image",
-    )(spectrum, kernels, far_kernels, eigen_values, far_eigen, freqs, freqs_col)
+    )(spectrum, kernels, eigen_values, freqs)
+    across_z = [(i, (i + 128) % 256) for i in range(256)]
     across_cores = [(i, i + 64 if (i // 64) % 2 == 0 else i - 64) for i in range(256)]
-    got = lax.ppermute(send, ALL, across_cores)
+    chip = keep + lax.ppermute(send, ALL, across_cores)
+    own = chip + lax.ppermute(chip, ALL, across_z)
+    other = lax.ppermute(own, ALL, across_cores)
     block = jax.ShapeDtypeStruct((ROWS, COLS), f32)
+    high, low = dirichlet()
     return pl.pallas_call(
         bake_kernel,
         out_shape=(block, block),
-        in_specs=[VMEM, VMEM, SMEM],
+        in_specs=[VMEM, VMEM, VMEM, VMEM, SMEM],
         out_specs=(VMEM, VMEM),
+        scratch_shapes=[
+            pltpu.VMEM((2 * MXU_ROWS, COARSE), jnp.bfloat16),
+            pltpu.VMEM((RING_ROWS, RING_COLS), f32),
+        ],
+        compiler_params=params,
         name="bake",
-    )(keep, got, bake_rates)
+    )(own, other, jnp.asarray(high), jnp.asarray(low), bake_rates)
 
 
 def solution(mesh):

time: 93.6 us -> 62.7 us (0.67)
  Pallas kernels: 16.9 us -> 5.8 us
  blocking collectives: 55 us -> 45.2 us
  starting transfers between devices: 8.69 us -> 1.84 us
  local copies, waits for them, and re-layouts: 3.36 us -> 1.76 us
  waiting for transfers between devices: 8.6 us -> 7.05 us
    all_to_all x2 -> x3, blocking collectives: 55 us -> 45.2 us  [exchange(): lax.all_to_all(blocks, ALL, 0, 0, tiled=True, axis_index_groups=groups)]
    pallas_call x1, Pallas kernels: 12.2 us -> 2.52 us  [shards(): pl.pallas_call(image_kernel, out_shape=(half, half), in_specs=[VMEM, VMEM...]
    all_to_all x1 -> x0, waiting for transfers between devices: 5.3 us -> none  [exchange(): lax.all_to_all(blocks, ALL, 0, 0, tiled=True, axis_index_groups=groups)]
    all_to_all x1 -> x0, starting transfers between devices: 4.71 us -> none  [exchange(): lax.all_to_all(blocks, ALL, 0, 0, tiled=True, axis_index_groups=groups)]
    ppermute x3, waiting for transfers between devices: 3.29 us -> 7.05 us  [the longest x1 4.69 us: shards(): own = chip + lax.ppermute(chip, ALL, across_z)]
    ppermute x3, starting transfers between devices: 3.99 us -> 1.84 us  [the longest x1 1.09 us: shards(): other = lax.ppermute(own, ALL, across_cores)]
    pallas_call x1, Pallas kernels: 2.43 us -> 0.81 us  [shards(): pl.pallas_call(transform_kernel, out_shape=jax.ShapeDtypeStruct((2 * W, W...]
    unnamed x12 -> x16, local copies, waits for them, and re-layouts: 1.94 us -> 1.74 us
  transfers between devices with their start and end apart: 4 -> 3, of which waited for: 3 -> 3; matrix products, arithmetic and copies ran while one was open for 2% -> 0% of each run, Pallas kernels for 3% -> 0%
where the time goes in v2:
time: 62.7 us; the launch traced here: 62.5 us
  blocking collectives  45.2 us (72%)
  waiting for transfers between devices  7.05 us (11%)
  Pallas kernels  5.8 us (9%)
  starting transfers between devices  1.84 us (3%)
  local copies, waits for them, and re-layouts  1.76 us (3%)
  between operations  0.71 us (1%)
    all_to_all x3, blocking collectives, exchange(): lax.all_to_all(blocks, ALL, 0, 0, tiled=True, axis_index_groups=groups)  45.2 us
    ppermute x1, waiting for transfers between devices, shards(): own = chip + lax.ppermute(chip, ALL, across_z)  4.69 us
    pallas_call x1, Pallas kernels, shards(): pl.pallas_call(image_kernel, out_shape=(half, half), in_specs=[VMEM, VMEM...  2.52 us
    pallas_call x1, Pallas kernels, shards(): pl.pallas_call(bake_kernel, out_shape=(block, block), in_specs=[VMEM, VME...  2.46 us
    unnamed x16, local copies, waits for them, and re-layouts  1.74 us
    ppermute x1, waiting for transfers between devices, shards(): chip = keep + lax.ppermute(send, ALL, across_cores)  1.36 us
  transfers between devices with their start and end apart: 3, of which 3 were waited for; matrix products, arithmetic and copies ran while one was open for 0% of the time, Pallas kernels for 0%

profile of v2, /device:TPU:1, one launch (start us, length us, event | category | flops | bytes accessed | tf_op | source)
XLA Modules:
  0.0 62.5 jit_solution(2031146521757857159)
XLA Ops:
  0.6 0.0 copy-start
  0.6 0.0 copy-start.1
  0.7 1.1 %copy-done.1 = s32[64,1024]{1,0:T(8,128)S(1)} copy-done((s32[64,1024]{1,0:T(8,128)S(1)}, s32[64,1024]{1,0:T(8,128)}, u32[]{:S(2)}) %copy-start.1) | copy-done | bytes 262168
  1.7 0.0 copy-start.4
  1.7 0.7 %copy-done.4 = s32[128]{0:T(128)S(1)} copy-done((s32[128]{0:T(128)S(1)}, s32[128]{0:T(128)}, u32[]{:S(2)}) %copy-start.4) | copy-done | bytes 536
  2.4 0.0 copy-start.5
  2.4 0.0 copy-start.6
  2.4 0.8 %transform.1 = f32[256,128]{1,0:T(8,128)S(1)} custom-call(s32[64,1024]{1,0:T(8,128)S(1)} %copy-done.1, s32[1,128]{1,0:T(1,128)S(1)} %bitcast.5), custom_call_target="tpu_custom_call" | custom-call | tf_op jit(solution)/shard_map/transform/pallas_call | solution.py:257
  3.2 18.7 %all_to_all.23 = f32[16,16,128]{2,1,0:T(8,128)S(1)} all-to-all(f32[16,16,128]{2,1,0:T(8,128)S(1)} %bitcast.4), channel_id=1, replica_groups={{0,16,32,48,64,80,96,112,128,144,160,176,192,208,224,240},{1,17,33,49,6..., dimensions={0} | all-to-all | bytes 262144 | tf_op jit(solution)/shard_map/all_to_all | solution.py:240
  21.9 13.9 %all_to_all.24 = f32[16,16,128]{2,1,0:T(8,128)S(1)} all-to-all(f32[16,16,128]{2,1,0:T(8,128)S(1)} %broadcast_in_dim.4), channel_id=1, replica_groups={{0,1,2,3,4,5,6,7,8,9,10,11,12,13,14,15},{16,17,18,19,20,21,22,23,24,25,..., dimensions={0} | all-to-all | bytes 262144 | tf_op jit(solution)/shard_map/all_to_all | solution.py:240
  35.8 0.0 copy-start.2
  35.8 0.0 copy-start.3
  35.9 0.0 copy-start.7
  35.9 12.6 %all_to_all.25 = f32[16,16,128]{2,1,0:T(8,128)S(1)} all-to-all(f32[16,16,128]{2,1,0:T(8,128)S(1)} %broadcast_in_dim.5), channel_id=1, replica_groups={{0,16,32,48,64,80,96,112,128,144,160,176,192,208,224,240},{1,17,33,49,6..., dimensions={0} | all-to-all | bytes 262144 | tf_op jit(solution)/shard_map/all_to_all | solution.py:240
  48.5 0.0 copy-done
  48.5 0.0 copy-done.5
  48.5 0.0 copy-done.6
  48.5 2.5 %image.1 = (f32[72,512]{1,0:T(8,128)S(1)}, f32[72,512]{1,0:T(8,128)S(1)}) custom-call(f32[256,128]{1,0:T(8,128)S(1)} %bitcast.3, f32[2,12,128,128]{3,2,1,0:T(8,128)S(1)} %copy-done, f32[12]{0:T(128)S(1)} %copy-done.6, s32[1,128]{1,0:T(1,128)S(1)} %bitcast.6), custom_call_target="tpu_custom_call" | custom-call | tf_op jit(solution)/shard_map/image/pallas_call | solution.py:268
  51.0 0.1 collective-permute-start
  51.1 1.4 %collective-permute-done = f32[72,512]{1,0:T(8,128)S(1)} collective-permute-done((f32[72,512]{1,0:T(8,128)S(1)}, f32[72,512]{1,0:T(8,128)S(1)}, u32[]{:S(2)}, u32[]{:S(2)}) %collective-permute-start) | collective-permute-done | bytes 147488 | tf_op jit(solution)/shard_map/ppermute | solution.py:283
  52.5 0.7 %collective-permute-start.1 = (f32[72,512]{1,0:T(8,128)S(1)}, f32[72,512]{1,0:T(8,128)S(1)}, u32[]{:S(2)}, u32[]{:S(2)}) collective-permute-start(f32[72,512]{1,0:T(8,128)S(1)} %add.6), channel_id=1, source_target_pairs={{0,128},{1,129},{2,130},{3,131},{4,132},{5,133},{6,134},{7,135},{8... | collective-permute-start | bytes 442376 | tf_op jit(solution)/shard_map/ppermute | solution.py:284
  53.2 4.7 %collective-permute-done.1 = f32[72,512]{1,0:T(8,128)S(1)} collective-permute-done((f32[72,512]{1,0:T(8,128)S(1)}, f32[72,512]{1,0:T(8,128)S(1)}, u32[]{:S(2)}, u32[]{:S(2)}) %collective-permute-start.1) | collective-permute-done | bytes 147488 | tf_op jit(solution)/shard_map/ppermute | solution.py:284
  57.9 1.1 %collective-permute-start.2 = (f32[72,512]{1,0:T(8,128)S(1)}, f32[72,512]{1,0:T(8,128)S(1)}, u32[]{:S(2)}, u32[]{:S(2)}) collective-permute-start(f32[72,512]{1,0:T(8,128)S(1)} %add.7.own_ref), channel_id=1, source_target_pairs={{0,64},{1,65},{2,66},{3,67},{4,68},{5,69},{6,70},{7,71},{8,72},{9,... | collective-permute-start | bytes 442376 | tf_op jit(solution)/shard_map/ppermute | solution.py:285
  59.0 1.0 %collective-permute-done.2.other_ref = f32[72,512]{1,0:T(8,128)S(1)} collective-permute-done((f32[72,512]{1,0:T(8,128)S(1)}, f32[72,512]{1,0:T(8,128)S(1)}, u32[]{:S(2)}, u32[]{:S(2)}) %collective-permute-start.2) | collective-permute-done | bytes 147488 | tf_op jit(solution)/shard_map/ppermute | solution.py:285
  60.0 0.0 copy-done.2
  60.0 0.0 copy-done.3
  60.0 0.0 copy-done.7
  60.0 2.5 %bake.1 = (f32[64,1024]{1,0:T(8,128)}, f32[64,1024]{1,0:T(8,128)}) custom-call(f32[72,512]{1,0:T(8,128)S(1)} %add.7.own_ref, f32[72,512]{1,0:T(8,128)S(1)} %collective-permute-done.2.other_ref, bf16[32,4096]{1,0:T(8,128)(2,1)S(1)} %copy-done.3, bf16[32,4096]{1,0:T(8,128)(2,1)S(1)} %copy-done.2, f32[5]{0:T(128)S(1)} %copy-done.7), custom_call_target="tpu_custom_call" | custom-call | tf_op jit(solution)/shard_map/bake/pallas_call | solution.py:288
  (6 shorter events, 0.1 us)
Async XLA Ops:
  0.6 47.9 %copy-start = (f32[2,12,128,128]{3,2,1,0:T(8,128)S(1)}, f32[2,12,128,128]{3,2,1,0:T(8,128)}, u32[]{:S(2)}) copy-start(f32[2,12,128,128]{3,2,1,0:T(8,128)} %kernels_ref.1) | copy-start | bytes 4718596
  0.6 1.1 %copy-start.1 = (s32[64,1024]{1,0:T(8,128)S(1)}, s32[64,1024]{1,0:T(8,128)}, u32[]{:S(2)}) copy-start(s32[64,1024]{1,0:T(8,128)} %layout_ref.1) | copy-start | bytes 786436
  1.7 0.7 %copy-start.4 = (s32[128]{0:T(128)S(1)}, s32[128]{0:T(128)}, u32[]{:S(2)}) copy-start(s32[128]{0:T(128)} %param.8) | copy-start | bytes 1540
  2.4 46.1 %copy-start.5 = (s32[128]{0:T(128)S(1)}, s32[128]{0:T(128)}, u32[]{:S(2)}) copy-start(s32[128]{0:T(128)} %param.8) | copy-start | bytes 1540
  2.4 46.1 %copy-start.6 = (f32[12]{0:T(128)S(1)}, f32[12]{0:T(128)}, u32[]{:S(2)}) copy-start(f32[12]{0:T(128)} %eigen.1) | copy-start | bytes 148
  35.8 24.1 %copy-start.2 = (bf16[32,4096]{1,0:T(8,128)(2,1)S(1)}, bf16[32,4096]{1,0:T(8,128)(2,1)}, u32[]{:S(2)}) copy-start(bf16[32,4096]{1,0:T(8,128)(2,1)} %constant.7.clone.low_ref) | copy-start | bytes 786436
  35.8 24.1 %copy-start.3 = (bf16[32,4096]{1,0:T(8,128)(2,1)S(1)}, bf16[32,4096]{1,0:T(8,128)(2,1)}, u32[]{:S(2)}) copy-start(bf16[32,4096]{1,0:T(8,128)(2,1)} %constant.6.clone.high_ref) | copy-start | bytes 786436
  35.9 24.1 %copy-start.7 = (f32[5]{0:T(128)S(1)}, f32[5]{0:T(128)}, u32[]{:S(2)}) copy-start(f32[5]{0:T(128)} %rates.1) | copy-start | bytes 64
  51.0 1.5 %collective-permute-start = (f32[72,512]{1,0:T(8,128)S(1)}, f32[72,512]{1,0:T(8,128)S(1)}, u32[]{:S(2)}, u32[]{:S(2)}) collective-permute-start(f32[72,512]{1,0:T(8,128)S(1)} %get-tuple-element.5), channel_id=1, source_target_pairs={{0,64},{1,65},{2,66},{3,67},{4,68},{5,69},{6,70},{7,71},{8,72},{9,... | collective-permute-start | bytes 442376 | tf_op jit(solution)/shard_map/ppermute | solution.py:283
  52.5 5.3 %collective-permute-start.1 = (f32[72,512]{1,0:T(8,128)S(1)}, f32[72,512]{1,0:T(8,128)S(1)}, u32[]{:S(2)}, u32[]{:S(2)}) collective-permute-start(f32[72,512]{1,0:T(8,128)S(1)} %add.6), channel_id=1, source_target_pairs={{0,128},{1,129},{2,130},{3,131},{4,132},{5,133},{6,134},{7,135},{8... | collective-permute-start | bytes 442376 | tf_op jit(solution)/shard_map/ppermute | solution.py:284
  57.9 2.1 %collective-permute-start.2 = (f32[72,512]{1,0:T(8,128)S(1)}, f32[72,512]{1,0:T(8,128)S(1)}, u32[]{:S(2)}, u32[]{:S(2)}) collective-permute-start(f32[72,512]{1,0:T(8,128)S(1)} %add.7.own_ref), channel_id=1, source_target_pairs={{0,64},{1,65},{2,66},{3,67},{4,68},{5,69},{6,70},{7,71},{8,72},{9,... | collective-permute-start | bytes 442376 | tf_op jit(solution)/shard_map/ppermute | solution.py:285

commit v3 on v2

--- a/solution.py
+++ b/solution.py
@@ -21,7 +21,6 @@
 RING_COLS = 1152
 SPARSE = 4
 COARSE = N // SPARSE
-HALF = COARSE // 2
 ALL = ("kern", "slab")
 CHIP_Z, CORES, FAR_Z, SIDE = 2, 2, 4, 4
 
@@ -30,21 +29,33 @@
     return (z_lo * CORES + core) * 64 + (z_hi * SIDE + y) * SIDE + x
 
 
-def column_groups():
-    return [
-        [device(a, b, c, y, x) for a in range(CHIP_Z) for b in range(CORES) for c in range(FAR_Z)]
-        for y in range(SIDE)
-        for x in range(SIDE)
-    ]
+def place(i):
+    kern, slab = divmod(i, 64)
+    return kern // CORES, kern % CORES, slab // SIDE**2, slab // SIDE % SIDE, slab % SIDE
+
+
+def groups_along(kept):
+    groups = {}
+    for i in range(256):
+        groups.setdefault(tuple(place(i)[axis] for axis in kept), []).append(i)
+    return list(groups.values())
 
 
 def plane_groups():
-    return [
-        [device(a, b, c, y, x) for y in range(SIDE) for x in range(SIDE)]
-        for a in range(CHIP_Z)
-        for b in range(CORES)
-        for c in range(FAR_Z)
-    ]
+    return groups_along((0, 2))
+
+
+def z_groups():
+    return groups_along((1, 3, 4))
+
+
+def from_next_z():
+    pairs = []
+    for i in range(256):
+        z_lo, core, z_hi, y, x = place(i)
+        z = (z_hi * CHIP_Z + z_lo + (1 if z_lo == core else -1)) % (FAR_Z * CHIP_Z)
+        pairs.append((device(z % CHIP_Z, core, z // CHIP_Z, y, x), i))
+    return pairs
 
 
 def cos_sin(turns):
@@ -71,9 +82,37 @@
     return lax.broadcasted_iota(jnp.int32, shape, dim)
 
 
-def transform_kernel(layout_ref, freqs_ref, out_ref, table):
+def image_tables(freqs, row_first, re_ref, im_ref, row_ref):
+    row = iota((MXU_ROWS, W), 0)
+    row = jnp.where(row < ROWS + 4, row, row - RING_ROWS)
+    cos_row, sin_row = cos_sin((row_first + row) * freqs)
+    row_ref[:, 0:W] = cos_row.astype(jnp.bfloat16)
+    row_ref[:, W : 2 * W] = sin_row.astype(jnp.bfloat16)
+
+    freqs_col = jnp.broadcast_to(freqs, (W, W)).astype(jnp.float32).T.astype(jnp.int32)
+    cos, sin = cos_sin((SPARSE * iota((W, 128), 1)) * freqs_col)
+    turn_cos, turn_sin = cos_sin((SPARSE * 128) * freqs_col)
+    for tile in range(COARSE // 128):
+        at = slice(tile * 128, tile * 128 + 128)
+        re_ref[0:W, at] = cos.astype(jnp.bfloat16)
+        re_ref[W : 2 * W, at] = (-sin).astype(jnp.bfloat16)
+        im_ref[0:W, at] = sin.astype(jnp.bfloat16)
+        im_ref[W : 2 * W, at] = cos.astype(jnp.bfloat16)
+        cos, sin = cos * turn_cos - sin * turn_sin, sin * turn_cos + cos * turn_sin
+
+
+def transform_kernel(
+    layout_hbm, freqs_hbm, eigen_hbm, out_ref, re_ref, im_ref, row_ref, eigen_ref, table, layout_ref, freqs_ref, sems
+):
+    freqs_copy = pltpu.make_async_copy(freqs_hbm, freqs_ref, sems.at[0])
+    layout_copy = pltpu.make_async_copy(layout_hbm, layout_ref, sems.at[1])
+    eigen_copy = pltpu.make_async_copy(eigen_hbm, eigen_ref, sems.at[2])
+    freqs_copy.start()
+    layout_copy.start()
+    eigen_copy.start()
     row_first = lax.axis_index("slab") * ROWS
     col_first = lax.axis_index("kern") * COLS
+    freqs_copy.wait()
     freqs = freqs_ref[...]
     step = 32
     base_cos, base_sin = cos_sin((col_first + iota((step, W), 0)) * freqs)
@@ -89,12 +128,15 @@
         table[at, W : 2 * W] = sin_high
         table[at, 2 * W : 3 * W] = cos_low
         table[at, 3 * W : 4 * W] = sin_low
+    cos_row, sin_row = cos_sin((row_first + iota((ROWS, W), 0)) * freqs)
+    left_high, left_low = split(jnp.concatenate([cos_row, sin_row], 0))
+    image_tables(freqs, row_first, re_ref, im_ref, row_ref)
+    layout_copy.wait()
+    eigen_copy.wait()
     transmit = (2 * layout_ref[...] - 1).astype(jnp.float32).astype(jnp.bfloat16)
     along = jnp.dot(transmit, table[...], preferred_element_type=jnp.float32)
     along_re = along[:, 0:W] + along[:, 2 * W : 3 * W]
     along_im = -(along[:, W : 2 * W] + along[:, 3 * W : 4 * W])
-    cos_row, sin_row = cos_sin((row_first + iota((ROWS, W), 0)) * freqs)
-    left_high, left_low = split(jnp.concatenate([cos_row, sin_row], 0))
     right = jnp.concatenate(
         [
             jnp.concatenate([along_re, along_im], 1),
@@ -113,31 +155,17 @@
     out_ref[W : 2 * W, :] = both[:, W : 2 * W]
 
 
-def image_kernel(spec_ref, kernels_ref, eigen, freqs_ref, send_ref, keep_ref, table_re, table_im, fields):
-    row_first = lax.axis_index("slab") * ROWS
-    core = lax.rem(lax.axis_index("kern"), CORES)
-    freqs = freqs_ref[...]
-
-    freqs_col = jnp.broadcast_to(freqs, (W, W)).astype(jnp.float32).T.astype(jnp.int32)
-    cos, sin = cos_sin((SPARSE * iota((W, 128), 1)) * freqs_col)
-    turn_cos, turn_sin = cos_sin((SPARSE * 128) * freqs_col)
-    for tile in range(COARSE // 128):
-        at = pl.ds(tile * 128, 128)
-        table_re[0:W, at] = cos.astype(jnp.bfloat16)
-        table_re[W : 2 * W, at] = (-sin).astype(jnp.bfloat16)
-        table_im[0:W, at] = sin.astype(jnp.bfloat16)
-        table_im[W : 2 * W, at] = cos.astype(jnp.bfloat16)
-        cos, sin = cos * turn_cos - sin * turn_sin, sin * turn_cos + cos * turn_sin
-
-    place = iota((MXU_ROWS, W), 0)
-    place = jnp.where(place < ROWS + 4, place, place - RING_ROWS)
-    cos_row, sin_row = cos_sin((row_first + place) * freqs)
-    row_table = jnp.concatenate([cos_row, sin_row], 1).astype(jnp.bfloat16)
-
+def image_kernel(
+    spec_ref, near_hbm, far_ref, table_re, table_im, row_ref, near_eigen, far_eigen, image_ref, fields, near_ref, sem
+):
+    near_copy = pltpu.make_async_copy(near_hbm, near_ref, sem)
+    near_copy.start()
+    row_table = row_ref[...]
     spec_re = spec_ref[0:W, :]
     spec_im = spec_ref[W : 2 * W, :]
-    count = kernels_ref.shape[1]
-    for f in range(count):
+    own = far_ref.shape[1]
+
+    def row_field(kernels_ref, f):
         kern_re = kernels_ref[0, f]
         kern_im = kernels_ref[1, f]
         re16 = (spec_re * kern_re - spec_im * kern_im).astype(jnp.bfloat16)
@@ -145,21 +173,28 @@
         block = jnp.concatenate(
             [jnp.concatenate([re16, im16], 1), jnp.concatenate([-im16, re16], 1)], 0
         )
-        row_field = jnp.dot(row_table, block, preferred_element_type=jnp.float32) / W
-        fields[f * MXU_ROWS : (f + 1) * MXU_ROWS, :] = row_field.astype(jnp.bfloat16)
-
-    for ref, which in ((send_ref, 1 - core), (keep_ref, core)):
-        for p in range(HALF // 256):
-            at = pl.ds(pl.multiple_of(which * HALF + p * 256, 256), 256)
-            rows = fields[...]
-            real = jnp.dot(rows, table_re[:, at], preferred_element_type=jnp.float32)
-            imag = jnp.dot(rows, table_im[:, at], preferred_element_type=jnp.float32)
-            total = jnp.zeros((RING_ROWS, 256), jnp.float32)
-            for f in range(count):
-                re = real[f * MXU_ROWS : f * MXU_ROWS + RING_ROWS]
-                im = imag[f * MXU_ROWS : f * MXU_ROWS + RING_ROWS]
-                total = total + eigen[f] * (re * re + im * im)
-            ref[:, p * 256 : (p + 1) * 256] = total
+        return jnp.dot(row_table, block, preferred_element_type=jnp.float32)[0:RING_ROWS] / W
+
+    for kernels_ref, first in ((far_ref, 0), (near_ref, own)):
+        if first:
+            near_copy.wait()
+        for f in range(0, own, 2):
+            both = jnp.concatenate([row_field(kernels_ref, f), row_field(kernels_ref, f + 1)], 0)
+            at = (first + f) * RING_ROWS
+            fields[at : at + 2 * RING_ROWS, :] = both.astype(jnp.bfloat16)
+
+    eigen = [ref[0:1, f : f + 1] for ref in (far_eigen, near_eigen) for f in range(own)]
+    for p in range(COARSE // 256):
+        at = slice(p * 256, (p + 1) * 256)
+        rows = fields[...]
+        real = jnp.dot(rows, table_re[:, at], preferred_element_type=jnp.float32)
+        imag = jnp.dot(rows, table_im[:, at], preferred_element_type=jnp.float32)
+        total = jnp.zeros((RING_ROWS, 256), jnp.float32)
+        for f in range(2 * own):
+            re = real[f * RING_ROWS : (f + 1) * RING_ROWS]
+            im = imag[f * RING_ROWS : (f + 1) * RING_ROWS]
+            total = total + eigen[f] * (re * re + im * im)
+        image_ref[:, at] = total
 
 
 def dirichlet():
@@ -186,14 +221,12 @@
 
 def bake_kernel(own_ref, other_ref, high_ref, low_ref, rates, image_ref, acid_ref, parts, ring):
     kern = lax.axis_index("kern")
-    core = lax.rem(kern, CORES)
-    for ref, which in ((own_ref, core), (other_ref, 1 - core)):
-        for p in range(HALF // 256):
-            block = jnp.bitwise_and(which * (HALF // 256) + p - kern, COARSE // 256 - 1)
-            at = pl.ds(pl.multiple_of(block * 256, 256), 256)
-            high, low = split(ref[:, p * 256 : (p + 1) * 256])
-            parts[0:RING_ROWS, at] = high
-            parts[MXU_ROWS : MXU_ROWS + RING_ROWS, at] = low
+    for p in range(COARSE // 256):
+        block = jnp.bitwise_and(p - kern, COARSE // 256 - 1)
+        at = pl.ds(pl.multiple_of(block * 256, 256), 256)
+        high, low = split(own_ref[:, p * 256 : (p + 1) * 256] + other_ref[:, p * 256 : (p + 1) * 256])
+        parts[0:RING_ROWS, at] = high
+        parts[MXU_ROWS : MXU_ROWS + RING_ROWS, at] = low
 
     def weights(ref, tiles):
         rows = [
@@ -229,11 +262,16 @@
 
 VMEM = pl.BlockSpec(memory_space=pltpu.VMEM)
 SMEM = pl.BlockSpec(memory_space=pltpu.SMEM)
+HBM = pl.BlockSpec(memory_space=pltpu.HBM)
+
+
+def in_hbm(array):
+    return pltpu.with_memory_space_constraint(array, pltpu.HBM)
 
 
 def sum_everywhere(part):
-    ring, plane = column_groups(), plane_groups()
-    count = len(ring[0])
+    plane, along_z = plane_groups(), z_groups()
+    count = len(plane[0])
     piece = part.shape[0] // count
 
     def exchange(blocks, groups):
@@ -245,44 +283,56 @@
     def copies(block, many):
         return jnp.broadcast_to(block[None], (many,) + block.shape).reshape(-1, block.shape[1])
 
-    some = total(exchange(part, ring))
-    full = total(exchange(copies(some, len(plane[0])), plane))
-    return exchange(copies(full, count), ring)
+    some = total(exchange(part, plane))
+    full = total(exchange(copies(some, len(along_z[0])), along_z))
+    return exchange(copies(full, count), plane)
 
 
 def shards(layout, band_freqs, kernels, eigen_values, bake_rates):
     freqs = band_freqs.reshape(1, W)
     f32 = jnp.float32
     params = pltpu.CompilerParams(vmem_limit_bytes=24 * 2**20)
-    part = pl.pallas_call(
+    far_kernels = lax.ppermute(kernels, ALL, from_next_z())
+    far_eigen = lax.ppermute(eigen_values, ALL, from_next_z())
+    own = kernels.shape[1]
+    table = jax.ShapeDtypeStruct((2 * W, COARSE), jnp.bfloat16)
+    part, *tables, near_eigen = pl.pallas_call(
         transform_kernel,
-        out_shape=jax.ShapeDtypeStruct((2 * W, W), f32),
-        in_specs=[VMEM, VMEM],
-        out_specs=VMEM,
-        scratch_shapes=[pltpu.VMEM((COLS, 4 * W), jnp.bfloat16)],
+        out_shape=(
+            jax.ShapeDtypeStruct((2 * W, W), f32),
+            table,
+            table,
+            jax.ShapeDtypeStruct((MXU_ROWS, 2 * W), jnp.bfloat16),
+            jax.ShapeDtypeStruct((1, own), f32),
+        ),
+        in_specs=[HBM, HBM, HBM],
+        out_specs=(VMEM,) * 5,
+        scratch_shapes=[
+            pltpu.VMEM((COLS, 4 * W), jnp.bfloat16),
+            pltpu.VMEM((ROWS, COLS), jnp.int32),
+            pltpu.VMEM((1, W), jnp.int32),
+            pltpu.SemaphoreType.DMA((3,)),
+        ],
         compiler_params=params,
         name="transform",
-    )(layout, freqs)
+    )(in_hbm(layout), in_hbm(freqs), in_hbm(eigen_values.reshape(1, own)))
+    part, far_eigen = lax.optimization_barrier((part, far_eigen))
     spectrum = sum_everywhere(part)
-    half = jax.ShapeDtypeStruct((RING_ROWS, HALF), f32)
-    send, keep = pl.pallas_call(
+    own_image = pl.pallas_call(
         image_kernel,
-        out_shape=(half, half),
-        in_specs=[VMEM, VMEM, SMEM, VMEM],
-        out_specs=(VMEM, VMEM),
+        out_shape=jax.ShapeDtypeStruct((RING_ROWS, COARSE), f32),
+        in_specs=[VMEM, HBM] + [VMEM] * 6,
+        out_specs=VMEM,
         scratch_shapes=[
-            pltpu.VMEM((2 * W, COARSE), jnp.bfloat16),
-            pltpu.VMEM((2 * W, COARSE), jnp.bfloat16),
-            pltpu.VMEM((kernels.shape[1] * MXU_ROWS, 2 * W), jnp.bfloat16),
+            pltpu.VMEM((2 * own * RING_ROWS, 2 * W), jnp.bfloat16),
+            pltpu.VMEM(kernels.shape, f32),
+            pltpu.SemaphoreType.DMA,
         ],
         compiler_params=params,
         name="image",
-    )(spectrum, kernels, eigen_values, freqs)
-    across_z = [(i, (i + 128) % 256) for i in range(256)]
+    )(spectrum, in_hbm(kernels), far_kernels, *tables, near_eigen, far_eigen.reshape(1, own))
     across_cores = [(i, i + 64 if (i // 64) % 2 == 0 else i - 64) for i in range(256)]
-    chip = keep + lax.ppermute(send, ALL, across_cores)
-    own = chip + lax.ppermute(chip, ALL, across_z)
-    other = lax.ppermute(own, ALL, across_cores)
+    other_image = lax.ppermute(own_image, ALL, across_cores)
     block = jax.ShapeDtypeStruct((ROWS, COLS), f32)
     high, low = dirichlet()
     return pl.pallas_call(
@@ -296,7 +346,7 @@
         ],
         compiler_params=params,
         name="bake",
-    )(own, other, jnp.asarray(high), jnp.asarray(low), bake_rates)
+    )(own_image, other_image, jnp.asarray(high), jnp.asarray(low), bake_rates)
 
 
 def solution(mesh):

time: 62.7 us -> 73.2 us (1.17)
  waiting for transfers between devices: 7.05 us -> 17.1 us
  blocking collectives: 45.2 us -> 39.3 us
  starting transfers between devices: 1.84 us -> 7.2 us
  Pallas kernels: 5.8 us -> 8.6 us
  local copies, waits for them, and re-layouts: 1.76 us -> 0.03 us
    ppermute x3, waiting for transfers between devices: 7.05 us -> 17.1 us  [the longest x1 15.9 us: shards(): far_eigen = lax.ppermute(eigen_values, ALL, from_next_z())]
    all_to_all x3, blocking collectives: 45.2 us -> 39.3 us  [exchange(): lax.all_to_all(blocks, ALL, 0, 0, tiled=True, axis_index_groups=groups)]
    ppermute x3, starting transfers between devices: 1.84 us -> 7.2 us  [the longest x1 6.48 us: shards(): far_kernels = lax.ppermute(kernels, ALL, from_next_z())]
    pallas_call x2, Pallas kernels: 3.34 us -> 6.12 us  [the longest x1 4 us: shards(): pl.pallas_call(image_kernel, out_shape=jax.ShapeDtypeStruct((RING_ROWS, C...]
    unnamed x16 -> x6, local copies, waits for them, and re-layouts: 1.74 us -> 0.01 us
  transfers between devices with their start and end apart: 3 -> 3, of which waited for: 3 -> 2; matrix products, arithmetic and copies ran while one was open for 0% -> 0% of each run, Pallas kernels for 0% -> 3%
where the time goes in v3:
time: 73.2 us; the launch traced here: 72.9 us
  blocking collectives  39.3 us (54%)
  waiting for transfers between devices  17.1 us (23%)
  Pallas kernels  8.6 us (12%)
  starting transfers between devices  7.2 us (10%)
    all_to_all x3, blocking collectives, exchange(): lax.all_to_all(blocks, ALL, 0, 0, tiled=True, axis_index_groups=groups)  39.3 us
    ppermute x1, waiting for transfers between devices, shards(): far_eigen = lax.ppermute(eigen_values, ALL, from_next_z())  15.9 us
    ppermute x1, starting transfers between devices, shards(): far_kernels = lax.ppermute(kernels, ALL, from_next_z())  6.48 us
    pallas_call x1, Pallas kernels, shards(): pl.pallas_call(image_kernel, out_shape=jax.ShapeDtypeStruct((RING_ROWS, C...  4 us
    pallas_call x1, Pallas kernels, shards(): pl.pallas_call(bake_kernel, out_shape=(block, block), in_specs=[VMEM, VME...  2.47 us
    pallas_call x1, Pallas kernels, shards(): pl.pallas_call(transform_kernel, out_shape=(jax.ShapeDtypeStruct((2 * W,...  2.12 us
  transfers between devices with their start and end apart: 3, of which 2 were waited for; matrix products, arithmetic and copies ran while one was open for 0% of the time, Pallas kernels for 3%

profile of v3, /device:TPU:1, one launch (start us, length us, event | category | flops | bytes accessed | tf_op | source)
XLA Modules:
  0.0 72.9 jit_solution(12087732061958033744)
XLA Ops:
  0.6 6.5 %collective-permute-start.1 = (f32[2,12,128,128]{3,2,1,0:T(8,128)}, f32[2,12,128,128]{3,2,1,0:T(8,128)S(1)}, u32[]{:S(2)}, u32[]{:S(2)}) collective-permute-start(f32[2,12,128,128]{3,2,1,0:T(8,128)} %near_hbm.1), channel_id=1, source_target_pairs={{128,0},{129,1},{130,2},{131,3},{132,4},{133,5},{134,6},{135,7},{1... | collective-permute-start | bytes 4718600 | tf_op jit(solution)/shard_map/ppermute | solution.py:295
  7.1 0.1 collective-permute-start
  7.2 2.1 %transform.1 = (f32[256,128]{1,0:T(8,128)S(1)}, bf16[256,1024]{1,0:T(8,128)(2,1)S(1)}, bf16[256,1024]{1,0:T(8,128)(2,1)S(1)}, bf16[80,256]{1,0:T(8,128)(2,1)S(1)}, f32[1,12]{1,0:T(1,128)S(1)}) custom-call(s32[64,1024]{1,0:T(8,128)} %layout_hbm.1, s32[1,128]{1,0:T(1,128)} %bitcast.8, f32[1,12]{1,0:T(1,128)} %bitcast.9), custom_call_target="tpu_custom_call" | custom-call | tf_op jit(solution)/shard_map/transform/pallas_call | solution.py:299
  9.3 15.9 %collective-permute-done = f32[12]{0:T(128)S(1)} collective-permute-done((f32[12]{0:T(128)}, f32[12]{0:T(128)S(1)}, u32[]{:S(2)}, u32[]{:S(2)}) %collective-permute-start) | collective-permute-done | bytes 80 | tf_op jit(solution)/shard_map/ppermute | solution.py:296
  25.2 14.5 %all_to_all.23 = f32[32,8,128]{2,1,0:T(8,128)S(1)} all-to-all(f32[32,8,128]{2,1,0:T(8,128)S(1)} %bitcast.6), channel_id=1, replica_groups={{0,1,2,3,4,5,6,7,8,9,10,11,12,13,14,15,64,65,66,67,68,69,70,71,72,73,74..., dimensions={0} | all-to-all | bytes 262144 | tf_op jit(solution)/shard_map/all_to_all | solution.py:278
  39.8 12.2 %all_to_all.24 = f32[8,8,128]{2,1,0:T(8,128)S(1)} all-to-all(f32[8,8,128]{2,1,0:T(8,128)S(1)} %broadcast_in_dim.4), channel_id=1, replica_groups={{0,16,32,48,128,144,160,176},{1,17,33,49,129,145,161,177},{2,18,34,50,1..., dimensions={0} | all-to-all | bytes 65536 | tf_op jit(solution)/shard_map/all_to_all | solution.py:278
  52.0 12.6 %all_to_all.25 = f32[32,8,128]{2,1,0:T(8,128)S(1)} all-to-all(f32[32,8,128]{2,1,0:T(8,128)S(1)} %broadcast_in_dim.5), channel_id=1, replica_groups={{0,1,2,3,4,5,6,7,8,9,10,11,12,13,14,15,64,65,66,67,68,69,70,71,72,73,74..., dimensions={0} | all-to-all | bytes 262144 | tf_op jit(solution)/shard_map/all_to_all | solution.py:278
  64.6 0.0 collective-permute-done.1.far_ref
  64.6 0.0 copy-start
  64.6 0.0 copy-start.1
  64.6 0.0 copy-start.2
  64.6 4.0 %image.1.own_ref = f32[72,1024]{1,0:T(8,128)S(1)} custom-call(f32[256,128]{1,0:T(8,128)S(1)} %bitcast.5, f32[2,12,128,128]{3,2,1,0:T(8,128)} %near_hbm.1, f32[2,12,128,128]{3,2,1,0:T(8,128)S(1)} %collective-permute-done.1.far_ref, bf16[256,1024]{1,0:T(8,128)(2,1)S(1)} %get-tuple-element.11.table_re, bf16[256,1024]{1,0:T(8,128)(2,1)S(1)} %get-tuple-element.12.table_im, ...), custom_call_target="tpu_custom_call" | custom-call | tf_op jit(solution)/shard_map/image/pallas_call | solution.py:321
  68.6 0.6 collective-permute-start.2
  69.2 1.2 %collective-permute-done.2.other_ref = f32[72,1024]{1,0:T(8,128)S(1)} collective-permute-done((f32[72,1024]{1,0:T(8,128)S(1)}, f32[72,1024]{1,0:T(8,128)S(1)}, u32[]{:S(2)}, u32[]{:S(2)}) %collective-permute-start.2) | collective-permute-done | bytes 294944 | tf_op jit(solution)/shard_map/ppermute | solution.py:335
  70.5 0.0 copy-done
  70.5 0.0 copy-done.1
  70.5 0.0 copy-done.2
  70.5 2.5 %bake.1 = (f32[64,1024]{1,0:T(8,128)}, f32[64,1024]{1,0:T(8,128)}) custom-call(f32[72,1024]{1,0:T(8,128)S(1)} %image.1.own_ref, f32[72,1024]{1,0:T(8,128)S(1)} %collective-permute-done.2.other_ref, bf16[32,4096]{1,0:T(8,128)(2,1)S(1)} %copy-done.1, bf16[32,4096]{1,0:T(8,128)(2,1)S(1)} %copy-done, f32[5]{0:T(128)S(1)} %copy-done.2), custom_call_target="tpu_custom_call" | custom-call | tf_op jit(solution)/shard_map/bake/pallas_call | solution.py:338
  (4 shorter events, 0.1 us)
Async XLA Ops:
  0.6 64.0 %collective-permute-start.1 = (f32[2,12,128,128]{3,2,1,0:T(8,128)}, f32[2,12,128,128]{3,2,1,0:T(8,128)S(1)}, u32[]{:S(2)}, u32[]{:S(2)}) collective-permute-start(f32[2,12,128,128]{3,2,1,0:T(8,128)} %near_hbm.1), channel_id=1, source_target_pairs={{128,0},{129,1},{130,2},{131,3},{132,4},{133,5},{134,6},{135,7},{1... | collective-permute-start | bytes 4718600 | tf_op jit(solution)/shard_map/ppermute | solution.py:295
  7.1 18.1 %collective-permute-start = (f32[12]{0:T(128)}, f32[12]{0:T(128)S(1)}, u32[]{:S(2)}, u32[]{:S(2)}) collective-permute-start(f32[12]{0:T(128)} %param.10), channel_id=1, source_target_pairs={{128,0},{129,1},{130,2},{131,3},{132,4},{133,5},{134,6},{135,7},{1... | collective-permute-start | bytes 152 | tf_op jit(solution)/shard_map/ppermute | solution.py:296
  64.6 5.8 %copy-start = (bf16[32,4096]{1,0:T(8,128)(2,1)S(1)}, bf16[32,4096]{1,0:T(8,128)(2,1)}, u32[]{:S(2)}) copy-start(bf16[32,4096]{1,0:T(8,128)(2,1)} %constant.7.clone.low_ref) | copy-start | bytes 786436
  64.6 5.8 %copy-start.1 = (bf16[32,4096]{1,0:T(8,128)(2,1)S(1)}, bf16[32,4096]{1,0:T(8,128)(2,1)}, u32[]{:S(2)}) copy-start(bf16[32,4096]{1,0:T(8,128)(2,1)} %constant.6.clone.high_ref) | copy-start | bytes 786436
  64.6 5.8 %copy-start.2 = (f32[5]{0:T(128)S(1)}, f32[5]{0:T(128)}, u32[]{:S(2)}) copy-start(f32[5]{0:T(128)} %rates.1) | copy-start | bytes 64
  68.6 1.8 %collective-permute-start.2 = (f32[72,1024]{1,0:T(8,128)S(1)}, f32[72,1024]{1,0:T(8,128)S(1)}, u32[]{:S(2)}, u32[]{:S(2)}) collective-permute-start(f32[72,1024]{1,0:T(8,128)S(1)} %image.1.own_ref), channel_id=1, source_target_pairs={{0,64},{1,65},{2,66},{3,67},{4,68},{5,69},{6,70},{7,71},{8,72},{9,... | collective-permute-start | bytes 884744 | tf_op jit(solution)/shard_map/ppermute | solution.py:335

commit v4 on v3

--- a/solution.py
+++ b/solution.py
@@ -49,11 +49,11 @@
     return groups_along((1, 3, 4))
 
 
-def from_next_z():
+def from_next_z(side):
     pairs = []
     for i in range(256):
         z_lo, core, z_hi, y, x = place(i)
-        z = (z_hi * CHIP_Z + z_lo + (1 if z_lo == core else -1)) % (FAR_Z * CHIP_Z)
+        z = (z_hi * CHIP_Z + z_lo + (side if z_lo == core else -side)) % (FAR_Z * CHIP_Z)
         pairs.append((device(z % CHIP_Z, core, z // CHIP_Z, y, x), i))
     return pairs
 
@@ -292,8 +292,8 @@
     freqs = band_freqs.reshape(1, W)
     f32 = jnp.float32
     params = pltpu.CompilerParams(vmem_limit_bytes=24 * 2**20)
-    far_kernels = lax.ppermute(kernels, ALL, from_next_z())
-    far_eigen = lax.ppermute(eigen_values, ALL, from_next_z())
+    far_kernels = lax.ppermute(kernels, ALL, from_next_z(1))
+    far_eigen = lax.ppermute(eigen_values, ALL, from_next_z(-1))
     own = kernels.shape[1]
     table = jax.ShapeDtypeStruct((2 * W, COARSE), jnp.bfloat16)
     part, *tables, near_eigen = pl.pallas_call(

time: 73.2 us -> 58.4 us (0.80)
  waiting for transfers between devices: 17.1 us -> 1.93 us
    ppermute x2, waiting for transfers between devices: 15.9 us -> 0.72 us  [the longest x1 0.72 us: shards(): far_eigen = lax.ppermute(eigen_values, ALL, from_next_z(-1))]
  transfers between devices with their start and end apart: 3 -> 3, of which waited for: 2 -> 2; matrix products, arithmetic and copies ran while one was open for 0% -> 0% of each run, Pallas kernels for 3% -> 4%
where the time goes in v4:
time: 58.4 us; the launch traced here: 58.1 us
  blocking collectives  39.8 us (68%)
  Pallas kernels  8.59 us (15%)
  starting transfers between devices  7.1 us (12%)
  waiting for transfers between devices  1.93 us (3%)
  between operations  0.66 us (1%)
    all_to_all x3, blocking collectives, exchange(): lax.all_to_all(blocks, ALL, 0, 0, tiled=True, axis_index_groups=groups)  39.8 us
    ppermute x1, starting transfers between devices, shards(): far_kernels = lax.ppermute(kernels, ALL, from_next_z(1))  6.48 us
    pallas_call x1, Pallas kernels, shards(): pl.pallas_call(image_kernel, out_shape=jax.ShapeDtypeStruct((RING_ROWS, C...  3.99 us
    pallas_call x1, Pallas kernels, shards(): pl.pallas_call(bake_kernel, out_shape=(block, block), in_specs=[VMEM, VME...  2.48 us
    pallas_call x1, Pallas kernels, shards(): pl.pallas_call(transform_kernel, out_shape=(jax.ShapeDtypeStruct((2 * W,...  2.12 us
    ppermute x1, waiting for transfers between devices, shards(): other_image = lax.ppermute(own_image, ALL, across_cores)  1.21 us
  transfers between devices with their start and end apart: 3, of which 2 were waited for; matrix products, arithmetic and copies ran while one was open for 0% of the time, Pallas kernels for 4%

profile of v4, /device:TPU:1, one launch (start us, length us, event | category | flops | bytes accessed | tf_op | source)
XLA Modules:
  0.0 58.1 jit_solution(2488455924425557068)
XLA Ops:
  0.6 6.5 %collective-permute-start.1 = (f32[2,12,128,128]{3,2,1,0:T(8,128)}, f32[2,12,128,128]{3,2,1,0:T(8,128)S(1)}, u32[]{:S(2)}, u32[]{:S(2)}) collective-permute-start(f32[2,12,128,128]{3,2,1,0:T(8,128)} %near_hbm.1), channel_id=1, source_target_pairs={{128,0},{129,1},{130,2},{131,3},{132,4},{133,5},{134,6},{135,7},{1... | collective-permute-start | bytes 4718600 | tf_op jit(solution)/shard_map/ppermute | solution.py:295
  7.1 0.0 collective-permute-start
  7.1 2.1 %transform.1 = (f32[256,128]{1,0:T(8,128)S(1)}, bf16[256,1024]{1,0:T(8,128)(2,1)S(1)}, bf16[256,1024]{1,0:T(8,128)(2,1)S(1)}, bf16[80,256]{1,0:T(8,128)(2,1)S(1)}, f32[1,12]{1,0:T(1,128)S(1)}) custom-call(s32[64,1024]{1,0:T(8,128)} %layout_hbm.1, s32[1,128]{1,0:T(1,128)} %bitcast.8, f32[1,12]{1,0:T(1,128)} %bitcast.9), custom_call_target="tpu_custom_call" | custom-call | tf_op jit(solution)/shard_map/transform/pallas_call | solution.py:299
  9.2 0.7 %collective-permute-done = f32[12]{0:T(128)S(1)} collective-permute-done((f32[12]{0:T(128)}, f32[12]{0:T(128)S(1)}, u32[]{:S(2)}, u32[]{:S(2)}) %collective-permute-start) | collective-permute-done | bytes 80 | tf_op jit(solution)/shard_map/ppermute | solution.py:296
  10.0 15.7 %all_to_all.23 = f32[32,8,128]{2,1,0:T(8,128)S(1)} all-to-all(f32[32,8,128]{2,1,0:T(8,128)S(1)} %bitcast.6), channel_id=1, replica_groups={{0,1,2,3,4,5,6,7,8,9,10,11,12,13,14,15,64,65,66,67,68,69,70,71,72,73,74..., dimensions={0} | all-to-all | bytes 262144 | tf_op jit(solution)/shard_map/all_to_all | solution.py:278
  25.7 11.5 %all_to_all.24 = f32[8,8,128]{2,1,0:T(8,128)S(1)} all-to-all(f32[8,8,128]{2,1,0:T(8,128)S(1)} %broadcast_in_dim.4), channel_id=1, replica_groups={{0,16,32,48,128,144,160,176},{1,17,33,49,129,145,161,177},{2,18,34,50,1..., dimensions={0} | all-to-all | bytes 65536 | tf_op jit(solution)/shard_map/all_to_all | solution.py:278
  37.2 12.6 %all_to_all.25 = f32[32,8,128]{2,1,0:T(8,128)S(1)} all-to-all(f32[32,8,128]{2,1,0:T(8,128)S(1)} %broadcast_in_dim.5), channel_id=1, replica_groups={{0,1,2,3,4,5,6,7,8,9,10,11,12,13,14,15,64,65,66,67,68,69,70,71,72,73,74..., dimensions={0} | all-to-all | bytes 262144 | tf_op jit(solution)/shard_map/all_to_all | solution.py:278
  49.8 0.0 collective-permute-done.1.far_ref
  49.8 0.0 copy-start
  49.8 0.0 copy-start.1
  49.8 0.0 copy-start.2
  49.8 4.0 %image.1.own_ref = f32[72,1024]{1,0:T(8,128)S(1)} custom-call(f32[256,128]{1,0:T(8,128)S(1)} %bitcast.5, f32[2,12,128,128]{3,2,1,0:T(8,128)} %near_hbm.1, f32[2,12,128,128]{3,2,1,0:T(8,128)S(1)} %collective-permute-done.1.far_ref, bf16[256,1024]{1,0:T(8,128)(2,1)S(1)} %get-tuple-element.11.table_re, bf16[256,1024]{1,0:T(8,128)(2,1)S(1)} %get-tuple-element.12.table_im, ...), custom_call_target="tpu_custom_call" | custom-call | tf_op jit(solution)/shard_map/image/pallas_call | solution.py:321
  53.8 0.6 %collective-permute-start.2 = (f32[72,1024]{1,0:T(8,128)S(1)}, f32[72,1024]{1,0:T(8,128)S(1)}, u32[]{:S(2)}, u32[]{:S(2)}) collective-permute-start(f32[72,1024]{1,0:T(8,128)S(1)} %image.1.own_ref), channel_id=1, source_target_pairs={{0,64},{1,65},{2,66},{3,67},{4,68},{5,69},{6,70},{7,71},{8,72},{9,... | collective-permute-start | bytes 884744 | tf_op jit(solution)/shard_map/ppermute | solution.py:335
  54.5 1.2 %collective-permute-done.2.other_ref = f32[72,1024]{1,0:T(8,128)S(1)} collective-permute-done((f32[72,1024]{1,0:T(8,128)S(1)}, f32[72,1024]{1,0:T(8,128)S(1)}, u32[]{:S(2)}, u32[]{:S(2)}) %collective-permute-start.2) | collective-permute-done | bytes 294944 | tf_op jit(solution)/shard_map/ppermute | solution.py:335
  55.7 0.0 copy-done
  55.7 0.0 copy-done.1
  55.7 0.0 copy-done.2
  55.7 2.5 %bake.1 = (f32[64,1024]{1,0:T(8,128)}, f32[64,1024]{1,0:T(8,128)}) custom-call(f32[72,1024]{1,0:T(8,128)S(1)} %image.1.own_ref, f32[72,1024]{1,0:T(8,128)S(1)} %collective-permute-done.2.other_ref, bf16[32,4096]{1,0:T(8,128)(2,1)S(1)} %copy-done.1, bf16[32,4096]{1,0:T(8,128)(2,1)S(1)} %copy-done, f32[5]{0:T(128)S(1)} %copy-done.2), custom_call_target="tpu_custom_call" | custom-call | tf_op jit(solution)/shard_map/bake/pallas_call | solution.py:338
  (4 shorter events, 0.1 us)
Async XLA Ops:
  0.6 49.2 %collective-permute-start.1 = (f32[2,12,128,128]{3,2,1,0:T(8,128)}, f32[2,12,128,128]{3,2,1,0:T(8,128)S(1)}, u32[]{:S(2)}, u32[]{:S(2)}) collective-permute-start(f32[2,12,128,128]{3,2,1,0:T(8,128)} %near_hbm.1), channel_id=1, source_target_pairs={{128,0},{129,1},{130,2},{131,3},{132,4},{133,5},{134,6},{135,7},{1... | collective-permute-start | bytes 4718600 | tf_op jit(solution)/shard_map/ppermute | solution.py:295
  7.1 2.9 %collective-permute-start = (f32[12]{0:T(128)}, f32[12]{0:T(128)S(1)}, u32[]{:S(2)}, u32[]{:S(2)}) collective-permute-start(f32[12]{0:T(128)} %param.10), channel_id=1, source_target_pairs={{176,0},{177,1},{178,2},{179,3},{180,4},{181,5},{182,6},{183,7},{1... | collective-permute-start | bytes 152 | tf_op jit(solution)/shard_map/ppermute | solution.py:296
  49.8 5.8 %copy-start = (bf16[32,4096]{1,0:T(8,128)(2,1)S(1)}, bf16[32,4096]{1,0:T(8,128)(2,1)}, u32[]{:S(2)}) copy-start(bf16[32,4096]{1,0:T(8,128)(2,1)} %constant.7.clone.low_ref) | copy-start | bytes 786436
  49.8 5.8 %copy-start.1 = (bf16[32,4096]{1,0:T(8,128)(2,1)S(1)}, bf16[32,4096]{1,0:T(8,128)(2,1)}, u32[]{:S(2)}) copy-start(bf16[32,4096]{1,0:T(8,128)(2,1)} %constant.6.clone.high_ref) | copy-start | bytes 786436
  49.8 5.8 %copy-start.2 = (f32[5]{0:T(128)S(1)}, f32[5]{0:T(128)}, u32[]{:S(2)}) copy-start(f32[5]{0:T(128)} %rates.1) | copy-start | bytes 64
  53.8 1.8 %collective-permute-start.2 = (f32[72,1024]{1,0:T(8,128)S(1)}, f32[72,1024]{1,0:T(8,128)S(1)}, u32[]{:S(2)}, u32[]{:S(2)}) collective-permute-start(f32[72,1024]{1,0:T(8,128)S(1)} %image.1.own_ref), channel_id=1, source_target_pairs={{0,64},{1,65},{2,66},{3,67},{4,68},{5,69},{6,70},{7,71},{8,72},{9,... | collective-permute-start | bytes 884744 | tf_op jit(solution)/shard_map/ppermute | solution.py:335

commit v5 on v4

--- a/solution.py
+++ b/solution.py
@@ -82,27 +82,28 @@
     return lax.broadcasted_iota(jnp.int32, shape, dim)
 
 
-def image_tables(freqs, row_first, re_ref, im_ref, row_ref):
-    row = iota((MXU_ROWS, W), 0)
-    row = jnp.where(row < ROWS + 4, row, row - RING_ROWS)
-    cos_row, sin_row = cos_sin((row_first + row) * freqs)
-    row_ref[:, 0:W] = cos_row.astype(jnp.bfloat16)
-    row_ref[:, W : 2 * W] = sin_row.astype(jnp.bfloat16)
-
-    freqs_col = jnp.broadcast_to(freqs, (W, W)).astype(jnp.float32).T.astype(jnp.int32)
-    cos, sin = cos_sin((SPARSE * iota((W, 128), 1)) * freqs_col)
-    turn_cos, turn_sin = cos_sin((SPARSE * 128) * freqs_col)
+def image_tables(freqs, weights_ref):
+    low_cos, low_sin = cos_sin(SPARSE * iota((8, W), 0) * freqs)
+    high_cos, high_sin = cos_sin(SPARSE * 8 * iota((16, W), 0) * freqs)
+    turn_cos, turn_sin = cos_sin(jnp.broadcast_to(SPARSE * 128 * freqs, (8, W)))
+    cos_parts, sin_parts = [], []
+    for a in range(16):
+        ca, sa = high_cos[a : a + 1, :], high_sin[a : a + 1, :]
+        cos_parts.append(ca * low_cos - sa * low_sin)
+        sin_parts.append(sa * low_cos + ca * low_sin)
+    cos = jnp.concatenate(cos_parts, 0).T
+    sin = jnp.concatenate(sin_parts, 0).T
+    turn_cos = jnp.broadcast_to(turn_cos[0:1], (W, W)).T
+    turn_sin = jnp.broadcast_to(turn_sin[0:1], (W, W)).T
     for tile in range(COARSE // 128):
         at = slice(tile * 128, tile * 128 + 128)
-        re_ref[0:W, at] = cos.astype(jnp.bfloat16)
-        re_ref[W : 2 * W, at] = (-sin).astype(jnp.bfloat16)
-        im_ref[0:W, at] = sin.astype(jnp.bfloat16)
-        im_ref[W : 2 * W, at] = cos.astype(jnp.bfloat16)
+        weights_ref[0:W, at] = cos.astype(jnp.bfloat16)
+        weights_ref[W : 2 * W, at] = sin.astype(jnp.bfloat16)
         cos, sin = cos * turn_cos - sin * turn_sin, sin * turn_cos + cos * turn_sin
 
 
 def transform_kernel(
-    layout_hbm, freqs_hbm, eigen_hbm, out_ref, re_ref, im_ref, row_ref, eigen_ref, table, layout_ref, freqs_ref, sems
+    layout_hbm, freqs_hbm, eigen_hbm, out_ref, weights_ref, row_ref, eigen_ref, table, layout_ref, freqs_ref, sems
 ):
     freqs_copy = pltpu.make_async_copy(freqs_hbm, freqs_ref, sems.at[0])
     layout_copy = pltpu.make_async_copy(layout_hbm, layout_ref, sems.at[1])
@@ -128,11 +129,12 @@
         table[at, W : 2 * W] = sin_high
         table[at, 2 * W : 3 * W] = cos_low
         table[at, 3 * W : 4 * W] = sin_low
-    cos_row, sin_row = cos_sin((row_first + iota((ROWS, W), 0)) * freqs)
-    left_high, left_low = split(jnp.concatenate([cos_row, sin_row], 0))
-    image_tables(freqs, row_first, re_ref, im_ref, row_ref)
+    row = iota((MXU_ROWS, W), 0)
+    row = jnp.where(row < ROWS + 4, row, row - RING_ROWS)
+    cos_row, sin_row = cos_sin((row_first + row) * freqs)
+    row_ref[...] = (jnp.concatenate([cos_row, sin_row], 1) / W).astype(jnp.bfloat16)
+    left_high, left_low = split(jnp.concatenate([cos_row[0:ROWS], sin_row[0:ROWS]], 0))
     layout_copy.wait()
-    eigen_copy.wait()
     transmit = (2 * layout_ref[...] - 1).astype(jnp.float32).astype(jnp.bfloat16)
     along = jnp.dot(transmit, table[...], preferred_element_type=jnp.float32)
     along_re = along[:, 0:W] + along[:, 2 * W : 3 * W]
@@ -153,10 +155,13 @@
     ) * (1.0 / N)
     out_ref[0:W, :] = both[:, 0:W]
     out_ref[W : 2 * W, :] = both[:, W : 2 * W]
+    image_tables(freqs, weights_ref)
+    eigen_copy.wait()
 
 
 def image_kernel(
-    spec_ref, near_hbm, far_ref, table_re, table_im, row_ref, near_eigen, far_eigen, image_ref, fields, near_ref, sem
+    spec_ref, near_hbm, far_ref, weights_ref, row_ref, near_eigen, far_eigen, image_ref,
+    fields_re, fields_im, near_ref, sem,
 ):
     near_copy = pltpu.make_async_copy(near_hbm, near_ref, sem)
     near_copy.start()
@@ -173,28 +178,45 @@
         block = jnp.concatenate(
             [jnp.concatenate([re16, im16], 1), jnp.concatenate([-im16, re16], 1)], 0
         )
-        return jnp.dot(row_table, block, preferred_element_type=jnp.float32)[0:RING_ROWS] / W
-
-    for kernels_ref, first in ((far_ref, 0), (near_ref, own)):
-        if first:
-            near_copy.wait()
-        for f in range(0, own, 2):
-            both = jnp.concatenate([row_field(kernels_ref, f), row_field(kernels_ref, f + 1)], 0)
-            at = (first + f) * RING_ROWS
-            fields[at : at + 2 * RING_ROWS, :] = both.astype(jnp.bfloat16)
-
-    eigen = [ref[0:1, f : f + 1] for ref in (far_eigen, near_eigen) for f in range(own)]
-    for p in range(COARSE // 256):
-        at = slice(p * 256, (p + 1) * 256)
-        rows = fields[...]
-        real = jnp.dot(rows, table_re[:, at], preferred_element_type=jnp.float32)
-        imag = jnp.dot(rows, table_im[:, at], preferred_element_type=jnp.float32)
-        total = jnp.zeros((RING_ROWS, 256), jnp.float32)
-        for f in range(2 * own):
+        part = jnp.dot(row_table, block, preferred_element_type=jnp.float32)
+        real = part[0:RING_ROWS, 0:W]
+        imag = part[0:RING_ROWS, W : 2 * W]
+        return real, imag
+
+    def pair_of_fields(kernels_ref, f, first):
+        pair = [row_field(kernels_ref, f), row_field(kernels_ref, f + 1)]
+        real = jnp.concatenate([pair[0][0], pair[1][0]], 0).astype(jnp.bfloat16)
+        imag = jnp.concatenate([pair[0][1], pair[1][1]], 0).astype(jnp.bfloat16)
+        at = slice((first + f) * RING_ROWS, (first + f + 2) * RING_ROWS)
+        fields_re[at, 0:W] = real
+        fields_re[at, W : 2 * W] = -imag
+        fields_im[at, 0:W] = imag
+        fields_im[at, W : 2 * W] = real
+
+    def power(first, count, eigen_ref, f0, p, start):
+        rows = slice(first * RING_ROWS, (first + count) * RING_ROWS)
+        weights = weights_ref[:, p * 256 : (p + 1) * 256]
+        real = jnp.dot(fields_re[rows, :], weights, preferred_element_type=jnp.float32)
+        imag = jnp.dot(fields_im[rows, :], weights, preferred_element_type=jnp.float32)
+        for f in range(count):
             re = real[f * RING_ROWS : (f + 1) * RING_ROWS]
             im = imag[f * RING_ROWS : (f + 1) * RING_ROWS]
-            total = total + eigen[f] * (re * re + im * im)
-        image_ref[:, at] = total
+            term = eigen_ref[0:1, f0 + f : f0 + f + 1] * (re * re + im * im)
+            start = term if start is None else start + term
+        return start
+
+    parts = COARSE // 256
+    for f in range(0, own, 2):
+        pair_of_fields(far_ref, f, 0)
+    near_copy.wait()
+    for p in range(parts):
+        for f in range(0, own, 2):
+            if p == min(f * parts // own + (f > 0), parts - 1):
+                pair_of_fields(near_ref, f, own)
+        image_ref[:, p * 256 : (p + 1) * 256] = power(0, own, far_eigen, 0, p, None)
+    for p in range(parts):
+        at = slice(p * 256, (p + 1) * 256)
+        image_ref[:, at] = power(own, own, near_eigen, 0, p, image_ref[:, at])
 
 
 def dirichlet():
@@ -219,14 +241,16 @@
     )
 
 
-def bake_kernel(own_ref, other_ref, high_ref, low_ref, rates, image_ref, acid_ref, parts, ring):
+def bake_kernel(
+    own_ref, other_ref, high_ref, low_ref, rates, image_hbm, acid_hbm, parts, ring, image_ref, acid_ref, sems
+):
     kern = lax.axis_index("kern")
     for p in range(COARSE // 256):
         block = jnp.bitwise_and(p - kern, COARSE // 256 - 1)
         at = pl.ds(pl.multiple_of(block * 256, 256), 256)
-        high, low = split(own_ref[:, p * 256 : (p + 1) * 256] + other_ref[:, p * 256 : (p + 1) * 256])
-        parts[0:RING_ROWS, at] = high
-        parts[MXU_ROWS : MXU_ROWS + RING_ROWS, at] = low
+        value = own_ref[:, p * 256 : (p + 1) * 256] + other_ref[:, p * 256 : (p + 1) * 256]
+        high = value.astype(jnp.bfloat16).astype(jnp.float32)
+        parts[0 : 2 * RING_ROWS, at] = jnp.concatenate([high, value - high], 0).astype(jnp.bfloat16)
 
     def weights(ref, tiles):
         rows = [
@@ -237,9 +261,9 @@
 
     for p in range(5):
         tiles = (2 * p, 2 * p + 1) if p < 4 else (8, 31)
-        wide = jnp.dot(parts[...], weights(high_ref, tiles), preferred_element_type=jnp.float32)
+        wide = jnp.dot(parts[0 : 2 * RING_ROWS, :], weights(high_ref, tiles), preferred_element_type=jnp.float32)
         fine = jnp.dot(parts[0:MXU_ROWS, :], weights(low_ref, tiles), preferred_element_type=jnp.float32)
-        value = wide[0:RING_ROWS] + (wide[MXU_ROWS : MXU_ROWS + RING_ROWS] + fine[0:RING_ROWS])
+        value = wide[0:RING_ROWS] + (wide[RING_ROWS : 2 * RING_ROWS] + fine[0:RING_ROWS])
         if p < 4:
             ring[:, p * 256 : (p + 1) * 256] = value
         else:
@@ -249,6 +273,8 @@
     dill_rate, acid_rate, quench_rate, react_rate, quench_start = (rates[i] for i in range(5))
     aerial_image = ring[...] / FIELDS
     image_ref[...] = aerial_image[0:ROWS, 0:COLS]
+    image_copy = pltpu.make_async_copy(image_ref, image_hbm, sems.at[0])
+    image_copy.start()
     acid_field = 1.0 - jnp.exp((-4.0 * dill_rate) * aerial_image)
     acid_diffusion = acid_rate * (0.5 + 0.5 * acid_field)
     quencher = jnp.zeros_like(acid_field) + quench_start
@@ -258,6 +284,10 @@
         quencher = quencher + quench_rate * laplace(quencher) - reaction
         acid_field = new_acid
     acid_ref[...] = acid_field[0:ROWS, 0:COLS]
+    acid_copy = pltpu.make_async_copy(acid_ref, acid_hbm, sems.at[1])
+    acid_copy.start()
+    image_copy.wait()
+    acid_copy.wait()
 
 
 VMEM = pl.BlockSpec(memory_space=pltpu.VMEM)
@@ -295,18 +325,16 @@
     far_kernels = lax.ppermute(kernels, ALL, from_next_z(1))
     far_eigen = lax.ppermute(eigen_values, ALL, from_next_z(-1))
     own = kernels.shape[1]
-    table = jax.ShapeDtypeStruct((2 * W, COARSE), jnp.bfloat16)
     part, *tables, near_eigen = pl.pallas_call(
         transform_kernel,
         out_shape=(
             jax.ShapeDtypeStruct((2 * W, W), f32),
-            table,
-            table,
+            jax.ShapeDtypeStruct((2 * W, COARSE), jnp.bfloat16),
             jax.ShapeDtypeStruct((MXU_ROWS, 2 * W), jnp.bfloat16),
             jax.ShapeDtypeStruct((1, own), f32),
         ),
-        in_specs=[HBM, HBM, HBM],
-        out_specs=(VMEM,) * 5,
+        in_specs=[HBM] * 3,
+        out_specs=(VMEM,) * 4,
         scratch_shapes=[
             pltpu.VMEM((COLS, 4 * W), jnp.bfloat16),
             pltpu.VMEM((ROWS, COLS), jnp.int32),
@@ -321,9 +349,10 @@
     own_image = pl.pallas_call(
         image_kernel,
         out_shape=jax.ShapeDtypeStruct((RING_ROWS, COARSE), f32),
-        in_specs=[VMEM, HBM] + [VMEM] * 6,
+        in_specs=[VMEM, HBM] + [VMEM] * 5,
         out_specs=VMEM,
         scratch_shapes=[
+            pltpu.VMEM((2 * own * RING_ROWS, 2 * W), jnp.bfloat16),
             pltpu.VMEM((2 * own * RING_ROWS, 2 * W), jnp.bfloat16),
             pltpu.VMEM(kernels.shape, f32),
             pltpu.SemaphoreType.DMA,
@@ -339,10 +368,13 @@
         bake_kernel,
         out_shape=(block, block),
         in_specs=[VMEM, VMEM, VMEM, VMEM, SMEM],
-        out_specs=(VMEM, VMEM),
+        out_specs=(HBM, HBM),
         scratch_shapes=[
             pltpu.VMEM((2 * MXU_ROWS, COARSE), jnp.bfloat16),
             pltpu.VMEM((RING_ROWS, RING_COLS), f32),
+            pltpu.VMEM((ROWS, COLS), f32),
+            pltpu.VMEM((ROWS, COLS), f32),
+            pltpu.SemaphoreType.DMA((2,)),
         ],
         compiler_params=params,
         name="bake",

time: 58.4 us -> 58.5 us (level)
  transfers between devices with their start and end apart: 3 -> 3, of which waited for: 2 -> 2; matrix products, arithmetic and copies ran while one was open for 0% -> 0% of each run, Pallas kernels for 4% -> 3%
where the time goes in v5:
time: 58.5 us; the launch traced here: 58.3 us
  blocking collectives  39.8 us (68%)
  Pallas kernels  8.24 us (14%)
  starting transfers between devices  7.1 us (12%)
  waiting for transfers between devices  2.43 us (4%)
  between operations  0.66 us (1%)
    all_to_all x3, blocking collectives, exchange(): lax.all_to_all(blocks, ALL, 0, 0, tiled=True, axis_index_groups=groups)  39.8 us
    ppermute x1, starting transfers between devices, shards(): far_kernels = lax.ppermute(kernels, ALL, from_next_z(1))  6.48 us
    pallas_call x1, Pallas kernels, shards(): pl.pallas_call(image_kernel, out_shape=jax.ShapeDtypeStruct((RING_ROWS, C...  4.08 us
    pallas_call x1, Pallas kernels, shards(): pl.pallas_call(bake_kernel, out_shape=(block, block), in_specs=[VMEM, VME...  2.54 us
    pallas_call x1, Pallas kernels, shards(): pl.pallas_call(transform_kernel, out_shape=(jax.ShapeDtypeStruct((2 * W,...  1.62 us
    ppermute x1, waiting for transfers between devices, shards(): far_eigen = lax.ppermute(eigen_values, ALL, from_next_z(-1))  1.22 us
    ppermute x1, waiting for transfers between devices, shards(): other_image = lax.ppermute(own_image, ALL, across_cores)  1.21 us
  transfers between devices with their start and end apart: 3, of which 2 were waited for; matrix products, arithmetic and copies ran while one was open for 0% of the time, Pallas kernels for 3%

profile of v5, /device:TPU:1, one launch (start us, length us, event | category | flops | bytes accessed | tf_op | source)
XLA Modules:
  0.0 58.3 jit_solution(8830077347435401372)
XLA Ops:
  0.6 6.5 %collective-permute-start.1 = (f32[2,12,128,128]{3,2,1,0:T(8,128)}, f32[2,12,128,128]{3,2,1,0:T(8,128)S(1)}, u32[]{:S(2)}, u32[]{:S(2)}) collective-permute-start(f32[2,12,128,128]{3,2,1,0:T(8,128)} %near_hbm.1), channel_id=1, source_target_pairs={{128,0},{129,1},{130,2},{131,3},{132,4},{133,5},{134,6},{135,7},{1... | collective-permute-start | bytes 4718600 | tf_op jit(solution)/shard_map/ppermute | solution.py:325
  7.1 0.0 collective-permute-start
  7.1 1.6 %transform.1 = (f32[256,128]{1,0:T(8,128)S(1)}, bf16[256,1024]{1,0:T(8,128)(2,1)S(1)}, bf16[80,256]{1,0:T(8,128)(2,1)S(1)}, f32[1,12]{1,0:T(1,128)S(1)}) custom-call(s32[64,1024]{1,0:T(8,128)} %layout_hbm.1, s32[1,128]{1,0:T(1,128)} %bitcast.8, f32[1,12]{1,0:T(1,128)} %bitcast.9), custom_call_target="tpu_custom_call" | custom-call | tf_op jit(solution)/shard_map/transform/pallas_call | solution.py:328
  8.7 1.2 %collective-permute-done = f32[12]{0:T(128)S(1)} collective-permute-done((f32[12]{0:T(128)}, f32[12]{0:T(128)S(1)}, u32[]{:S(2)}, u32[]{:S(2)}) %collective-permute-start) | collective-permute-done | bytes 80 | tf_op jit(solution)/shard_map/ppermute | solution.py:326
  10.0 15.2 %all_to_all.23 = f32[32,8,128]{2,1,0:T(8,128)S(1)} all-to-all(f32[32,8,128]{2,1,0:T(8,128)S(1)} %bitcast.6), channel_id=1, replica_groups={{0,1,2,3,4,5,6,7,8,9,10,11,12,13,14,15,64,65,66,67,68,69,70,71,72,73,74..., dimensions={0} | all-to-all | bytes 262144 | tf_op jit(solution)/shard_map/all_to_all | solution.py:308
  25.2 12.0 %all_to_all.24 = f32[8,8,128]{2,1,0:T(8,128)S(1)} all-to-all(f32[8,8,128]{2,1,0:T(8,128)S(1)} %broadcast_in_dim.4), channel_id=1, replica_groups={{0,16,32,48,128,144,160,176},{1,17,33,49,129,145,161,177},{2,18,34,50,1..., dimensions={0} | all-to-all | bytes 65536 | tf_op jit(solution)/shard_map/all_to_all | solution.py:308
  37.2 12.6 %all_to_all.25 = f32[32,8,128]{2,1,0:T(8,128)S(1)} all-to-all(f32[32,8,128]{2,1,0:T(8,128)S(1)} %broadcast_in_dim.5), channel_id=1, replica_groups={{0,1,2,3,4,5,6,7,8,9,10,11,12,13,14,15,64,65,66,67,68,69,70,71,72,73,74..., dimensions={0} | all-to-all | bytes 262144 | tf_op jit(solution)/shard_map/all_to_all | solution.py:308
  49.8 0.0 collective-permute-done.1.far_ref
  49.8 0.0 copy-start
  49.8 0.0 copy-start.1
  49.8 0.0 copy-start.2
  49.8 4.1 %image.1.own_ref = f32[72,1024]{1,0:T(8,128)S(1)} custom-call(f32[256,128]{1,0:T(8,128)S(1)} %bitcast.5, f32[2,12,128,128]{3,2,1,0:T(8,128)} %near_hbm.1, f32[2,12,128,128]{3,2,1,0:T(8,128)S(1)} %collective-permute-done.1.far_ref, bf16[256,1024]{1,0:T(8,128)(2,1)S(1)} %get-tuple-element.10.weights_ref, bf16[80,256]{1,0:T(8,128)(2,1)S(1)} %get-tuple-element.11.row_ref, ...), custom_call_target="tpu_custom_call" | custom-call | tf_op jit(solution)/shard_map/image/pallas_call | solution.py:349
  53.9 0.6 %collective-permute-start.2 = (f32[72,1024]{1,0:T(8,128)S(1)}, f32[72,1024]{1,0:T(8,128)S(1)}, u32[]{:S(2)}, u32[]{:S(2)}) collective-permute-start(f32[72,1024]{1,0:T(8,128)S(1)} %image.1.own_ref), channel_id=1, source_target_pairs={{0,64},{1,65},{2,66},{3,67},{4,68},{5,69},{6,70},{7,71},{8,72},{9,... | collective-permute-start | bytes 884744 | tf_op jit(solution)/shard_map/ppermute | solution.py:364
  54.5 1.2 %collective-permute-done.2.other_ref = f32[72,1024]{1,0:T(8,128)S(1)} collective-permute-done((f32[72,1024]{1,0:T(8,128)S(1)}, f32[72,1024]{1,0:T(8,128)S(1)}, u32[]{:S(2)}, u32[]{:S(2)}) %collective-permute-start.2) | collective-permute-done | bytes 294944 | tf_op jit(solution)/shard_map/ppermute | solution.py:364
  55.8 0.0 copy-done
  55.8 0.0 copy-done.1
  55.8 0.0 copy-done.2
  55.8 2.5 %bake.1 = (f32[64,1024]{1,0:T(8,128)}, f32[64,1024]{1,0:T(8,128)}) custom-call(f32[72,1024]{1,0:T(8,128)S(1)} %image.1.own_ref, f32[72,1024]{1,0:T(8,128)S(1)} %collective-permute-done.2.other_ref, bf16[32,4096]{1,0:T(8,128)(2,1)S(1)} %copy-done.1, bf16[32,4096]{1,0:T(8,128)(2,1)S(1)} %copy-done, f32[5]{0:T(128)S(1)} %copy-done.2), custom_call_target="tpu_custom_call" | custom-call | tf_op jit(solution)/shard_map/bake/pallas_call | solution.py:367
  (4 shorter events, 0.1 us)
Async XLA Ops:
  0.6 49.2 %collective-permute-start.1 = (f32[2,12,128,128]{3,2,1,0:T(8,128)}, f32[2,12,128,128]{3,2,1,0:T(8,128)S(1)}, u32[]{:S(2)}, u32[]{:S(2)}) collective-permute-start(f32[2,12,128,128]{3,2,1,0:T(8,128)} %near_hbm.1), channel_id=1, source_target_pairs={{128,0},{129,1},{130,2},{131,3},{132,4},{133,5},{134,6},{135,7},{1... | collective-permute-start | bytes 4718600 | tf_op jit(solution)/shard_map/ppermute | solution.py:325
  7.1 2.9 %collective-permute-start = (f32[12]{0:T(128)}, f32[12]{0:T(128)S(1)}, u32[]{:S(2)}, u32[]{:S(2)}) collective-permute-start(f32[12]{0:T(128)} %param.10), channel_id=1, source_target_pairs={{176,0},{177,1},{178,2},{179,3},{180,4},{181,5},{182,6},{183,7},{1... | collective-permute-start | bytes 152 | tf_op jit(solution)/shard_map/ppermute | solution.py:326
  49.8 5.9 %copy-start = (bf16[32,4096]{1,0:T(8,128)(2,1)S(1)}, bf16[32,4096]{1,0:T(8,128)(2,1)}, u32[]{:S(2)}) copy-start(bf16[32,4096]{1,0:T(8,128)(2,1)} %constant.7.clone.low_ref) | copy-start | bytes 786436
  49.8 5.9 %copy-start.1 = (bf16[32,4096]{1,0:T(8,128)(2,1)S(1)}, bf16[32,4096]{1,0:T(8,128)(2,1)}, u32[]{:S(2)}) copy-start(bf16[32,4096]{1,0:T(8,128)(2,1)} %constant.6.clone.high_ref) | copy-start | bytes 786436
  49.8 5.9 %copy-start.2 = (f32[5]{0:T(128)S(1)}, f32[5]{0:T(128)}, u32[]{:S(2)}) copy-start(f32[5]{0:T(128)} %rates.1) | copy-start | bytes 64
  53.9 1.8 %collective-permute-start.2 = (f32[72,1024]{1,0:T(8,128)S(1)}, f32[72,1024]{1,0:T(8,128)S(1)}, u32[]{:S(2)}, u32[]{:S(2)}) collective-permute-start(f32[72,1024]{1,0:T(8,128)S(1)} %image.1.own_ref), channel_id=1, source_target_pairs={{0,64},{1,65},{2,66},{3,67},{4,68},{5,69},{6,70},{7,71},{8,72},{9,... | collective-permute-start | bytes 884744 | tf_op jit(solution)/shard_map/ppermute | solution.py:364

commit v6 on v5

--- a/solution.py
+++ b/solution.py
@@ -82,7 +82,13 @@
     return lax.broadcasted_iota(jnp.int32, shape, dim)
 
 
-def image_tables(freqs, weights_ref):
+def tables_kernel(freqs_ref, weights_ref, row_ref):
+    freqs = freqs_ref[...]
+    row = iota((MXU_ROWS, W), 0)
+    row = jnp.where(row < ROWS + 4, row, row - RING_ROWS)
+    cos_row, sin_row = cos_sin((lax.axis_index("slab") * ROWS + row) * freqs)
+    row_ref[...] = (jnp.concatenate([cos_row, sin_row], 1) / W).astype(jnp.bfloat16)
+
     low_cos, low_sin = cos_sin(SPARSE * iota((8, W), 0) * freqs)
     high_cos, high_sin = cos_sin(SPARSE * 8 * iota((16, W), 0) * freqs)
     turn_cos, turn_sin = cos_sin(jnp.broadcast_to(SPARSE * 128 * freqs, (8, W)))
@@ -103,7 +109,7 @@
 
 
 def transform_kernel(
-    layout_hbm, freqs_hbm, eigen_hbm, out_ref, weights_ref, row_ref, eigen_ref, table, layout_ref, freqs_ref, sems
+    layout_hbm, freqs_hbm, eigen_hbm, out_ref, freqs_ref, eigen_ref, table, layout_ref, sems
 ):
     freqs_copy = pltpu.make_async_copy(freqs_hbm, freqs_ref, sems.at[0])
     layout_copy = pltpu.make_async_copy(layout_hbm, layout_ref, sems.at[1])
@@ -129,11 +135,8 @@
         table[at, W : 2 * W] = sin_high
         table[at, 2 * W : 3 * W] = cos_low
         table[at, 3 * W : 4 * W] = sin_low
-    row = iota((MXU_ROWS, W), 0)
-    row = jnp.where(row < ROWS + 4, row, row - RING_ROWS)
-    cos_row, sin_row = cos_sin((row_first + row) * freqs)
-    row_ref[...] = (jnp.concatenate([cos_row, sin_row], 1) / W).astype(jnp.bfloat16)
-    left_high, left_low = split(jnp.concatenate([cos_row[0:ROWS], sin_row[0:ROWS]], 0))
+    cos_row, sin_row = cos_sin((row_first + iota((ROWS, W), 0)) * freqs)
+    left_high, left_low = split(jnp.concatenate([cos_row, sin_row], 0))
     layout_copy.wait()
     transmit = (2 * layout_ref[...] - 1).astype(jnp.float32).astype(jnp.bfloat16)
     along = jnp.dot(transmit, table[...], preferred_element_type=jnp.float32)
@@ -155,7 +158,6 @@
     ) * (1.0 / N)
     out_ref[0:W, :] = both[:, 0:W]
     out_ref[W : 2 * W, :] = both[:, W : 2 * W]
-    image_tables(freqs, weights_ref)
     eigen_copy.wait()
 
 
@@ -299,7 +301,7 @@
     return pltpu.with_memory_space_constraint(array, pltpu.HBM)
 
 
-def sum_everywhere(part):
+def sum_everywhere(part, beside):
     plane, along_z = plane_groups(), z_groups()
     count = len(plane[0])
     piece = part.shape[0] // count
@@ -313,9 +315,10 @@
     def copies(block, many):
         return jnp.broadcast_to(block[None], (many,) + block.shape).reshape(-1, block.shape[1])
 
-    some = total(exchange(part, plane))
+    blocks, beside = lax.optimization_barrier((exchange(part, plane), beside))
+    some = total(blocks)
     full = total(exchange(copies(some, len(along_z[0])), along_z))
-    return exchange(copies(full, count), plane)
+    return exchange(copies(full, count), plane), beside
 
 
 def shards(layout, band_freqs, kernels, eigen_values, bake_rates):
@@ -325,27 +328,36 @@
     far_kernels = lax.ppermute(kernels, ALL, from_next_z(1))
     far_eigen = lax.ppermute(eigen_values, ALL, from_next_z(-1))
     own = kernels.shape[1]
-    part, *tables, near_eigen = pl.pallas_call(
+    part, freqs_here, near_eigen = pl.pallas_call(
         transform_kernel,
         out_shape=(
             jax.ShapeDtypeStruct((2 * W, W), f32),
-            jax.ShapeDtypeStruct((2 * W, COARSE), jnp.bfloat16),
-            jax.ShapeDtypeStruct((MXU_ROWS, 2 * W), jnp.bfloat16),
+            jax.ShapeDtypeStruct((1, W), jnp.int32),
             jax.ShapeDtypeStruct((1, own), f32),
         ),
         in_specs=[HBM] * 3,
-        out_specs=(VMEM,) * 4,
+        out_specs=(VMEM,) * 3,
         scratch_shapes=[
             pltpu.VMEM((COLS, 4 * W), jnp.bfloat16),
             pltpu.VMEM((ROWS, COLS), jnp.int32),
-            pltpu.VMEM((1, W), jnp.int32),
             pltpu.SemaphoreType.DMA((3,)),
         ],
         compiler_params=params,
         name="transform",
     )(in_hbm(layout), in_hbm(freqs), in_hbm(eigen_values.reshape(1, own)))
-    part, far_eigen = lax.optimization_barrier((part, far_eigen))
-    spectrum = sum_everywhere(part)
+    tables = pl.pallas_call(
+        tables_kernel,
+        out_shape=(
+            jax.ShapeDtypeStruct((2 * W, COARSE), jnp.bfloat16),
+            jax.ShapeDtypeStruct((MXU_ROWS, 2 * W), jnp.bfloat16),
+        ),
+        in_specs=[VMEM],
+        out_specs=(VMEM, VMEM),
+        compiler_params=params,
+        cost_estimate=pl.CostEstimate(flops=2_000_000, transcendentals=0, bytes_accessed=1_000_000),
+        name="tables",
+    )(freqs_here)
+    spectrum, (far_eigen, tables) = sum_everywhere(part, (far_eigen, tables))
     own_image = pl.pallas_call(
         image_kernel,
         out_shape=jax.ShapeDtypeStruct((RING_ROWS, COARSE), f32),

time: 58.5 us -> 57.1 us (0.976)
  blocking collectives: 39.8 us -> 24.2 us
  starting transfers between devices: 7.1 us -> 14.4 us
  waiting for transfers between devices: 2.43 us -> 8.32 us
  Pallas kernels: 8.24 us -> 9.21 us
    all_to_all x3 -> x2, blocking collectives: 39.8 us -> 24.2 us  [exchange(): lax.all_to_all(blocks, ALL, 0, 0, tiled=True, axis_index_groups=groups)]
    all_to_all x0 -> x1, starting transfers between devices: none -> 7.22 us  [exchange(): lax.all_to_all(blocks, ALL, 0, 0, tiled=True, axis_index_groups=groups)]
    all_to_all x0 -> x1, waiting for transfers between devices: none -> 4.59 us  [exchange(): lax.all_to_all(blocks, ALL, 0, 0, tiled=True, axis_index_groups=groups)]
    ppermute x1, waiting for transfers between devices: 1.22 us -> 2.52 us  [shards(): far_eigen = lax.ppermute(eigen_values, ALL, from_next_z(-1))]
    pallas_call x1, Pallas kernels: 1.62 us -> 2.27 us  [shards(): pl.pallas_call(transform_kernel, out_shape=(jax.ShapeDtypeStruct((2 * W,...]
  transfers between devices with their start and end apart: 3 -> 4, of which waited for: 2 -> 3; matrix products, arithmetic and copies ran while one was open for 0% -> 0% of each run, Pallas kernels for 3% -> 5%
where the time goes in v6:
time: 57.1 us; the launch traced here: 56.9 us
  blocking collectives  24.2 us (42%)
  starting transfers between devices  14.4 us (25%)
  Pallas kernels  9.21 us (16%)
  waiting for transfers between devices  8.32 us (15%)
  between operations  0.68 us (1%)
    all_to_all x2, blocking collectives, exchange(): lax.all_to_all(blocks, ALL, 0, 0, tiled=True, axis_index_groups=groups)  24.2 us
    all_to_all x1, starting transfers between devices, exchange(): lax.all_to_all(blocks, ALL, 0, 0, tiled=True, axis_index_groups=groups)  7.22 us
    ppermute x1, starting transfers between devices, shards(): far_kernels = lax.ppermute(kernels, ALL, from_next_z(1))  6.48 us
    all_to_all x1, waiting for transfers between devices, exchange(): lax.all_to_all(blocks, ALL, 0, 0, tiled=True, axis_index_groups=groups)  4.59 us
    pallas_call x1, Pallas kernels, shards(): pl.pallas_call(image_kernel, out_shape=jax.ShapeDtypeStruct((RING_ROWS, C...  4.1 us
    pallas_call x1, Pallas kernels, shards(): pl.pallas_call(bake_kernel, out_shape=(block, block), in_specs=[VMEM, VME...  2.54 us
    ppermute x1, waiting for transfers between devices, shards(): far_eigen = lax.ppermute(eigen_values, ALL, from_next_z(-1))  2.52 us
    pallas_call x1, Pallas kernels, shards(): pl.pallas_call(transform_kernel, out_shape=(jax.ShapeDtypeStruct((2 * W,...  2.27 us
  transfers between devices with their start and end apart: 4, of which 3 were waited for; matrix products, arithmetic and copies ran while one was open for 0% of the time, Pallas kernels for 5%

profile of v6, /device:TPU:1, one launch (start us, length us, event | category | flops | bytes accessed | tf_op | source)
XLA Modules:
  0.0 56.9 jit_solution(9153359973916216502)
XLA Ops:
  0.6 6.5 %collective-permute-start.1 = (f32[2,12,128,128]{3,2,1,0:T(8,128)}, f32[2,12,128,128]{3,2,1,0:T(8,128)S(1)}, u32[]{:S(2)}, u32[]{:S(2)}) collective-permute-start(f32[2,12,128,128]{3,2,1,0:T(8,128)} %near_hbm.1), channel_id=1, source_target_pairs={{128,0},{129,1},{130,2},{131,3},{132,4},{133,5},{134,6},{135,7},{1... | collective-permute-start | bytes 4718600 | tf_op jit(solution)/shard_map/ppermute | solution.py:328
  7.1 2.3 %transform.1 = (f32[256,128]{1,0:T(8,128)}, s32[1,128]{1,0:T(1,128)S(1)}, f32[1,12]{1,0:T(1,128)S(1)}) custom-call(s32[64,1024]{1,0:T(8,128)} %layout_hbm.1, s32[1,128]{1,0:T(1,128)} %bitcast.11, f32[1,12]{1,0:T(1,128)} %bitcast.12), custom_call_target="tpu_custom_call" | custom-call | tf_op jit(solution)/shard_map/transform/pallas_call | solution.py:331
  9.4 7.2 %all-to-all-start = ((f32[32,8,128]{2,1,0:T(8,128)}), f32[32,8,128]{2,1,0:T(8,128)S(1)}, u32[]{:S(2)}, u32[]{:S(2)}) async-start(f32[32,8,128]{2,1,0:T(8,128)} %bitcast.2), calls=%async_computation | async-start | bytes 262144 | tf_op jit(solution)/shard_map/all_to_all | solution.py:310
  16.6 0.1 collective-permute-start
  16.7 0.3 tables.1
  17.0 2.5 %collective-permute-done = f32[12]{0:T(128)S(1)} collective-permute-done((f32[12]{0:T(128)}, f32[12]{0:T(128)S(1)}, u32[]{:S(2)}, u32[]{:S(2)}) %collective-permute-start) | collective-permute-done | bytes 80 | tf_op jit(solution)/shard_map/ppermute | solution.py:329
  19.5 4.6 %all-to-all-done = f32[32,8,128]{2,1,0:T(8,128)S(1)} async-done(((f32[32,8,128]{2,1,0:T(8,128)}), f32[32,8,128]{2,1,0:T(8,128)S(1)}, u32[]{:S(2)}, u32[]{:S(2)}) %all-to-all-start) | async-done | bytes 131104 | tf_op jit(solution)/shard_map/all_to_all | solution.py:310
  24.2 10.6 %all_to_all.26 = f32[8,8,128]{2,1,0:T(8,128)S(1)} all-to-all(f32[8,8,128]{2,1,0:T(8,128)S(1)} %broadcast_in_dim.4), channel_id=1, replica_groups={{0,16,32,48,128,144,160,176},{1,17,33,49,129,145,161,177},{2,18,34,50,1..., dimensions={0} | all-to-all | bytes 65536 | tf_op jit(solution)/shard_map/all_to_all | solution.py:310
  34.8 13.6 %all_to_all.27 = f32[32,8,128]{2,1,0:T(8,128)S(1)} all-to-all(f32[32,8,128]{2,1,0:T(8,128)S(1)} %broadcast_in_dim.5), channel_id=1, replica_groups={{0,1,2,3,4,5,6,7,8,9,10,11,12,13,14,15,64,65,66,67,68,69,70,71,72,73,74..., dimensions={0} | all-to-all | bytes 262144 | tf_op jit(solution)/shard_map/all_to_all | solution.py:310
  48.4 0.0 collective-permute-done.1.far_ref
  48.4 0.0 copy-start
  48.4 0.0 copy-start.1
  48.4 0.0 copy-start.2
  48.4 4.1 %image.1.own_ref = f32[72,1024]{1,0:T(8,128)S(1)} custom-call(f32[256,128]{1,0:T(8,128)S(1)} %bitcast.8, f32[2,12,128,128]{3,2,1,0:T(8,128)} %near_hbm.1, f32[2,12,128,128]{3,2,1,0:T(8,128)S(1)} %collective-permute-done.1.far_ref, bf16[256,1024]{1,0:T(8,128)(2,1)S(1)} %get-tuple-element.16.weights_ref, bf16[80,256]{1,0:T(8,128)(2,1)S(1)} %get-tuple-element.17.row_ref, ...), custom_call_target="tpu_custom_call" | custom-call | tf_op jit(solution)/shard_map/image/pallas_call | solution.py:361
  52.5 0.6 %collective-permute-start.2 = (f32[72,1024]{1,0:T(8,128)S(1)}, f32[72,1024]{1,0:T(8,128)S(1)}, u32[]{:S(2)}, u32[]{:S(2)}) collective-permute-start(f32[72,1024]{1,0:T(8,128)S(1)} %image.1.own_ref), channel_id=1, source_target_pairs={{0,64},{1,65},{2,66},{3,67},{4,68},{5,69},{6,70},{7,71},{8,72},{9,... | collective-permute-start | bytes 884744 | tf_op jit(solution)/shard_map/ppermute | solution.py:376
  53.1 1.2 %collective-permute-done.2.other_ref = f32[72,1024]{1,0:T(8,128)S(1)} collective-permute-done((f32[72,1024]{1,0:T(8,128)S(1)}, f32[72,1024]{1,0:T(8,128)S(1)}, u32[]{:S(2)}, u32[]{:S(2)}) %collective-permute-start.2) | collective-permute-done | bytes 294944 | tf_op jit(solution)/shard_map/ppermute | solution.py:376
  54.3 0.0 copy-done
  54.3 0.0 copy-done.1
  54.3 0.0 copy-done.2
  54.3 2.5 %bake.1 = (f32[64,1024]{1,0:T(8,128)}, f32[64,1024]{1,0:T(8,128)}) custom-call(f32[72,1024]{1,0:T(8,128)S(1)} %image.1.own_ref, f32[72,1024]{1,0:T(8,128)S(1)} %collective-permute-done.2.other_ref, bf16[32,4096]{1,0:T(8,128)(2,1)S(1)} %copy-done.1, bf16[32,4096]{1,0:T(8,128)(2,1)S(1)} %copy-done, f32[5]{0:T(128)S(1)} %copy-done.2), custom_call_target="tpu_custom_call" | custom-call | tf_op jit(solution)/shard_map/bake/pallas_call | solution.py:379
  (4 shorter events, 0.1 us)
Async XLA Ops:
  0.6 47.7 %collective-permute-start.1 = (f32[2,12,128,128]{3,2,1,0:T(8,128)}, f32[2,12,128,128]{3,2,1,0:T(8,128)S(1)}, u32[]{:S(2)}, u32[]{:S(2)}) collective-permute-start(f32[2,12,128,128]{3,2,1,0:T(8,128)} %near_hbm.1), channel_id=1, source_target_pairs={{128,0},{129,1},{130,2},{131,3},{132,4},{133,5},{134,6},{135,7},{1... | collective-permute-start | bytes 4718600 | tf_op jit(solution)/shard_map/ppermute | solution.py:328
  9.4 14.7 %all-to-all-start = ((f32[32,8,128]{2,1,0:T(8,128)}), f32[32,8,128]{2,1,0:T(8,128)S(1)}, u32[]{:S(2)}, u32[]{:S(2)}) async-start(f32[32,8,128]{2,1,0:T(8,128)} %bitcast.2), calls=%async_computation | async-start | bytes 262144 | tf_op jit(solution)/shard_map/all_to_all | solution.py:310
  16.6 2.9 %collective-permute-start = (f32[12]{0:T(128)}, f32[12]{0:T(128)S(1)}, u32[]{:S(2)}, u32[]{:S(2)}) collective-permute-start(f32[12]{0:T(128)} %param.10), channel_id=1, source_target_pairs={{176,0},{177,1},{178,2},{179,3},{180,4},{181,5},{182,6},{183,7},{1... | collective-permute-start | bytes 152 | tf_op jit(solution)/shard_map/ppermute | solution.py:329
  48.4 5.9 %copy-start = (bf16[32,4096]{1,0:T(8,128)(2,1)S(1)}, bf16[32,4096]{1,0:T(8,128)(2,1)}, u32[]{:S(2)}) copy-start(bf16[32,4096]{1,0:T(8,128)(2,1)} %constant.7.clone.low_ref) | copy-start | bytes 786436
  48.4 5.9 %copy-start.1 = (bf16[32,4096]{1,0:T(8,128)(2,1)S(1)}, bf16[32,4096]{1,0:T(8,128)(2,1)}, u32[]{:S(2)}) copy-start(bf16[32,4096]{1,0:T(8,128)(2,1)} %constant.6.clone.high_ref) | copy-start | bytes 786436
  48.4 5.9 %copy-start.2 = (f32[5]{0:T(128)S(1)}, f32[5]{0:T(128)}, u32[]{:S(2)}) copy-start(f32[5]{0:T(128)} %rates.1) | copy-start | bytes 64
  52.5 1.8 %collective-permute-start.2 = (f32[72,1024]{1,0:T(8,128)S(1)}, f32[72,1024]{1,0:T(8,128)S(1)}, u32[]{:S(2)}, u32[]{:S(2)}) collective-permute-start(f32[72,1024]{1,0:T(8,128)S(1)} %image.1.own_ref), channel_id=1, source_target_pairs={{0,64},{1,65},{2,66},{3,67},{4,68},{5,69},{6,70},{7,71},{8,72},{9,... | collective-permute-start | bytes 884744 | tf_op jit(solution)/shard_map/ppermute | solution.py:376

commit v7 on v5

--- a/solution.py
+++ b/solution.py
@@ -278,7 +278,7 @@
     acid_field = 1.0 - jnp.exp((-4.0 * dill_rate) * aerial_image)
     acid_diffusion = acid_rate * (0.5 + 0.5 * acid_field)
     quencher = jnp.zeros_like(acid_field) + quench_start
-    for bake_step in range(STEPS):
+    for _ in range(STEPS):
         reaction = (4.0 * react_rate) * acid_field * quencher
         new_acid = acid_field + acid_diffusion * laplace(acid_field) - reaction
         quencher = quencher + quench_rate * laplace(quencher) - reaction
@@ -299,7 +299,7 @@
     return pltpu.with_memory_space_constraint(array, pltpu.HBM)
 
 
-def sum_everywhere(part):
+def sum_everywhere(part, beside):
     plane, along_z = plane_groups(), z_groups()
     count = len(plane[0])
     piece = part.shape[0] // count
@@ -313,9 +313,11 @@
     def copies(block, many):
         return jnp.broadcast_to(block[None], (many,) + block.shape).reshape(-1, block.shape[1])
 
-    some = total(exchange(part, plane))
+    blocks = exchange(part, plane)
+    some = total(blocks)
+    some, beside = lax.optimization_barrier((some, beside))
     full = total(exchange(copies(some, len(along_z[0])), along_z))
-    return exchange(copies(full, count), plane)
+    return exchange(copies(full, count), plane), beside
 
 
 def shards(layout, band_freqs, kernels, eigen_values, bake_rates):
@@ -323,7 +325,6 @@
     f32 = jnp.float32
     params = pltpu.CompilerParams(vmem_limit_bytes=24 * 2**20)
     far_kernels = lax.ppermute(kernels, ALL, from_next_z(1))
-    far_eigen = lax.ppermute(eigen_values, ALL, from_next_z(-1))
     own = kernels.shape[1]
     part, *tables, near_eigen = pl.pallas_call(
         transform_kernel,
@@ -344,8 +345,8 @@
         compiler_params=params,
         name="transform",
     )(in_hbm(layout), in_hbm(freqs), in_hbm(eigen_values.reshape(1, own)))
-    part, far_eigen = lax.optimization_barrier((part, far_eigen))
-    spectrum = sum_everywhere(part)
+    far_eigen = lax.ppermute(near_eigen, ALL, from_next_z(-1))
+    spectrum, far_eigen = sum_everywhere(part, far_eigen)
     own_image = pl.pallas_call(
         image_kernel,
         out_shape=jax.ShapeDtypeStruct((RING_ROWS, COARSE), f32),
@@ -359,7 +360,7 @@
         ],
         compiler_params=params,
         name="image",
-    )(spectrum, in_hbm(kernels), far_kernels, *tables, near_eigen, far_eigen.reshape(1, own))
+    )(spectrum, in_hbm(kernels), far_kernels, *tables, near_eigen, far_eigen)
     across_cores = [(i, i + 64 if (i // 64) % 2 == 0 else i - 64) for i in range(256)]
     other_image = lax.ppermute(own_image, ALL, across_cores)
     block = jax.ShapeDtypeStruct((ROWS, COLS), f32)

time: 58.5 us -> 56.9 us (0.973)
  blocking collectives: 39.8 us -> 24 us
  starting transfers between devices: 7.1 us -> 14.4 us
  waiting for transfers between devices: 2.43 us -> 8.64 us
  Pallas kernels: 8.24 us -> 8.89 us
    all_to_all x3 -> x2, blocking collectives: 39.8 us -> 24 us  [exchange(): lax.all_to_all(blocks, ALL, 0, 0, tiled=True, axis_index_groups=groups)]
    all_to_all x0 -> x1, waiting for transfers between devices: none -> 7.42 us  [exchange(): lax.all_to_all(blocks, ALL, 0, 0, tiled=True, axis_index_groups=groups)]
    all_to_all x0 -> x1, starting transfers between devices: none -> 7.22 us  [exchange(): lax.all_to_all(blocks, ALL, 0, 0, tiled=True, axis_index_groups=groups)]
    ppermute x1, waiting for transfers between devices: 1.22 us -> 0.01 us  [shards(): far_eigen = lax.ppermute(near_eigen, ALL, from_next_z(-1))]
    pallas_call x1, Pallas kernels: 1.62 us -> 2.27 us  [shards(): pl.pallas_call(transform_kernel, out_shape=(jax.ShapeDtypeStruct((2 * W,...]
  transfers between devices with their start and end apart: 3 -> 4, of which waited for: 2 -> 2; matrix products, arithmetic and copies ran while one was open for 0% -> 0% of each run, Pallas kernels for 3% -> 4%
where the time goes in v7:
time: 56.9 us; the launch traced here: 56.7 us
  blocking collectives  24 us (42%)
  starting transfers between devices  14.4 us (25%)
  Pallas kernels  8.89 us (16%)
  waiting for transfers between devices  8.64 us (15%)
  between operations  0.68 us (1%)
    all_to_all x2, blocking collectives, exchange(): lax.all_to_all(blocks, ALL, 0, 0, tiled=True, axis_index_groups=groups)  24 us
    all_to_all x1, waiting for transfers between devices, exchange(): lax.all_to_all(blocks, ALL, 0, 0, tiled=True, axis_index_groups=groups)  7.42 us
    all_to_all x1, starting transfers between devices, exchange(): lax.all_to_all(blocks, ALL, 0, 0, tiled=True, axis_index_groups=groups)  7.22 us
    ppermute x1, starting transfers between devices, shards(): far_kernels = lax.ppermute(kernels, ALL, from_next_z(1))  6.48 us
    pallas_call x1, Pallas kernels, shards(): pl.pallas_call(image_kernel, out_shape=jax.ShapeDtypeStruct((RING_ROWS, C...  4.08 us
    pallas_call x1, Pallas kernels, shards(): pl.pallas_call(bake_kernel, out_shape=(block, block), in_specs=[VMEM, VME...  2.54 us
    pallas_call x1, Pallas kernels, shards(): pl.pallas_call(transform_kernel, out_shape=(jax.ShapeDtypeStruct((2 * W,...  2.27 us
    ppermute x1, waiting for transfers between devices, shards(): other_image = lax.ppermute(own_image, ALL, across_cores)  1.21 us
  transfers between devices with their start and end apart: 4, of which 2 were waited for; matrix products, arithmetic and copies ran while one was open for 0% of the time, Pallas kernels for 4%

profile of v7, /device:TPU:1, one launch (start us, length us, event | category | flops | bytes accessed | tf_op | source)
XLA Modules:
  0.0 56.7 jit_solution(3755786994184726821)
XLA Ops:
  0.6 6.5 %collective-permute-start.1 = (f32[2,12,128,128]{3,2,1,0:T(8,128)}, f32[2,12,128,128]{3,2,1,0:T(8,128)S(1)}, u32[]{:S(2)}, u32[]{:S(2)}) collective-permute-start(f32[2,12,128,128]{3,2,1,0:T(8,128)} %near_hbm.1), channel_id=1, source_target_pairs={{128,0},{129,1},{130,2},{131,3},{132,4},{133,5},{134,6},{135,7},{1... | collective-permute-start | bytes 4718600 | tf_op jit(solution)/shard_map/ppermute | solution.py:327
  7.1 2.3 %transform.1 = (f32[256,128]{1,0:T(8,128)}, bf16[256,1024]{1,0:T(8,128)(2,1)S(1)}, bf16[80,256]{1,0:T(8,128)(2,1)S(1)}, f32[1,12]{1,0:T(1,128)S(1)}) custom-call(s32[64,1024]{1,0:T(8,128)} %layout_hbm.1, s32[1,128]{1,0:T(1,128)} %bitcast.5, f32[1,12]{1,0:T(1,128)} %bitcast.6), custom_call_target="tpu_custom_call" | custom-call | tf_op jit(solution)/shard_map/transform/pallas_call | solution.py:329
  9.4 7.2 %all-to-all-start = ((f32[32,8,128]{2,1,0:T(8,128)}), f32[32,8,128]{2,1,0:T(8,128)S(1)}, u32[]{:S(2)}, u32[]{:S(2)}) async-start(f32[32,8,128]{2,1,0:T(8,128)} %bitcast.2), calls=%async_computation | async-start | bytes 262144 | tf_op jit(solution)/shard_map/all_to_all | solution.py:308
  16.6 0.1 collective-permute-start
  16.7 7.4 %all-to-all-done = f32[32,8,128]{2,1,0:T(8,128)S(1)} async-done(((f32[32,8,128]{2,1,0:T(8,128)}), f32[32,8,128]{2,1,0:T(8,128)S(1)}, u32[]{:S(2)}, u32[]{:S(2)}) %all-to-all-start) | async-done | bytes 131104 | tf_op jit(solution)/shard_map/all_to_all | solution.py:308
  24.2 0.0 collective-permute-done.far_eigen
  24.2 10.6 %all_to_all.23 = f32[8,8,128]{2,1,0:T(8,128)S(1)} all-to-all(f32[8,8,128]{2,1,0:T(8,128)S(1)} %broadcast_in_dim.4), channel_id=1, replica_groups={{0,16,32,48,128,144,160,176},{1,17,33,49,129,145,161,177},{2,18,34,50,1..., dimensions={0} | all-to-all | bytes 65536 | tf_op jit(solution)/shard_map/all_to_all | solution.py:308
  34.8 13.4 %all_to_all.24 = f32[32,8,128]{2,1,0:T(8,128)S(1)} all-to-all(f32[32,8,128]{2,1,0:T(8,128)S(1)} %broadcast_in_dim.5), channel_id=1, replica_groups={{0,1,2,3,4,5,6,7,8,9,10,11,12,13,14,15,64,65,66,67,68,69,70,71,72,73,74..., dimensions={0} | all-to-all | bytes 262144 | tf_op jit(solution)/shard_map/all_to_all | solution.py:308
  48.2 0.0 collective-permute-done.1.far_ref
  48.2 0.0 copy-start
  48.2 0.0 copy-start.1
  48.2 0.0 copy-start.2
  48.2 4.1 %image.1.own_ref = f32[72,1024]{1,0:T(8,128)S(1)} custom-call(f32[256,128]{1,0:T(8,128)S(1)} %bitcast.4, f32[2,12,128,128]{3,2,1,0:T(8,128)} %near_hbm.1, f32[2,12,128,128]{3,2,1,0:T(8,128)S(1)} %collective-permute-done.1.far_ref, bf16[256,1024]{1,0:T(8,128)(2,1)S(1)} %get-tuple-element.11.weights_ref, bf16[80,256]{1,0:T(8,128)(2,1)S(1)} %get-tuple-element.12.row_ref, ...), custom_call_target="tpu_custom_call" | custom-call | tf_op jit(solution)/shard_map/image/pallas_call | solution.py:350
  52.3 0.6 %collective-permute-start.2 = (f32[72,1024]{1,0:T(8,128)S(1)}, f32[72,1024]{1,0:T(8,128)S(1)}, u32[]{:S(2)}, u32[]{:S(2)}) collective-permute-start(f32[72,1024]{1,0:T(8,128)S(1)} %image.1.own_ref), channel_id=1, source_target_pairs={{0,64},{1,65},{2,66},{3,67},{4,68},{5,69},{6,70},{7,71},{8,72},{9,... | collective-permute-start | bytes 884744 | tf_op jit(solution)/shard_map/ppermute | solution.py:365
  52.9 1.2 %collective-permute-done.2.other_ref = f32[72,1024]{1,0:T(8,128)S(1)} collective-permute-done((f32[72,1024]{1,0:T(8,128)S(1)}, f32[72,1024]{1,0:T(8,128)S(1)}, u32[]{:S(2)}, u32[]{:S(2)}) %collective-permute-start.2) | collective-permute-done | bytes 294944 | tf_op jit(solution)/shard_map/ppermute | solution.py:365
  54.1 0.0 copy-done
  54.1 0.0 copy-done.1
  54.1 0.0 copy-done.2
  54.1 2.5 %bake.1 = (f32[64,1024]{1,0:T(8,128)}, f32[64,1024]{1,0:T(8,128)}) custom-call(f32[72,1024]{1,0:T(8,128)S(1)} %image.1.own_ref, f32[72,1024]{1,0:T(8,128)S(1)} %collective-permute-done.2.other_ref, bf16[32,4096]{1,0:T(8,128)(2,1)S(1)} %copy-done.1, bf16[32,4096]{1,0:T(8,128)(2,1)S(1)} %copy-done, f32[5]{0:T(128)S(1)} %copy-done.2), custom_call_target="tpu_custom_call" | custom-call | tf_op jit(solution)/shard_map/bake/pallas_call | solution.py:368
  (4 shorter events, 0.1 us)
Async XLA Ops:
  0.6 47.6 %collective-permute-start.1 = (f32[2,12,128,128]{3,2,1,0:T(8,128)}, f32[2,12,128,128]{3,2,1,0:T(8,128)S(1)}, u32[]{:S(2)}, u32[]{:S(2)}) collective-permute-start(f32[2,12,128,128]{3,2,1,0:T(8,128)} %near_hbm.1), channel_id=1, source_target_pairs={{128,0},{129,1},{130,2},{131,3},{132,4},{133,5},{134,6},{135,7},{1... | collective-permute-start | bytes 4718600 | tf_op jit(solution)/shard_map/ppermute | solution.py:327
  9.4 14.7 %all-to-all-start = ((f32[32,8,128]{2,1,0:T(8,128)}), f32[32,8,128]{2,1,0:T(8,128)S(1)}, u32[]{:S(2)}, u32[]{:S(2)}) async-start(f32[32,8,128]{2,1,0:T(8,128)} %bitcast.2), calls=%async_computation | async-start | bytes 262144 | tf_op jit(solution)/shard_map/all_to_all | solution.py:308
  16.6 7.6 %collective-permute-start = (f32[1,12]{1,0:T(1,128)S(1)}, f32[1,12]{1,0:T(1,128)S(1)}, u32[]{:S(2)}, u32[]{:S(2)}) collective-permute-start(f32[1,12]{1,0:T(1,128)S(1)} %get-tuple-element.9.near_eigen), channel_id=1, source_target_pairs={{176,0},{177,1},{178,2},{179,3},{180,4},{181,5},{182,6},{183,7},{1... | collective-permute-start | bytes 152 | tf_op jit(solution)/shard_map/ppermute | solution.py:348
  48.2 5.9 %copy-start = (bf16[32,4096]{1,0:T(8,128)(2,1)S(1)}, bf16[32,4096]{1,0:T(8,128)(2,1)}, u32[]{:S(2)}) copy-start(bf16[32,4096]{1,0:T(8,128)(2,1)} %constant.7.clone.low_ref) | copy-start | bytes 786436
  48.2 5.9 %copy-start.1 = (bf16[32,4096]{1,0:T(8,128)(2,1)S(1)}, bf16[32,4096]{1,0:T(8,128)(2,1)}, u32[]{:S(2)}) copy-start(bf16[32,4096]{1,0:T(8,128)(2,1)} %constant.6.clone.high_ref) | copy-start | bytes 786436
  48.2 5.9 %copy-start.2 = (f32[5]{0:T(128)S(1)}, f32[5]{0:T(128)}, u32[]{:S(2)}) copy-start(f32[5]{0:T(128)} %rates.1) | copy-start | bytes 64
  52.3 1.8 %collective-permute-start.2 = (f32[72,1024]{1,0:T(8,128)S(1)}, f32[72,1024]{1,0:T(8,128)S(1)}, u32[]{:S(2)}, u32[]{:S(2)}) collective-permute-start(f32[72,1024]{1,0:T(8,128)S(1)} %image.1.own_ref), channel_id=1, source_target_pairs={{0,64},{1,65},{2,66},{3,67},{4,68},{5,69},{6,70},{7,71},{8,72},{9,... | collective-permute-start | bytes 884744 | tf_op jit(solution)/shard_map/ppermute | solution.py:365

commit v8 on v7

--- a/solution.py
+++ b/solution.py
@@ -299,7 +299,7 @@
     return pltpu.with_memory_space_constraint(array, pltpu.HBM)
 
 
-def sum_everywhere(part, beside):
+def sum_everywhere(part, eigen):
     plane, along_z = plane_groups(), z_groups()
     count = len(plane[0])
     piece = part.shape[0] // count
@@ -313,11 +313,12 @@
     def copies(block, many):
         return jnp.broadcast_to(block[None], (many,) + block.shape).reshape(-1, block.shape[1])
 
-    blocks = exchange(part, plane)
-    some = total(blocks)
-    some, beside = lax.optimization_barrier((some, beside))
-    full = total(exchange(copies(some, len(along_z[0])), along_z))
-    return exchange(copies(full, count), plane), beside
+    some, eigen = lax.optimization_barrier((total(exchange(part, plane)), eigen))
+    far_eigen = lax.ppermute(eigen, ALL, from_next_z(-1))
+    blocks = exchange(copies(some, len(along_z[0])), along_z)
+    full = total(blocks)
+    full, far_eigen = lax.optimization_barrier((full, far_eigen))
+    return exchange(copies(full, count), plane), far_eigen
 
 
 def shards(layout, band_freqs, kernels, eigen_values, bake_rates):
@@ -345,8 +346,7 @@
         compiler_params=params,
         name="transform",
     )(in_hbm(layout), in_hbm(freqs), in_hbm(eigen_values.reshape(1, own)))
-    far_eigen = lax.ppermute(near_eigen, ALL, from_next_z(-1))
-    spectrum, far_eigen = sum_everywhere(part, far_eigen)
+    spectrum, far_eigen = sum_everywhere(part, near_eigen)
     own_image = pl.pallas_call(
         image_kernel,
         out_shape=jax.ShapeDtypeStruct((RING_ROWS, COARSE), f32),

time: 56.9 us -> 56.1 us (0.986)
  blocking collectives: 24 us -> 27.2 us
  waiting for transfers between devices: 8.64 us -> 6.34 us
  starting transfers between devices: 14.4 us -> 12.8 us
  Pallas kernels: 8.89 us -> 8.24 us
  local copies, waits for them, and re-layouts: 0.03 us -> 0.64 us
    all_to_all x2, blocking collectives: 24 us -> 27.2 us  [exchange(): lax.all_to_all(blocks, ALL, 0, 0, tiled=True, axis_index_groups=groups)]
    all_to_all x1, starting transfers between devices: 7.22 us -> 4.19 us  [exchange(): lax.all_to_all(blocks, ALL, 0, 0, tiled=True, axis_index_groups=groups)]
    all_to_all x1, waiting for transfers between devices: 7.42 us -> 5.12 us  [exchange(): lax.all_to_all(blocks, ALL, 0, 0, tiled=True, axis_index_groups=groups)]
    ppermute x1, starting transfers between devices: 0.09 us -> 1.46 us  [sum_everywhere(): far_eigen = lax.ppermute(eigen, ALL, from_next_z(-1))]
    pallas_call x1, Pallas kernels: 2.27 us -> 1.62 us  [shards(): pl.pallas_call(transform_kernel, out_shape=(jax.ShapeDtypeStruct((2 * W,...]
    broadcast_in_dim x2, local copies, waits for them, and re-layouts: 0.02 us -> 0.63 us  [copies(): jnp.broadcast_to(block[None], (many,) + block.shape)]
  transfers between devices with their start and end apart: 4 -> 4, of which waited for: 2 -> 2; matrix products, arithmetic and copies ran while one was open for 0% -> 1% of each run, Pallas kernels for 4% -> 3%
where the time goes in v8:
time: 56.1 us; the launch traced here: 55.8 us
  blocking collectives  27.2 us (48%)
  starting transfers between devices  12.8 us (23%)
  Pallas kernels  8.24 us (15%)
  waiting for transfers between devices  6.34 us (11%)
  between operations  0.67 us (1%)
  local copies, waits for them, and re-layouts  0.64 us (1%)
    all_to_all x2, blocking collectives, exchange(): lax.all_to_all(blocks, ALL, 0, 0, tiled=True, axis_index_groups=groups)  27.2 us
    ppermute x1, starting transfers between devices, shards(): far_kernels = lax.ppermute(kernels, ALL, from_next_z(1))  6.48 us
    all_to_all x1, waiting for transfers between devices, exchange(): lax.all_to_all(blocks, ALL, 0, 0, tiled=True, axis_index_groups=groups)  5.12 us
    all_to_all x1, starting transfers between devices, exchange(): lax.all_to_all(blocks, ALL, 0, 0, tiled=True, axis_index_groups=groups)  4.19 us
    pallas_call x1, Pallas kernels, shards(): pl.pallas_call(image_kernel, out_shape=jax.ShapeDtypeStruct((RING_ROWS, C...  4.08 us
    pallas_call x1, Pallas kernels, shards(): pl.pallas_call(bake_kernel, out_shape=(block, block), in_specs=[VMEM, VME...  2.53 us
    pallas_call x1, Pallas kernels, shards(): pl.pallas_call(transform_kernel, out_shape=(jax.ShapeDtypeStruct((2 * W,...  1.62 us
    ppermute x1, starting transfers between devices, sum_everywhere(): far_eigen = lax.ppermute(eigen, ALL, from_next_z(-1))  1.46 us
  transfers between devices with their start and end apart: 4, of which 2 were waited for; matrix products, arithmetic and copies ran while one was open for 1% of the time, Pallas kernels for 3%

profile of v8, /device:TPU:1, one launch (start us, length us, event | category | flops | bytes accessed | tf_op | source)
XLA Modules:
  0.0 55.8 jit_solution(1173589114026491704)
XLA Ops:
  0.6 6.5 %collective-permute-start.1 = (f32[2,12,128,128]{3,2,1,0:T(8,128)}, f32[2,12,128,128]{3,2,1,0:T(8,128)S(1)}, u32[]{:S(2)}, u32[]{:S(2)}) collective-permute-start(f32[2,12,128,128]{3,2,1,0:T(8,128)} %near_hbm.1), channel_id=1, source_target_pairs={{128,0},{129,1},{130,2},{131,3},{132,4},{133,5},{134,6},{135,7},{1... | collective-permute-start | bytes 4718600 | tf_op jit(solution)/shard_map/ppermute | solution.py:328
  7.1 1.6 %transform.1 = (f32[256,128]{1,0:T(8,128)S(1)}, bf16[256,1024]{1,0:T(8,128)(2,1)S(1)}, bf16[80,256]{1,0:T(8,128)(2,1)S(1)}, f32[1,12]{1,0:T(1,128)S(1)}) custom-call(s32[64,1024]{1,0:T(8,128)} %layout_hbm.1, s32[1,128]{1,0:T(1,128)} %bitcast.6, f32[1,12]{1,0:T(1,128)} %bitcast.7), custom_call_target="tpu_custom_call" | custom-call | tf_op jit(solution)/shard_map/transform/pallas_call | solution.py:330
  8.7 14.5 %all_to_all.23 = f32[32,8,128]{2,1,0:T(8,128)S(1)} all-to-all(f32[32,8,128]{2,1,0:T(8,128)S(1)} %bitcast.5), channel_id=1, replica_groups={{0,1,2,3,4,5,6,7,8,9,10,11,12,13,14,15,64,65,66,67,68,69,70,71,72,73,74..., dimensions={0} | all-to-all | bytes 262144 | tf_op jit(solution)/shard_map/all_to_all | solution.py:308
  23.3 0.6 %broadcast_in_dim.4 = f32[8,8,128]{2,1,0:T(8,128)} broadcast(f32[8,128]{1,0:T(8,128)S(1)} %reduce_sum.18), dimensions={1,2} | broadcast | bytes 36864 | tf_op jit(solution)/shard_map/broadcast_in_dim | solution.py:314
  23.9 4.2 %all-to-all-start.1 = ((f32[8,8,128]{2,1,0:T(8,128)}), f32[8,8,128]{2,1,0:T(8,128)S(1)}, u32[]{:S(2)}, u32[]{:S(2)}) async-start(f32[8,8,128]{2,1,0:T(8,128)} %broadcast_in_dim.4), calls=%async_computation.1 | async-start | bytes 65536 | tf_op jit(solution)/shard_map/all_to_all | solution.py:308
  28.1 1.5 %collective-permute-start = (f32[1,12]{1,0:T(1,128)S(1)}, f32[1,12]{1,0:T(1,128)S(1)}, u32[]{:S(2)}, u32[]{:S(2)}) collective-permute-start(f32[1,12]{1,0:T(1,128)S(1)} %get-tuple-element.13.near_eigen), channel_id=1, source_target_pairs={{176,0},{177,1},{178,2},{179,3},{180,4},{181,5},{182,6},{183,7},{1... | collective-permute-start | bytes 152 | tf_op jit(solution)/shard_map/ppermute | solution.py:317
  29.6 5.1 %all-to-all-done.1 = f32[8,8,128]{2,1,0:T(8,128)S(1)} async-done(((f32[8,8,128]{2,1,0:T(8,128)}), f32[8,8,128]{2,1,0:T(8,128)S(1)}, u32[]{:S(2)}, u32[]{:S(2)}) %all-to-all-start.1) | async-done | bytes 32800 | tf_op jit(solution)/shard_map/all_to_all | solution.py:308
  34.7 0.0 collective-permute-done.far_eigen
  34.7 12.6 %all_to_all.24 = f32[32,8,128]{2,1,0:T(8,128)S(1)} all-to-all(f32[32,8,128]{2,1,0:T(8,128)S(1)} %broadcast_in_dim.5), channel_id=1, replica_groups={{0,1,2,3,4,5,6,7,8,9,10,11,12,13,14,15,64,65,66,67,68,69,70,71,72,73,74..., dimensions={0} | all-to-all | bytes 262144 | tf_op jit(solution)/shard_map/all_to_all | solution.py:308
  47.4 0.0 collective-permute-done.1.far_ref
  47.4 0.0 copy-start
  47.4 0.0 copy-start.1
  47.4 0.0 copy-start.2
  47.4 4.1 %image.1.own_ref = f32[72,1024]{1,0:T(8,128)S(1)} custom-call(f32[256,128]{1,0:T(8,128)S(1)} %bitcast.4, f32[2,12,128,128]{3,2,1,0:T(8,128)} %near_hbm.1, f32[2,12,128,128]{3,2,1,0:T(8,128)S(1)} %collective-permute-done.1.far_ref, bf16[256,1024]{1,0:T(8,128)(2,1)S(1)} %get-tuple-element.15.weights_ref, bf16[80,256]{1,0:T(8,128)(2,1)S(1)} %get-tuple-element.16.row_ref, ...), custom_call_target="tpu_custom_call" | custom-call | tf_op jit(solution)/shard_map/image/pallas_call | solution.py:350
  51.5 0.6 %collective-permute-start.2 = (f32[72,1024]{1,0:T(8,128)S(1)}, f32[72,1024]{1,0:T(8,128)S(1)}, u32[]{:S(2)}, u32[]{:S(2)}) collective-permute-start(f32[72,1024]{1,0:T(8,128)S(1)} %image.1.own_ref), channel_id=1, source_target_pairs={{0,64},{1,65},{2,66},{3,67},{4,68},{5,69},{6,70},{7,71},{8,72},{9,... | collective-permute-start | bytes 884744 | tf_op jit(solution)/shard_map/ppermute | solution.py:365
  52.1 1.2 %collective-permute-done.2.other_ref = f32[72,1024]{1,0:T(8,128)S(1)} collective-permute-done((f32[72,1024]{1,0:T(8,128)S(1)}, f32[72,1024]{1,0:T(8,128)S(1)}, u32[]{:S(2)}, u32[]{:S(2)}) %collective-permute-start.2) | collective-permute-done | bytes 294944 | tf_op jit(solution)/shard_map/ppermute | solution.py:365
  53.3 0.0 copy-done
  53.3 0.0 copy-done.1
  53.3 0.0 copy-done.2
  53.3 2.5 %bake.1 = (f32[64,1024]{1,0:T(8,128)}, f32[64,1024]{1,0:T(8,128)}) custom-call(f32[72,1024]{1,0:T(8,128)S(1)} %image.1.own_ref, f32[72,1024]{1,0:T(8,128)S(1)} %collective-permute-done.2.other_ref, bf16[32,4096]{1,0:T(8,128)(2,1)S(1)} %copy-done.1, bf16[32,4096]{1,0:T(8,128)(2,1)S(1)} %copy-done, f32[5]{0:T(128)S(1)} %copy-done.2), custom_call_target="tpu_custom_call" | custom-call | tf_op jit(solution)/shard_map/bake/pallas_call | solution.py:368
  (3 shorter events, 0.1 us)
Async XLA Ops:
  0.6 46.7 %collective-permute-start.1 = (f32[2,12,128,128]{3,2,1,0:T(8,128)}, f32[2,12,128,128]{3,2,1,0:T(8,128)S(1)}, u32[]{:S(2)}, u32[]{:S(2)}) collective-permute-start(f32[2,12,128,128]{3,2,1,0:T(8,128)} %near_hbm.1), channel_id=1, source_target_pairs={{128,0},{129,1},{130,2},{131,3},{132,4},{133,5},{134,6},{135,7},{1... | collective-permute-start | bytes 4718600 | tf_op jit(solution)/shard_map/ppermute | solution.py:328
  23.9 10.8 %all-to-all-start.1 = ((f32[8,8,128]{2,1,0:T(8,128)}), f32[8,8,128]{2,1,0:T(8,128)S(1)}, u32[]{:S(2)}, u32[]{:S(2)}) async-start(f32[8,8,128]{2,1,0:T(8,128)} %broadcast_in_dim.4), calls=%async_computation.1 | async-start | bytes 65536 | tf_op jit(solution)/shard_map/all_to_all | solution.py:308
  28.1 6.6 %collective-permute-start = (f32[1,12]{1,0:T(1,128)S(1)}, f32[1,12]{1,0:T(1,128)S(1)}, u32[]{:S(2)}, u32[]{:S(2)}) collective-permute-start(f32[1,12]{1,0:T(1,128)S(1)} %get-tuple-element.13.near_eigen), channel_id=1, source_target_pairs={{176,0},{177,1},{178,2},{179,3},{180,4},{181,5},{182,6},{183,7},{1... | collective-permute-start | bytes 152 | tf_op jit(solution)/shard_map/ppermute | solution.py:317
  47.4 5.9 %copy-start = (bf16[32,4096]{1,0:T(8,128)(2,1)S(1)}, bf16[32,4096]{1,0:T(8,128)(2,1)}, u32[]{:S(2)}) copy-start(bf16[32,4096]{1,0:T(8,128)(2,1)} %constant.7.clone.low_ref) | copy-start | bytes 786436
  47.4 5.9 %copy-start.1 = (bf16[32,4096]{1,0:T(8,128)(2,1)S(1)}, bf16[32,4096]{1,0:T(8,128)(2,1)}, u32[]{:S(2)}) copy-start(bf16[32,4096]{1,0:T(8,128)(2,1)} %constant.6.clone.high_ref) | copy-start | bytes 786436
  47.4 5.9 %copy-start.2 = (f32[5]{0:T(128)S(1)}, f32[5]{0:T(128)}, u32[]{:S(2)}) copy-start(f32[5]{0:T(128)} %rates.1) | copy-start | bytes 64
  51.5 1.8 %collective-permute-start.2 = (f32[72,1024]{1,0:T(8,128)S(1)}, f32[72,1024]{1,0:T(8,128)S(1)}, u32[]{:S(2)}, u32[]{:S(2)}) collective-permute-start(f32[72,1024]{1,0:T(8,128)S(1)} %image.1.own_ref), channel_id=1, source_target_pairs={{0,64},{1,65},{2,66},{3,67},{4,68},{5,69},{6,70},{7,71},{8,72},{9,... | collective-permute-start | bytes 884744 | tf_op jit(solution)/shard_map/ppermute | solution.py:365

commit v9 on v5

--- a/solution.py
+++ b/solution.py
@@ -21,6 +21,7 @@
 RING_COLS = 1152
 SPARSE = 4
 COARSE = N // SPARSE
+NEAR_BLOCKS = ((0, 3), (0,), (0,), (0, 1), (0, 1, 3))
 ALL = ("kern", "slab")
 CHIP_Z, CORES, FAR_Z, SIDE = 2, 2, 4, 4
 
@@ -95,22 +96,27 @@
     sin = jnp.concatenate(sin_parts, 0).T
     turn_cos = jnp.broadcast_to(turn_cos[0:1], (W, W)).T
     turn_sin = jnp.broadcast_to(turn_sin[0:1], (W, W)).T
-    for tile in range(COARSE // 128):
-        at = slice(tile * 128, tile * 128 + 128)
-        weights_ref[0:W, at] = cos.astype(jnp.bfloat16)
-        weights_ref[W : 2 * W, at] = sin.astype(jnp.bfloat16)
-        cos, sin = cos * turn_cos - sin * turn_sin, sin * turn_cos + cos * turn_sin
+    for start in range(0, W, 32):
+        rows = slice(start, start + 32)
+        c, s, tc, ts = cos[rows], sin[rows], turn_cos[rows], turn_sin[rows]
+        for tile in range(COARSE // 128):
+            at = slice(tile * 128, tile * 128 + 128)
+            weights_ref[rows, at] = c.astype(jnp.bfloat16)
+            weights_ref[W + start : W + start + 32, at] = s.astype(jnp.bfloat16)
+            c, s = c * tc - s * ts, s * tc + c * ts
 
 
 def transform_kernel(
-    layout_hbm, freqs_hbm, eigen_hbm, out_ref, weights_ref, row_ref, eigen_ref, table, layout_ref, freqs_ref, sems
+    layout_hbm, freqs_hbm, eigen_hbm, out_ref, weights_ref, row_ref, eigen_ref, table, layout_ref, freqs_ref, eigen_row,
+    sems,
 ):
     freqs_copy = pltpu.make_async_copy(freqs_hbm, freqs_ref, sems.at[0])
     layout_copy = pltpu.make_async_copy(layout_hbm, layout_ref, sems.at[1])
-    eigen_copy = pltpu.make_async_copy(eigen_hbm, eigen_ref, sems.at[2])
+    eigen_copy = pltpu.make_async_copy(eigen_hbm, eigen_row, sems.at[2])
     freqs_copy.start()
     layout_copy.start()
     eigen_copy.start()
+    eigen_ref[...] = jnp.zeros_like(eigen_ref)
     row_first = lax.axis_index("slab") * ROWS
     col_first = lax.axis_index("kern") * COLS
     freqs_copy.wait()
@@ -157,14 +163,20 @@
     out_ref[W : 2 * W, :] = both[:, W : 2 * W]
     image_tables(freqs, weights_ref)
     eigen_copy.wait()
+    eigen_ref[0:1, 0 : eigen_row.shape[1]] = eigen_row[...]
 
 
 def image_kernel(
-    spec_ref, near_hbm, far_ref, weights_ref, row_ref, near_eigen, far_eigen, image_ref,
+    spec_ref, near_hbm, far_ref, weights_ref, row_ref, along_z_ref, image_ref,
     fields_re, fields_im, near_ref, sem,
 ):
     near_copy = pltpu.make_async_copy(near_hbm, near_ref, sem)
     near_copy.start()
+    even_eigen = along_z_ref[8:9, :]
+    odd_eigen = along_z_ref[FAR_Z * 16 + 8 : FAR_Z * 16 + 9, :]
+    odd = lax.axis_index("kern") // CORES == 1
+    near_eigen = jnp.where(odd, odd_eigen, even_eigen)
+    far_eigen = jnp.where(odd, even_eigen, odd_eigen)
     row_table = row_ref[...]
     spec_re = spec_ref[0:W, :]
     spec_im = spec_ref[W : 2 * W, :]
@@ -193,7 +205,7 @@
         fields_im[at, 0:W] = imag
         fields_im[at, W : 2 * W] = real
 
-    def power(first, count, eigen_ref, f0, p, start):
+    def power(first, count, eigen_row, f0, p, start):
         rows = slice(first * RING_ROWS, (first + count) * RING_ROWS)
         weights = weights_ref[:, p * 256 : (p + 1) * 256]
         real = jnp.dot(fields_re[rows, :], weights, preferred_element_type=jnp.float32)
@@ -201,7 +213,7 @@
         for f in range(count):
             re = real[f * RING_ROWS : (f + 1) * RING_ROWS]
             im = imag[f * RING_ROWS : (f + 1) * RING_ROWS]
-            term = eigen_ref[0:1, f0 + f : f0 + f + 1] * (re * re + im * im)
+            term = eigen_row[0:1, f0 + f : f0 + f + 1] * (re * re + im * im)
             start = term if start is None else start + term
         return start
 
@@ -252,17 +264,28 @@
         high = value.astype(jnp.bfloat16).astype(jnp.float32)
         parts[0 : 2 * RING_ROWS, at] = jnp.concatenate([high, value - high], 0).astype(jnp.bfloat16)
 
-    def weights(ref, tiles):
+    def weights(ref, tiles, blocks):
         rows = [
             jnp.concatenate([ref[:, ((t - m) % 32) * 128 : ((t - m) % 32) * 128 + 128] for t in tiles], 1)
-            for m in range(COARSE // 32)
+            for block in blocks
+            for m in range(8 * block, 8 * block + 8)
         ]
         return jnp.concatenate(rows, 0)
 
+    everywhere = range(COARSE // 256)
     for p in range(5):
         tiles = (2 * p, 2 * p + 1) if p < 4 else (8, 31)
-        wide = jnp.dot(parts[0 : 2 * RING_ROWS, :], weights(high_ref, tiles), preferred_element_type=jnp.float32)
-        fine = jnp.dot(parts[0:MXU_ROWS, :], weights(low_ref, tiles), preferred_element_type=jnp.float32)
+        wide = jnp.dot(
+            parts[0 : 2 * RING_ROWS, :], weights(high_ref, tiles, everywhere), preferred_element_type=jnp.float32
+        )
+        fine = sum(
+            jnp.dot(
+                parts[0:MXU_ROWS, block * 256 : (block + 1) * 256],
+                weights(low_ref, tiles, (block,)),
+                preferred_element_type=jnp.float32,
+            )
+            for block in NEAR_BLOCKS[p]
+        )
         value = wide[0:RING_ROWS] + (wide[RING_ROWS : 2 * RING_ROWS] + fine[0:RING_ROWS])
         if p < 4:
             ring[:, p * 256 : (p + 1) * 256] = value
@@ -299,23 +322,20 @@
     return pltpu.with_memory_space_constraint(array, pltpu.HBM)
 
 
-def sum_everywhere(part):
+def sum_everywhere(part, beside):
     plane, along_z = plane_groups(), z_groups()
-    count = len(plane[0])
-    piece = part.shape[0] // count
+    count, piece = len(plane[0]), part.shape[0] // len(plane[0])
 
     def exchange(blocks, groups):
         return lax.all_to_all(blocks, ALL, 0, 0, tiled=True, axis_index_groups=groups)
 
-    def total(blocks):
-        return jnp.sum(blocks.reshape(-1, piece, part.shape[1]), 0)
-
     def copies(block, many):
         return jnp.broadcast_to(block[None], (many,) + block.shape).reshape(-1, block.shape[1])
 
-    some = total(exchange(part, plane))
-    full = total(exchange(copies(some, len(along_z[0])), along_z))
-    return exchange(copies(full, count), plane)
+    some = jnp.sum(exchange(part, plane).reshape(count, piece, -1), 0)
+    brought = exchange(copies(jnp.concatenate([some, beside], 0), len(along_z[0])), along_z)
+    full = jnp.sum(brought.reshape(len(along_z[0]), 2 * piece, -1)[:, :piece], 0)
+    return exchange(copies(full, count), plane), brought
 
 
 def shards(layout, band_freqs, kernels, eigen_values, bake_rates):
@@ -323,15 +343,14 @@
     f32 = jnp.float32
     params = pltpu.CompilerParams(vmem_limit_bytes=24 * 2**20)
     far_kernels = lax.ppermute(kernels, ALL, from_next_z(1))
-    far_eigen = lax.ppermute(eigen_values, ALL, from_next_z(-1))
     own = kernels.shape[1]
-    part, *tables, near_eigen = pl.pallas_call(
+    part, *tables, eigen_tile = pl.pallas_call(
         transform_kernel,
         out_shape=(
             jax.ShapeDtypeStruct((2 * W, W), f32),
             jax.ShapeDtypeStruct((2 * W, COARSE), jnp.bfloat16),
             jax.ShapeDtypeStruct((MXU_ROWS, 2 * W), jnp.bfloat16),
-            jax.ShapeDtypeStruct((1, own), f32),
+            jax.ShapeDtypeStruct((8, W), f32),
         ),
         in_specs=[HBM] * 3,
         out_specs=(VMEM,) * 4,
@@ -339,17 +358,17 @@
             pltpu.VMEM((COLS, 4 * W), jnp.bfloat16),
             pltpu.VMEM((ROWS, COLS), jnp.int32),
             pltpu.VMEM((1, W), jnp.int32),
+            pltpu.VMEM((1, own), f32),
             pltpu.SemaphoreType.DMA((3,)),
         ],
         compiler_params=params,
         name="transform",
     )(in_hbm(layout), in_hbm(freqs), in_hbm(eigen_values.reshape(1, own)))
-    part, far_eigen = lax.optimization_barrier((part, far_eigen))
-    spectrum = sum_everywhere(part)
+    spectrum, along_z = sum_everywhere(part, eigen_tile)
     own_image = pl.pallas_call(
         image_kernel,
         out_shape=jax.ShapeDtypeStruct((RING_ROWS, COARSE), f32),
-        in_specs=[VMEM, HBM] + [VMEM] * 5,
+        in_specs=[VMEM, HBM] + [VMEM] * 4,
         out_specs=VMEM,
         scratch_shapes=[
             pltpu.VMEM((2 * own * RING_ROWS, 2 * W), jnp.bfloat16),
@@ -359,7 +378,7 @@
         ],
         compiler_params=params,
         name="image",
-    )(spectrum, in_hbm(kernels), far_kernels, *tables, near_eigen, far_eigen.reshape(1, own))
+    )(spectrum, in_hbm(kernels), far_kernels, *tables, along_z)
     across_cores = [(i, i + 64 if (i // 64) % 2 == 0 else i - 64) for i in range(256)]
     other_image = lax.ppermute(own_image, ALL, across_cores)
     block = jax.ShapeDtypeStruct((ROWS, COLS), f32)

time: 58.5 us -> 55.1 us (0.942)
  blocking collectives: 39.8 us -> 37.8 us
  waiting for transfers between devices: 2.43 us -> 1.21 us
    all_to_all x3, blocking collectives: 39.8 us -> 37.8 us  [exchange(): lax.all_to_all(blocks, ALL, 0, 0, tiled=True, axis_index_groups=groups)]
    ppermute x1 -> x0, waiting for transfers between devices: 1.22 us -> none  [shards(): far_eigen = lax.ppermute(eigen_values, ALL, from_next_z(-1))]
  transfers between devices with their start and end apart: 3 -> 2, of which waited for: 2 -> 1; matrix products, arithmetic and copies ran while one was open for 0% -> 0% of each run, Pallas kernels for 3% -> 3%
where the time goes in v9:
time: 55.1 us; the launch traced here: 54.9 us
  blocking collectives  37.8 us (69%)
  Pallas kernels  8.05 us (15%)
  starting transfers between devices  7.1 us (13%)
  waiting for transfers between devices  1.21 us (2%)
  between operations  0.66 us (1%)
    all_to_all x3, blocking collectives, exchange(): lax.all_to_all(blocks, ALL, 0, 0, tiled=True, axis_index_groups=groups)  37.8 us
    ppermute x1, starting transfers between devices, shards(): far_kernels = lax.ppermute(kernels, ALL, from_next_z(1))  6.48 us
    pallas_call x1, Pallas kernels, shards(): pl.pallas_call(image_kernel, out_shape=jax.ShapeDtypeStruct((RING_ROWS, C...  4.13 us
    pallas_call x1, Pallas kernels, shards(): pl.pallas_call(bake_kernel, out_shape=(block, block), in_specs=[VMEM, VME...  2.29 us
    pallas_call x1, Pallas kernels, shards(): pl.pallas_call(transform_kernel, out_shape=(jax.ShapeDtypeStruct((2 * W,...  1.62 us
    ppermute x1, waiting for transfers between devices, shards(): other_image = lax.ppermute(own_image, ALL, across_cores)  1.21 us
  transfers between devices with their start and end apart: 2, of which 1 were waited for; matrix products, arithmetic and copies ran while one was open for 0% of the time, Pallas kernels for 3%

profile of v9, /device:TPU:1, one launch (start us, length us, event | category | flops | bytes accessed | tf_op | source)
XLA Modules:
  0.0 54.9 jit_solution(9341745869160762560)
XLA Ops:
  0.6 6.5 %collective-permute-start = (f32[2,12,128,128]{3,2,1,0:T(8,128)}, f32[2,12,128,128]{3,2,1,0:T(8,128)S(1)}, u32[]{:S(2)}, u32[]{:S(2)}) collective-permute-start(f32[2,12,128,128]{3,2,1,0:T(8,128)} %near_hbm.1), channel_id=1, source_target_pairs={{128,0},{129,1},{130,2},{131,3},{132,4},{133,5},{134,6},{135,7},{1... | collective-permute-start | bytes 4718600 | tf_op jit(solution)/shard_map/ppermute | solution.py:345
  7.1 1.6 %transform.1 = (f32[256,128]{1,0:T(8,128)S(1)}, bf16[256,1024]{1,0:T(8,128)(2,1)S(1)}, bf16[80,256]{1,0:T(8,128)(2,1)S(1)}, f32[8,128]{1,0:T(8,128)S(1)}) custom-call(s32[64,1024]{1,0:T(8,128)} %layout_hbm.1, s32[1,128]{1,0:T(1,128)} %bitcast.8, f32[1,12]{1,0:T(1,128)} %bitcast.9), custom_call_target="tpu_custom_call" | custom-call | tf_op jit(solution)/shard_map/transform/pallas_call | solution.py:347
  8.7 14.5 %all_to_all.25 = f32[32,8,128]{2,1,0:T(8,128)S(1)} all-to-all(f32[32,8,128]{2,1,0:T(8,128)S(1)} %bitcast.7), channel_id=1, replica_groups={{0,1,2,3,4,5,6,7,8,9,10,11,12,13,14,15,64,65,66,67,68,69,70,71,72,73,74..., dimensions={0} | all-to-all | bytes 262144 | tf_op jit(solution)/shard_map/all_to_all | solution.py:330
  23.3 10.6 %all_to_all.26 = f32[8,16,128]{2,1,0:T(8,128)S(1)} all-to-all(f32[8,16,128]{2,1,0:T(8,128)S(1)} %broadcast_in_dim.4), channel_id=1, replica_groups={{0,16,32,48,128,144,160,176},{1,17,33,49,129,145,161,177},{2,18,34,50,1..., dimensions={0} | all-to-all | bytes 131072 | tf_op jit(solution)/shard_map/all_to_all | solution.py:330
  34.0 12.6 %all_to_all.27 = f32[32,8,128]{2,1,0:T(8,128)S(1)} all-to-all(f32[32,8,128]{2,1,0:T(8,128)S(1)} %broadcast_in_dim.5), channel_id=1, replica_groups={{0,1,2,3,4,5,6,7,8,9,10,11,12,13,14,15,64,65,66,67,68,69,70,71,72,73,74..., dimensions={0} | all-to-all | bytes 262144 | tf_op jit(solution)/shard_map/all_to_all | solution.py:330
  46.6 0.0 collective-permute-done.far_ref
  46.6 0.0 copy-start
  46.6 0.0 copy-start.1
  46.6 0.0 copy-start.2
  46.6 4.1 %image.1.own_ref = f32[72,1024]{1,0:T(8,128)S(1)} custom-call(f32[256,128]{1,0:T(8,128)S(1)} %bitcast.5, f32[2,12,128,128]{3,2,1,0:T(8,128)} %near_hbm.1, f32[2,12,128,128]{3,2,1,0:T(8,128)S(1)} %collective-permute-done.far_ref, bf16[256,1024]{1,0:T(8,128)(2,1)S(1)} %get-tuple-element.8.weights_ref, bf16[80,256]{1,0:T(8,128)(2,1)S(1)} %get-tuple-element.9.row_ref, ...), custom_call_target="tpu_custom_call" | custom-call | tf_op jit(solution)/shard_map/image/pallas_call | solution.py:368
  50.7 0.6 %collective-permute-start.1 = (f32[72,1024]{1,0:T(8,128)S(1)}, f32[72,1024]{1,0:T(8,128)S(1)}, u32[]{:S(2)}, u32[]{:S(2)}) collective-permute-start(f32[72,1024]{1,0:T(8,128)S(1)} %image.1.own_ref), channel_id=1, source_target_pairs={{0,64},{1,65},{2,66},{3,67},{4,68},{5,69},{6,70},{7,71},{8,72},{9,... | collective-permute-start | bytes 884744 | tf_op jit(solution)/shard_map/ppermute | solution.py:383
  51.4 1.2 %collective-permute-done.1.other_ref = f32[72,1024]{1,0:T(8,128)S(1)} collective-permute-done((f32[72,1024]{1,0:T(8,128)S(1)}, f32[72,1024]{1,0:T(8,128)S(1)}, u32[]{:S(2)}, u32[]{:S(2)}) %collective-permute-start.1) | collective-permute-done | bytes 294944 | tf_op jit(solution)/shard_map/ppermute | solution.py:383
  52.6 0.0 copy-done
  52.6 0.0 copy-done.1
  52.6 0.0 copy-done.2
  52.6 2.3 %bake.1 = (f32[64,1024]{1,0:T(8,128)}, f32[64,1024]{1,0:T(8,128)}) custom-call(f32[72,1024]{1,0:T(8,128)S(1)} %image.1.own_ref, f32[72,1024]{1,0:T(8,128)S(1)} %collective-permute-done.1.other_ref, bf16[32,4096]{1,0:T(8,128)(2,1)S(1)} %copy-done.1, bf16[32,4096]{1,0:T(8,128)(2,1)S(1)} %copy-done, f32[5]{0:T(128)S(1)} %copy-done.2), custom_call_target="tpu_custom_call" | custom-call | tf_op jit(solution)/shard_map/bake/pallas_call | solution.py:386
  (5 shorter events, 0.1 us)
Async XLA Ops:
  0.6 46.0 %collective-permute-start = (f32[2,12,128,128]{3,2,1,0:T(8,128)}, f32[2,12,128,128]{3,2,1,0:T(8,128)S(1)}, u32[]{:S(2)}, u32[]{:S(2)}) collective-permute-start(f32[2,12,128,128]{3,2,1,0:T(8,128)} %near_hbm.1), channel_id=1, source_target_pairs={{128,0},{129,1},{130,2},{131,3},{132,4},{133,5},{134,6},{135,7},{1... | collective-permute-start | bytes 4718600 | tf_op jit(solution)/shard_map/ppermute | solution.py:345
  46.6 6.0 %copy-start = (bf16[32,4096]{1,0:T(8,128)(2,1)S(1)}, bf16[32,4096]{1,0:T(8,128)(2,1)}, u32[]{:S(2)}) copy-start(bf16[32,4096]{1,0:T(8,128)(2,1)} %constant.7.clone.low_ref) | copy-start | bytes 786436
  46.6 6.0 %copy-start.1 = (bf16[32,4096]{1,0:T(8,128)(2,1)S(1)}, bf16[32,4096]{1,0:T(8,128)(2,1)}, u32[]{:S(2)}) copy-start(bf16[32,4096]{1,0:T(8,128)(2,1)} %constant.6.clone.high_ref) | copy-start | bytes 786436
  46.6 6.0 %copy-start.2 = (f32[5]{0:T(128)S(1)}, f32[5]{0:T(128)}, u32[]{:S(2)}) copy-start(f32[5]{0:T(128)} %rates.1) | copy-start | bytes 64
  50.7 1.8 %collective-permute-start.1 = (f32[72,1024]{1,0:T(8,128)S(1)}, f32[72,1024]{1,0:T(8,128)S(1)}, u32[]{:S(2)}, u32[]{:S(2)}) collective-permute-start(f32[72,1024]{1,0:T(8,128)S(1)} %image.1.own_ref), channel_id=1, source_target_pairs={{0,64},{1,65},{2,66},{3,67},{4,68},{5,69},{6,70},{7,71},{8,72},{9,... | collective-permute-start | bytes 884744 | tf_op jit(solution)/shard_map/ppermute | solution.py:383

commit v10 on v9

--- a/solution.py
+++ b/solution.py
@@ -121,10 +121,11 @@
     col_first = lax.axis_index("kern") * COLS
     freqs_copy.wait()
     freqs = freqs_ref[...]
-    step = 32
+    step, quarter = 32, COLS // 4
     base_cos, base_sin = cos_sin((col_first + iota((step, W), 0)) * freqs)
-    turn_cos, turn_sin = cos_sin((step * iota((COLS // step, W), 0)) * freqs)
-    for a in range(COLS // step):
+    turn_cos, turn_sin = cos_sin((step * iota((quarter // step, W), 0)) * freqs)
+    join_cos, join_sin = cos_sin((quarter * iota((8, W), 0)) * freqs)
+    for a in range(quarter // step):
         ca, sa = turn_cos[a : a + 1, :], turn_sin[a : a + 1, :]
         cos = ca * base_cos - sa * base_sin
         sin = sa * base_cos + ca * base_sin
@@ -139,12 +140,21 @@
     row = jnp.where(row < ROWS + 4, row, row - RING_ROWS)
     cos_row, sin_row = cos_sin((row_first + row) * freqs)
     row_ref[...] = (jnp.concatenate([cos_row, sin_row], 1) / W).astype(jnp.bfloat16)
-    left_high, left_low = split(jnp.concatenate([cos_row[0:ROWS], sin_row[0:ROWS]], 0))
+    left_high, left_low = split(jnp.concatenate([cos_row[0:ROWS], sin_row[0:ROWS]], 0).T)
+    left = jnp.concatenate([left_high, left_high, left_low], 1)
+    image_tables(freqs, weights_ref)
     layout_copy.wait()
     transmit = (2 * layout_ref[...] - 1).astype(jnp.float32).astype(jnp.bfloat16)
-    along = jnp.dot(transmit, table[...], preferred_element_type=jnp.float32)
-    along_re = along[:, 0:W] + along[:, 2 * W : 3 * W]
-    along_im = -(along[:, W : 2 * W] + along[:, 3 * W : 4 * W])
+    stacked = jnp.concatenate([transmit[:, h * quarter : (h + 1) * quarter] for h in range(4)], 0)
+    along = jnp.dot(stacked, table[...], preferred_element_type=jnp.float32)
+    along_cos = along[:, 0:W] + along[:, 2 * W : 3 * W]
+    along_sin = along[:, W : 2 * W] + along[:, 3 * W : 4 * W]
+    along_re, along_im = along_cos[0:ROWS], -along_sin[0:ROWS]
+    for h in range(1, 4):
+        c, s = along_cos[h * ROWS : (h + 1) * ROWS], along_sin[h * ROWS : (h + 1) * ROWS]
+        jc, js = join_cos[h : h + 1, :], join_sin[h : h + 1, :]
+        along_re = along_re + (jc * c - js * s)
+        along_im = along_im - (jc * s + js * c)
     right = jnp.concatenate(
         [
             jnp.concatenate([along_re, along_im], 1),
@@ -153,15 +163,13 @@
         0,
     )
     right_high, right_low = split(right)
-    both = lax.dot_general(
-        jnp.concatenate([left_high, left_high, left_low], 0),
+    both = jnp.dot(
+        left,
         jnp.concatenate([right_high, right_low, right_high], 0),
-        (((0,), (0,)), ((), ())),
         preferred_element_type=jnp.float32,
     ) * (1.0 / N)
     out_ref[0:W, :] = both[:, 0:W]
     out_ref[W : 2 * W, :] = both[:, W : 2 * W]
-    image_tables(freqs, weights_ref)
     eigen_copy.wait()
     eigen_ref[0:1, 0 : eigen_row.shape[1]] = eigen_row[...]
 
@@ -355,7 +363,7 @@
         in_specs=[HBM] * 3,
         out_specs=(VMEM,) * 4,
         scratch_shapes=[
-            pltpu.VMEM((COLS, 4 * W), jnp.bfloat16),
+            pltpu.VMEM((COLS // 4, 4 * W), jnp.bfloat16),
             pltpu.VMEM((ROWS, COLS), jnp.int32),
             pltpu.VMEM((1, W), jnp.int32),
             pltpu.VMEM((1, own), f32),

time: 55.1 us -> 55.1 us (level)
  no operation moved by 1% of the time
where the time goes in v10:
time: 55.1 us; the launch traced here: 54.8 us
  blocking collectives  37.8 us (69%)
  Pallas kernels  8.01 us (15%)
  starting transfers between devices  7.1 us (13%)
  waiting for transfers between devices  1.21 us (2%)
  between operations  0.66 us (1%)
    all_to_all x3, blocking collectives, exchange(): lax.all_to_all(blocks, ALL, 0, 0, tiled=True, axis_index_groups=groups)  37.8 us
    ppermute x1, starting transfers between devices, shards(): far_kernels = lax.ppermute(kernels, ALL, from_next_z(1))  6.48 us
    pallas_call x1, Pallas kernels, shards(): pl.pallas_call(image_kernel, out_shape=jax.ShapeDtypeStruct((RING_ROWS, C...  4.13 us
    pallas_call x1, Pallas kernels, shards(): pl.pallas_call(bake_kernel, out_shape=(block, block), in_specs=[VMEM, VME...  2.3 us
    pallas_call x1, Pallas kernels, shards(): pl.pallas_call(transform_kernel, out_shape=(jax.ShapeDtypeStruct((2 * W,...  1.57 us
    ppermute x1, waiting for transfers between devices, shards(): other_image = lax.ppermute(own_image, ALL, across_cores)  1.21 us
  transfers between devices with their start and end apart: 2, of which 1 were waited for; matrix products, arithmetic and copies ran while one was open for 0% of the time, Pallas kernels for 3%

profile of v10, /device:TPU:1, one launch (start us, length us, event | category | flops | bytes accessed | tf_op | source)
XLA Modules:
  0.0 54.8 jit_solution(7371836811525585407)
XLA Ops:
  0.6 6.5 %collective-permute-start = (f32[2,12,128,128]{3,2,1,0:T(8,128)}, f32[2,12,128,128]{3,2,1,0:T(8,128)S(1)}, u32[]{:S(2)}, u32[]{:S(2)}) collective-permute-start(f32[2,12,128,128]{3,2,1,0:T(8,128)} %near_hbm.1), channel_id=1, source_target_pairs={{128,0},{129,1},{130,2},{131,3},{132,4},{133,5},{134,6},{135,7},{1... | collective-permute-start | bytes 4718600 | tf_op jit(solution)/shard_map/ppermute | solution.py:353
  7.1 1.6 %transform.1 = (f32[256,128]{1,0:T(8,128)S(1)}, bf16[256,1024]{1,0:T(8,128)(2,1)S(1)}, bf16[80,256]{1,0:T(8,128)(2,1)S(1)}, f32[8,128]{1,0:T(8,128)S(1)}) custom-call(s32[64,1024]{1,0:T(8,128)} %layout_hbm.1, s32[1,128]{1,0:T(1,128)} %bitcast.8, f32[1,12]{1,0:T(1,128)} %bitcast.9), custom_call_target="tpu_custom_call" | custom-call | tf_op jit(solution)/shard_map/transform/pallas_call | solution.py:355
  8.7 14.5 %all_to_all.25 = f32[32,8,128]{2,1,0:T(8,128)S(1)} all-to-all(f32[32,8,128]{2,1,0:T(8,128)S(1)} %bitcast.7), channel_id=1, replica_groups={{0,1,2,3,4,5,6,7,8,9,10,11,12,13,14,15,64,65,66,67,68,69,70,71,72,73,74..., dimensions={0} | all-to-all | bytes 262144 | tf_op jit(solution)/shard_map/all_to_all | solution.py:338
  23.3 10.6 %all_to_all.26 = f32[8,16,128]{2,1,0:T(8,128)S(1)} all-to-all(f32[8,16,128]{2,1,0:T(8,128)S(1)} %broadcast_in_dim.4), channel_id=1, replica_groups={{0,16,32,48,128,144,160,176},{1,17,33,49,129,145,161,177},{2,18,34,50,1..., dimensions={0} | all-to-all | bytes 131072 | tf_op jit(solution)/shard_map/all_to_all | solution.py:338
  33.9 12.6 %all_to_all.27 = f32[32,8,128]{2,1,0:T(8,128)S(1)} all-to-all(f32[32,8,128]{2,1,0:T(8,128)S(1)} %broadcast_in_dim.5), channel_id=1, replica_groups={{0,1,2,3,4,5,6,7,8,9,10,11,12,13,14,15,64,65,66,67,68,69,70,71,72,73,74..., dimensions={0} | all-to-all | bytes 262144 | tf_op jit(solution)/shard_map/all_to_all | solution.py:338
  46.5 0.0 collective-permute-done.far_ref
  46.5 0.0 copy-start
  46.5 0.0 copy-start.1
  46.5 0.0 copy-start.2
  46.6 4.1 %image.1.own_ref = f32[72,1024]{1,0:T(8,128)S(1)} custom-call(f32[256,128]{1,0:T(8,128)S(1)} %bitcast.5, f32[2,12,128,128]{3,2,1,0:T(8,128)} %near_hbm.1, f32[2,12,128,128]{3,2,1,0:T(8,128)S(1)} %collective-permute-done.far_ref, bf16[256,1024]{1,0:T(8,128)(2,1)S(1)} %get-tuple-element.8.weights_ref, bf16[80,256]{1,0:T(8,128)(2,1)S(1)} %get-tuple-element.9.row_ref, ...), custom_call_target="tpu_custom_call" | custom-call | tf_op jit(solution)/shard_map/image/pallas_call | solution.py:376
  50.7 0.6 %collective-permute-start.1 = (f32[72,1024]{1,0:T(8,128)S(1)}, f32[72,1024]{1,0:T(8,128)S(1)}, u32[]{:S(2)}, u32[]{:S(2)}) collective-permute-start(f32[72,1024]{1,0:T(8,128)S(1)} %image.1.own_ref), channel_id=1, source_target_pairs={{0,64},{1,65},{2,66},{3,67},{4,68},{5,69},{6,70},{7,71},{8,72},{9,... | collective-permute-start | bytes 884744 | tf_op jit(solution)/shard_map/ppermute | solution.py:391
  51.3 1.2 %collective-permute-done.1.other_ref = f32[72,1024]{1,0:T(8,128)S(1)} collective-permute-done((f32[72,1024]{1,0:T(8,128)S(1)}, f32[72,1024]{1,0:T(8,128)S(1)}, u32[]{:S(2)}, u32[]{:S(2)}) %collective-permute-start.1) | collective-permute-done | bytes 294944 | tf_op jit(solution)/shard_map/ppermute | solution.py:391
  52.5 0.0 copy-done
  52.5 0.0 copy-done.1
  52.5 0.0 copy-done.2
  52.5 2.3 %bake.1 = (f32[64,1024]{1,0:T(8,128)}, f32[64,1024]{1,0:T(8,128)}) custom-call(f32[72,1024]{1,0:T(8,128)S(1)} %image.1.own_ref, f32[72,1024]{1,0:T(8,128)S(1)} %collective-permute-done.1.other_ref, bf16[32,4096]{1,0:T(8,128)(2,1)S(1)} %copy-done.1, bf16[32,4096]{1,0:T(8,128)(2,1)S(1)} %copy-done, f32[5]{0:T(128)S(1)} %copy-done.2), custom_call_target="tpu_custom_call" | custom-call | tf_op jit(solution)/shard_map/bake/pallas_call | solution.py:394
  (5 shorter events, 0.1 us)
Async XLA Ops:
  0.6 45.9 %collective-permute-start = (f32[2,12,128,128]{3,2,1,0:T(8,128)}, f32[2,12,128,128]{3,2,1,0:T(8,128)S(1)}, u32[]{:S(2)}, u32[]{:S(2)}) collective-permute-start(f32[2,12,128,128]{3,2,1,0:T(8,128)} %near_hbm.1), channel_id=1, source_target_pairs={{128,0},{129,1},{130,2},{131,3},{132,4},{133,5},{134,6},{135,7},{1... | collective-permute-start | bytes 4718600 | tf_op jit(solution)/shard_map/ppermute | solution.py:353
  46.5 6.0 %copy-start = (bf16[32,4096]{1,0:T(8,128)(2,1)S(1)}, bf16[32,4096]{1,0:T(8,128)(2,1)}, u32[]{:S(2)}) copy-start(bf16[32,4096]{1,0:T(8,128)(2,1)} %constant.7.clone.low_ref) | copy-start | bytes 786436
  46.5 6.0 %copy-start.1 = (bf16[32,4096]{1,0:T(8,128)(2,1)S(1)}, bf16[32,4096]{1,0:T(8,128)(2,1)}, u32[]{:S(2)}) copy-start(bf16[32,4096]{1,0:T(8,128)(2,1)} %constant.6.clone.high_ref) | copy-start | bytes 786436
  46.5 6.0 %copy-start.2 = (f32[5]{0:T(128)S(1)}, f32[5]{0:T(128)}, u32[]{:S(2)}) copy-start(f32[5]{0:T(128)} %rates.1) | copy-start | bytes 64
  50.7 1.8 %collective-permute-start.1 = (f32[72,1024]{1,0:T(8,128)S(1)}, f32[72,1024]{1,0:T(8,128)S(1)}, u32[]{:S(2)}, u32[]{:S(2)}) collective-permute-start(f32[72,1024]{1,0:T(8,128)S(1)} %image.1.own_ref), channel_id=1, source_target_pairs={{0,64},{1,65},{2,66},{3,67},{4,68},{5,69},{6,70},{7,71},{8,72},{9,... | collective-permute-start | bytes 884744 | tf_op jit(solution)/shard_map/ppermute | solution.py:391
